TPU v7x, 512 devices: a whole 4x4x16 slice. The times are simulated.
512 devices in a mesh: slab: 64 (over z, x), shot: 8 (over y, core).
Axes of the slice: x: 4, y: 4, z: 16, core: 2. Of those that a mesh axis runs over, the one named last changes fastest.
Arguments:
- pressure_init: float32 [16, 512, 32, 256], P('shot', 'slab'), may hold values from -6 to 6
- adjoint_init: float32 [16, 512, 32, 256], P('shot', 'slab'), may hold values from -1.5 to 1.5
- density: float32 [512, 32, 256], P('slab'), may hold values from 0.5 to 2
- speed: float32 [512, 32, 256], P('slab'), may hold values from 0.6 to 1.1
- admittance: float32 [512, 32, 256], P('slab'), may hold values from 0.05 to 0.5
- bound_mask: int32 [512, 32, 256], P('slab'), may hold values 0 or 1
- rec_cells: int32 [192, 32], P('slab'), may hold values from 0 to 65535, as said below
- rec_live: int32 [192], P('slab'), may hold values from 0 to 1, as said below
- encoder: float32 [32, 25], replicated, may hold values from -1 to 1
- target: float32 [192, 16, 2, 25], P('slab', 'shot'), may hold values from -6 to 6
Outputs:
- recording: float32 [192, 16, 2, 25], P('slab', 'shot')
- gradient: float32 [512, 32, 256], P('slab')
Inputs may be any that keep to these rules, and one draw needn't show every extreme that they name: `rec_live`: in each aligned group of four slabs the numbers of live slots are 3, 1, 0 and 0 in an order drawn from the seed; a slab's live slots come first. `rec_cells`: each slot's 32 capsule cells form a block of 2 x 4 x 4 cells (z, x, y) inside its own slab.
All inputs are finite; a program needn't handle non-finite values. No bound on the sum of `bound_mask` on one device may be relied on, other than what follows from the above.
Results may differ from a plain program's by a relative error of at most 0.00017.
Values sent between devices are 32-bit elements; how exact they have to be, the bound alone decides.
No kernel may reach another device: no remote copies, remote signals or barrier semaphores. Data moves between devices by JAX's collectives and lax.ppermute only.
A program may use at most 64 MiB of HBM per device.

v0:
```python
import jax
import jax.numpy as jnp
from jax import lax
from jax.sharding import PartitionSpec as P


def from_behind(value, axis, steps):
    count = lax.axis_size(axis)
    leading, last = (max(0, -steps), min(count, count - steps))
    return lax.ppermute(value, axis, [(source, source + steps) for source in range(leading, last)])


def cut_along(array, dim, peers):
    before, after = (array.shape[:dim], array.shape[dim + 1 :])
    return jnp.moveaxis(array.reshape(*before, peers, -1, *after), dim, 0)


def sum_at_owner(array, axis, dim):
    tiles = cut_along(array, dim, lax.axis_size(axis))
    arrived = lax.all_to_all(tiles, axis, split_axis=0, concat_axis=0, tiled=True)
    return arrived.sum(axis=0)


def laid_out(tiles, dim):
    dims = list(tiles.shape[1:])
    dims[dim] *= tiles.shape[0]
    return jnp.moveaxis(tiles, 0, dim).reshape(dims)


def copy_for_each(array, axis):
    copies = jnp.broadcast_to(array, (lax.axis_size(axis), *array.shape))
    return lax.all_to_all(copies, axis, split_axis=0, concat_axis=0, tiled=True)


def gathered_copies(array, axis, dim):
    return laid_out(copy_for_each(array, axis), dim)


def rise_local(values, along):
    widths = [(0, 0)] * values.ndim
    widths[along] = (0, 1)
    padded = jnp.pad(values, widths)
    return lax.slice_in_dim(padded, 1, values.shape[along] + 1, axis=along) - values


def fall_local(values, along):
    widths = [(0, 0)] * values.ndim
    widths[along] = (1, 0)
    padded = jnp.pad(values, widths)
    return values - lax.slice_in_dim(padded, 0, values.shape[along], axis=along)


def selectors(rec_cells, width_x, width_y, planes, z_offset):
    flat = rec_cells.reshape(-1)
    depth_index = flat // (width_x * width_y) + z_offset
    row_index = flat // width_y % width_x
    col_index = flat % width_y
    plane_index = depth_index * width_x + row_index
    plane_pick = (
        plane_index[:, None] == jnp.arange(planes * width_x, dtype=jnp.int32)[None, :]
    ).astype(jnp.float32)
    col_pick = (col_index[:, None] == jnp.arange(width_y, dtype=jnp.int32)[None, :]).astype(
        jnp.float32
    )
    return (plane_pick, col_pick)


def sample_cells(field, plane_pick, col_pick):
    shots = field.shape[0]
    folded = field.reshape(shots, -1, field.shape[3])
    by_column = jnp.einsum("szy,ry->szr", folded, col_pick, precision=lax.Precision.HIGHEST)
    return jnp.sum(by_column * jnp.transpose(plane_pick)[None], axis=1)


def place_cells(values, plane_pick, col_pick, shape):
    spread = values[:, :, None] * col_pick[None]
    placed = jnp.einsum("rz,sry->szy", plane_pick, spread, precision=lax.Precision.HIGHEST)
    return placed.reshape(shape)


def body(
    pressure_init,
    adjoint_init,
    density,
    speed,
    admittance,
    bound_mask,
    rec_cells,
    rec_live,
    encoder,
    target,
):
    steps = target.shape[2]
    shots = pressure_init.shape[0]
    slab_depth = pressure_init.shape[1]
    width_x = pressure_init.shape[2]
    width_y = pressure_init.shape[3]
    slot_count = rec_cells.shape[0]
    capsules = rec_cells.shape[1]
    field_shape = pressure_init.shape
    wall = bound_mask.astype(jnp.float32)
    vel_coef = 0.5 / density
    pres_coef = 0.5 * density * speed * speed
    damping = 1.0 - admittance * wall
    coefs = jnp.stack([vel_coef, pres_coef, damping])
    live = rec_live.astype(jnp.float32)[:, None, None]
    lower_pack = jnp.concatenate([pressure_init[:, :steps], coefs[:, :steps]], axis=0)
    upper_pack = jnp.concatenate(
        [pressure_init[:, slab_depth - steps :], coefs[:, slab_depth - steps :]], axis=0
    )
    from_above = from_behind(lower_pack, "slab", -1)
    from_below = from_behind(upper_pack, "slab", 1)
    pressure = jnp.concatenate([from_below[:shots], pressure_init, from_above[:shots]], axis=1)
    coef_pad = jnp.concatenate([from_below[shots:], coefs, from_above[shots:]], axis=1)
    plane_front, col_front = selectors(rec_cells, width_x, width_y, slab_depth + 2 * steps, steps)
    vel_use = coef_pad[0]
    pres_use = coef_pad[1]
    damp_use = coef_pad[2]
    flow_x = jnp.zeros_like(pressure)
    flow_y = jnp.zeros_like(pressure)
    flow_z = jnp.zeros_like(pressure)
    saved = []
    misfit = []
    records = []
    for moment in range(steps):
        flow_x = flow_x - vel_use * rise_local(pressure, 2)
        flow_y = flow_y - vel_use * rise_local(pressure, 3)
        flow_z = flow_z - vel_use * rise_local(pressure, along=1)
        before = pressure - pres_use * (
            fall_local(flow_x, 2) + fall_local(flow_y, 3) + fall_local(flow_z, along=1)
        )
        pressure = before * damp_use
        saved.append(before[:, steps : steps + slab_depth])
        sampled = sample_cells(pressure, plane_front, col_front).reshape(
            shots, slot_count, capsules
        )
        encoded = (
            jnp.einsum("src,ck->rsk", sampled, encoder, precision=lax.Precision.HIGHEST) * live
        )
        records.append(encoded)
        misfit.append(encoded - target[:, :, moment, :] * live)
    recording = jnp.stack(records, axis=2)
    sources = [
        jnp.einsum("rsk,ck->src", misfit[moment], encoder, precision=lax.Precision.HIGHEST).reshape(
            shots, -1
        )
        for moment in range(steps)
    ]
    plane_own, col_own = selectors(rec_cells, width_x, width_y, slab_depth, 0)
    back_margin = steps - 1
    dense = [place_cells(source, plane_own, col_own, field_shape) for source in sources]
    lower_back = jnp.concatenate(
        [adjoint_init[:, :back_margin]] + [dense[1][:, :back_margin]], axis=0
    )
    upper_back = jnp.concatenate(
        [adjoint_init[:, slab_depth - back_margin :]] + [dense[1][:, slab_depth - back_margin :]],
        axis=0,
    )
    above_back = from_behind(lower_back, "slab", -1)
    below_back = from_behind(upper_back, "slab", 1)
    adjoint = jnp.concatenate([below_back[:shots], adjoint_init, above_back[:shots]], axis=1)
    ghost_zero = jnp.zeros((shots, back_margin) + field_shape[2:], jnp.float32)
    injections = [jnp.concatenate([ghost_zero, dense[0], ghost_zero], axis=1)]
    moment = 1
    lower_part = below_back[moment * shots : (moment + 1) * shots]
    upper_part = above_back[moment * shots : (moment + 1) * shots]
    injections.append(jnp.concatenate([lower_part, dense[moment], upper_part], axis=1))
    offset = steps - back_margin
    coef_back = coef_pad[:, offset : offset + slab_depth + 2 * back_margin]
    vel_back = coef_back[0]
    pres_back = coef_back[1]
    damp_back = coef_back[2]
    back_x = jnp.zeros_like(adjoint)
    back_y = jnp.zeros_like(adjoint)
    back_z = jnp.zeros_like(adjoint)
    partial_grad = jnp.zeros(density.shape, jnp.float32)
    for moment in reversed(range(steps)):
        adjoint = adjoint + injections[moment]
        inside = adjoint[:, back_margin : back_margin + slab_depth]
        partial_grad = partial_grad - wall * jnp.sum(saved[moment] * inside, axis=0)
        if moment > 0:
            scaled = adjoint * damp_back
            weighted = pres_back * scaled
            back_x = back_x - rise_local(weighted, 2)
            back_y = back_y - rise_local(weighted, 3)
            back_z = back_z - rise_local(weighted, along=1)
            adjoint = scaled - (
                fall_local(vel_back * back_x, 2)
                + fall_local(vel_back * back_y, 3)
                + fall_local(vel_back * back_z, along=1)
            )
    shared = sum_at_owner(partial_grad, "shot", 1)
    gradient = gathered_copies(shared, "shot", 1)
    return (recording, gradient)


def solution(mesh):
    placed = (
        P("shot", "slab", None, None),
        P("shot", "slab", None, None),
        P("slab", None, None),
        P("slab", None, None),
        P("slab", None, None),
        P("slab", None, None),
        P("slab", None),
        P("slab"),
        P(),
        P("slab", "shot", None, None),
    )
    return jax.shard_map(
        body,
        mesh=mesh,
        in_specs=placed,
        out_specs=(P("slab", "shot", None, None), P("slab", None, None)),
        check_vma=False,
    )
```

profile of v0, /device:TPU:230, one launch (start us, length us, event | category | flops | bytes accessed | tf_op | source)
XLA Modules:
  0.0 71.0 jit_solution(1914778142855022713)
XLA Ops:
  0.6 0.0 copy-start
  0.6 1.0 %fusion.91 = (f32[2,2,32,256]{3,2,1,0:T(8,128)S(1)}, f32[2,2,32,256]{3,2,1,0:T(8,128)S(1)}) fusion(f32[2,8,32,256]{3,2,1,0:T(8,128)} %param.10), kind=kLoop, calls=%fused_computation.157 | loop fusion | bytes 524288 | tf_op jit(solution)/shard_map/slice | solution.py:109
  1.6 1.3 %divide_bitcast_fusion = (f32[1,8,32,256]{3,2,1,0:T(8,128)S(1)}, f32[1,8,32,256]{3,2,1,0:T(8,128)S(1)}, f32[1,8,32,256]{3,2,1,0:T(8,128)S(1)}) fusion(f32[8,32,256]{2,1,0:T(8,128)} %param.12, f32[8,32,256]{2,1,0:T(8,128)} %param.13, f32[8,32,256]{2,1,0:T(8,128)} %param.14, s32[8,32,256]{2,1,0:T(8,128)} %param.15), kind=kLoop, calls=%fused_computation.103 | loop fusion | flops 458752 | bytes 1835008 | tf_op jit(solution)/shard_map/stack | solution.py:105
  2.9 0.0 copy-start.4
  3.0 0.0 copy-start.3
  3.0 0.0 copy-start.5
  3.0 0.1 fusion.50
  3.0 5.0 %collective-permute-start = (f32[5,2,32,256]{3,2,1,0:T(8,128)S(1)}, f32[5,2,32,256]{3,2,1,0:T(8,128)S(1)}, u32[]{:S(2)}, u32[]{:S(2)}) collective-permute-start(f32[5,2,32,256]{3,2,1,0:T(8,128)S(1)} %get-tuple-element.37), channel_id=1, source_target_pairs={{0,8},{8,16},{16,24},{24,32},{32,40},{40,48},{48,56},{56,64},{64,7... | collective-permute-start | bytes 983048 | tf_op jit(solution)/shard_map/ppermute | solution.py:10
  8.0 1.9 %collective-permute-start.1 = (f32[5,2,32,256]{3,2,1,0:T(8,128)S(1)}, f32[5,2,32,256]{3,2,1,0:T(8,128)S(1)}, u32[]{:S(2)}, u32[]{:S(2)}) collective-permute-start(f32[5,2,32,256]{3,2,1,0:T(8,128)S(1)} %get-tuple-element.38), channel_id=1, source_target_pairs={{8,0},{16,8},{24,16},{32,24},{40,32},{48,40},{56,48},{64,56},{72,6... | collective-permute-start | bytes 983048 | tf_op jit(solution)/shard_map/ppermute | solution.py:10
  9.9 0.1 reshape.161
  10.1 0.1 fusion.56
  10.1 0.1 fusion.61
  10.2 0.6 fusion.94
  10.8 1.5 %fusion.89 = (f32[2,1,32,256]{3,2,1,0:T(8,128)}, f32[2,1,32,256]{3,2,1,0:T(8,128)S(1)}) fusion(f32[2,8,32,256]{3,2,1,0:T(8,128)} %param.11), kind=kLoop, calls=%fused_computation.155 | loop fusion | bytes 262144 | tf_op jit(solution)/shard_map/slice | solution.py:156
  12.3 2.6 %collective-permute-done = f32[5,2,32,256]{3,2,1,0:T(8,128)S(1)} collective-permute-done((f32[5,2,32,256]{3,2,1,0:T(8,128)S(1)}, f32[5,2,32,256]{3,2,1,0:T(8,128)S(1)}, u32[]{:S(2)}, u32[]{:S(2)}) %collective-permute-start) | collective-permute-done | bytes 327712 | tf_op jit(solution)/shard_map/ppermute | solution.py:10
  15.0 7.4 %collective-permute-done.1 = f32[5,2,32,256]{3,2,1,0:T(8,128)S(1)} collective-permute-done((f32[5,2,32,256]{3,2,1,0:T(8,128)S(1)}, f32[5,2,32,256]{3,2,1,0:T(8,128)S(1)}, u32[]{:S(2)}, u32[]{:S(2)}) %collective-permute-start.1) | collective-permute-done | bytes 327712 | tf_op jit(solution)/shard_map/ppermute | solution.py:10
  22.4 0.1 pad_maximum_fusion
  22.5 0.1 slice_bitcast_fusion.2
  22.6 0.0 copy-start.1
  22.6 0.9 %slice_bitcast_fusion.4 = (f32[10,32,256]{2,1,0:T(8,128)S(1)}, f32[10,32,256]{2,1,0:T(8,128)}, f32[10,32,256]{2,1,0:T(8,128)}) fusion(f32[3,12,32,256]{3,2,1,0:T(8,128)S(1)} %pad_maximum_fusion), kind=kLoop, calls=%fused_computation.90 | loop fusion | bytes 1966080 | tf_op jit(solution)/shard_map/mul | solution.py:188
  23.5 0.3 copy-done.1
  23.8 0.1 pad_maximum_fusion.1
  23.8 0.4 fusion.18
  24.3 0.5 broadcast_multiply_fusion.1
  24.8 0.5 fusion.23
  25.3 0.6 broadcast_multiply_fusion
  25.9 0.6 fusion.1
  26.6 0.1 reshape.164
  26.6 0.2 convolution_multiply_fusion.2
  26.8 0.2 convolution_bitcast_fusion.1
  27.1 0.1 mul.259
  27.1 0.5 fusion.54
  27.7 1.5 %pad_maximum_fusion.8 = f32[4,1,32,256]{3,2,1,0:T(8,128)} fusion(f32[2,1,32,256]{3,2,1,0:T(8,128)S(1)} %get-tuple-element.41, f32[2,1,32,256]{3,2,1,0:T(8,128)} %get-tuple-element.39), kind=kLoop, calls=%fused_computation.110 | loop fusion | flops 32768 | bytes 262144 | tf_op jit(solution)/shard_map/concatenate | solution.py:155
  29.2 1.9 %collective-permute-start.2 = (f32[4,1,32,256]{3,2,1,0:T(8,128)}, f32[4,1,32,256]{3,2,1,0:T(8,128)}, u32[]{:S(2)}, u32[]{:S(2)}) collective-permute-start(f32[4,1,32,256]{3,2,1,0:T(8,128)} %pad_maximum_fusion.8), channel_id=1, source_target_pairs={{0,8},{8,16},{16,24},{24,32},{32,40},{40,48},{48,56},{56,64},{64,7... | collective-permute-start | bytes 393224 | tf_op jit(solution)/shard_map/ppermute | solution.py:10
  31.1 0.7 pad_maximum_fusion.9
  31.7 3.9 %collective-permute-start.3 = (f32[4,1,32,256]{3,2,1,0:T(8,128)}, f32[4,1,32,256]{3,2,1,0:T(8,128)}, u32[]{:S(2)}, u32[]{:S(2)}) collective-permute-start(f32[4,1,32,256]{3,2,1,0:T(8,128)} %pad_maximum_fusion.9), channel_id=1, source_target_pairs={{8,0},{16,8},{24,16},{32,24},{40,32},{48,40},{56,48},{64,56},{72,6... | collective-permute-start | bytes 393224 | tf_op jit(solution)/shard_map/ppermute | solution.py:10
  35.7 0.6 fusion
  36.3 0.1 reshape.162
  36.4 0.8 %convolution_multiply_fusion.3 = f32[2,3,25]{2,1,0:T(4,128)S(1)} fusion(f32[2,3,32]{2,1,0:T(4,128)S(1)} %reshape.162, f32[32,25]{1,0:T(8,128)S(1)} %copy-done, f32[3]{0:T(128)} %copy-done.6), kind=kOutput, calls=%fused_computation.12 | convolution fusion | flops 57750 | bytes 4580 | tf_op jit(solution)/shard_map/src,ck->rsk/dot_general | solution.py:138
  37.2 0.9 %convolution_bitcast_fusion = f32[2,3,32]{2,1,0:T(4,128)S(1)} fusion(f32[32,25]{1,0:T(8,128)S(1)} %copy-done, f32[3,2,1,25]{3,2,1,0:T(1,128)} %get-tuple-element.51, f32[2,3,25]{2,1,0:T(4,128)S(1)} %convolution_multiply_fusion.3, f32[3]{0:T(128)} %copy-done.6), kind=kOutput, calls=%fused_computation.9 | convolution fusion | flops 57900 | bytes 5180 | tf_op jit(solution)/shard_map/rsk,ck->src/dot_general | solution.py:144
  38.1 0.1 mul.278
  38.2 0.5 fusion.52
  38.7 0.0 collective-permute-done.2
  38.7 0.9 %fusion.92 = (f32[2,1,32,256]{3,2,1,0:T(8,128)S(1)}, f32[2,1,32,256]{3,2,1,0:T(8,128)S(1)}) fusion(f32[4,1,32,256]{3,2,1,0:T(8,128)} %collective-permute-done.2), kind=kLoop, calls=%fused_computation.158 | loop fusion | bytes 262144 | tf_op jit(solution)/shard_map/slice | solution.py:161
  39.6 2.6 %collective-permute-done.3 = f32[4,1,32,256]{3,2,1,0:T(8,128)} collective-permute-done((f32[4,1,32,256]{3,2,1,0:T(8,128)}, f32[4,1,32,256]{3,2,1,0:T(8,128)}, u32[]{:S(2)}, u32[]{:S(2)}) %collective-permute-start.3) | collective-permute-done | bytes 131104 | tf_op jit(solution)/shard_map/ppermute | solution.py:10
  42.2 0.9 %fusion.93 = (f32[2,1,32,256]{3,2,1,0:T(8,128)S(1)}, f32[2,1,32,256]{3,2,1,0:T(8,128)S(1)}) fusion(f32[4,1,32,256]{3,2,1,0:T(8,128)} %collective-permute-done.3), kind=kLoop, calls=%fused_computation.159 | loop fusion | bytes 262144 | tf_op jit(solution)/shard_map/slice | solution.py:161
  43.1 1.5 %broadcast_multiply_fusion.2 = (f32[2,10,32,256]{3,2,1,0:T(8,128)S(1)}, f32[2,10,32,256]{3,2,1,0:T(8,128)S(1)}, f32[2,10,32,256]{3,2,1,0:T(8,128)S(1)}) fusion(f32[10,32,256]{2,1,0:T(8,128)} %get-tuple-element.23, f32[10,32,256]{2,1,0:T(8,128)} %get-tuple-element.24, f32[2,1,32,256]{3,2,1,0:T(8,128)S(1)} %get-tuple-element.50, ...), kind=kLoop, calls=%fused_computation.98 | loop fusion | flops 1146880 | bytes 3932160 | tf_op jit(solution)/shard_map/mul | solution.py:183
  44.6 0.3 fusion.39
  44.9 0.1 pad_slice_fusion.14
  45.0 0.1 pad_slice_fusion.16
  45.1 0.2 pad_slice_fusion.4
  45.3 0.1 fusion.48
  45.4 0.0 copy-start.2
  45.4 0.5 fusion.45
  46.0 0.4 copy-done.2
  46.4 0.1 multiply_subtract_fusion
  46.4 0.2 copy.45
  46.6 0.1 copy.46
  46.7 11.8 %all_to_all.10 = f32[8,8,4,256]{3,2,1,0:T(4,128)S(1)} all-to-all(f32[8,8,4,256]{3,2,1,0:T(4,128)S(1)} %copy.46), channel_id=1, replica_groups=mesh['slab'=64,'shot'=8] {'shot'}, dimensions={0} | all-to-all | bytes 524288 | tf_op jit(solution)/shard_map/all_to_all | solution.py:20
  58.5 0.7 %broadcast_in_dim.8 = f32[8,8,4,256]{3,2,1,0:T(4,128)} broadcast(f32[8,4,256]{2,1,0:T(4,128)S(1)} %reduce_sum.49), dimensions={1,2,3} | broadcast | bytes 294912 | tf_op jit(solution)/shard_map/broadcast_in_dim | solution.py:31
  59.3 3.4 %all-to-all-start.1 = ((f32[8,8,4,256]{3,2,1,0:T(4,128)}), f32[8,8,4,256]{3,2,1,0:T(4,128)S(1)}, u32[]{:S(2)}, u32[]{:S(2)}) async-start(f32[8,8,4,256]{3,2,1,0:T(4,128)} %broadcast_in_dim.8), calls=%async_computation.1 | async-start | bytes 524288 | tf_op jit(solution)/shard_map/all_to_all | solution.py:32
  62.7 0.6 copy.48
  63.3 6.8 %all-to-all-done.1 = f32[8,8,4,256]{3,2,1,0:T(4,128)S(1)} async-done(((f32[8,8,4,256]{3,2,1,0:T(4,128)}), f32[8,8,4,256]{3,2,1,0:T(4,128)S(1)}, u32[]{:S(2)}, u32[]{:S(2)}) %all-to-all-start.1) | async-done | bytes 262176 | tf_op jit(solution)/shard_map/all_to_all | solution.py:32
  70.2 0.8 %copy.49 = f32[8,32,256]{2,1,0:T(8,128)} copy(f32[8,32,256]{2,0,1:T(8,128)S(1)} %bitcast.91) | data formatting | bytes 524288
  (18 shorter events, 0.2 us)
Async XLA Ops:
  0.6 26.0 %copy-start = (f32[32,25]{1,0:T(8,128)S(1)}, f32[32,25]{1,0:T(8,128)}, u32[]{:S(2)}) copy-start(f32[32,25]{1,0:T(8,128)} %param.18) | copy-start | bytes 9604
  2.9 7.0 %copy-start.4 = (s32[3,32]{1,0:T(4,128)S(1)}, s32[3,32]{1,0:T(4,128)}, u32[]{:S(2)}) copy-start(s32[3,32]{1,0:T(4,128)} %param.16) | copy-start | bytes 1156
  3.0 7.3 %copy-start.3 = (f32[3,2,2,25]{3,2,1,0:T(2,128)S(1)}, f32[3,2,2,25]{3,2,1,0:T(2,128)}, u32[]{:S(2)}) copy-start(f32[3,2,2,25]{3,2,1,0:T(2,128)} %param.19) | copy-start | bytes 3604
  3.0 7.9 %copy-start.5 = (s32[3]{0:T(128)S(1)}, s32[3]{0:T(128)}, u32[]{:S(2)}) copy-start(s32[3]{0:T(128)} %param.17) | copy-start | bytes 40
  3.0 11.9 %collective-permute-start = (f32[5,2,32,256]{3,2,1,0:T(8,128)S(1)}, f32[5,2,32,256]{3,2,1,0:T(8,128)S(1)}, u32[]{:S(2)}, u32[]{:S(2)}) collective-permute-start(f32[5,2,32,256]{3,2,1,0:T(8,128)S(1)} %get-tuple-element.37), channel_id=1, source_target_pairs={{0,8},{8,16},{16,24},{24,32},{32,40},{40,48},{48,56},{56,64},{64,7... | collective-permute-start | bytes 983048 | tf_op jit(solution)/shard_map/ppermute | solution.py:10
  8.0 14.4 %collective-permute-start.1 = (f32[5,2,32,256]{3,2,1,0:T(8,128)S(1)}, f32[5,2,32,256]{3,2,1,0:T(8,128)S(1)}, u32[]{:S(2)}, u32[]{:S(2)}) collective-permute-start(f32[5,2,32,256]{3,2,1,0:T(8,128)S(1)} %get-tuple-element.38), channel_id=1, source_target_pairs={{8,0},{16,8},{24,16},{32,24},{40,32},{48,40},{56,48},{64,56},{72,6... | collective-permute-start | bytes 983048 | tf_op jit(solution)/shard_map/ppermute | solution.py:10
  10.8 16.0 %copy-start.6 = (f32[3]{0:T(128)}, f32[3]{0:T(128)S(1)}, u32[]{:S(2)}) copy-start(f32[3]{0:T(128)S(1)} %convert_element_type.55) | copy-start | bytes 40
  22.6 1.2 %copy-start.1 = (f32[2,8,32,256]{3,2,1,0:T(8,128)S(1)}, f32[2,8,32,256]{3,2,1,0:T(8,128)}, u32[]{:S(2)}) copy-start(f32[2,8,32,256]{3,2,1,0:T(8,128)} %param.10) | copy-start | bytes 1572868
  29.2 9.6 %collective-permute-start.2 = (f32[4,1,32,256]{3,2,1,0:T(8,128)}, f32[4,1,32,256]{3,2,1,0:T(8,128)}, u32[]{:S(2)}, u32[]{:S(2)}) collective-permute-start(f32[4,1,32,256]{3,2,1,0:T(8,128)} %pad_maximum_fusion.8), channel_id=1, source_target_pairs={{0,8},{8,16},{16,24},{24,32},{32,40},{40,48},{48,56},{56,64},{64,7... | collective-permute-start | bytes 393224 | tf_op jit(solution)/shard_map/ppermute | solution.py:10
  31.7 10.5 %collective-permute-start.3 = (f32[4,1,32,256]{3,2,1,0:T(8,128)}, f32[4,1,32,256]{3,2,1,0:T(8,128)}, u32[]{:S(2)}, u32[]{:S(2)}) collective-permute-start(f32[4,1,32,256]{3,2,1,0:T(8,128)} %pad_maximum_fusion.9), channel_id=1, source_target_pairs={{8,0},{16,8},{24,16},{32,24},{40,32},{48,40},{56,48},{64,56},{72,6... | collective-permute-start | bytes 393224 | tf_op jit(solution)/shard_map/ppermute | solution.py:10
  45.4 1.0 %copy-start.2 = (s32[8,32,256]{2,1,0:T(8,128)S(1)}, s32[8,32,256]{2,1,0:T(8,128)}, u32[]{:S(2)}) copy-start(s32[8,32,256]{2,1,0:T(8,128)} %param.15) | copy-start | bytes 786436
  59.3 10.9 %all-to-all-start.1 = ((f32[8,8,4,256]{3,2,1,0:T(4,128)}), f32[8,8,4,256]{3,2,1,0:T(4,128)S(1)}, u32[]{:S(2)}, u32[]{:S(2)}) async-start(f32[8,8,4,256]{3,2,1,0:T(4,128)} %broadcast_in_dim.8), calls=%async_computation.1 | async-start | bytes 524288 | tf_op jit(solution)/shard_map/all_to_all | solution.py:32
where the time goes:
time: 71.7 us; the launch traced here: 71 us
  waiting for transfers between devices  19.5 us (27%)
  starting transfers between devices  16.1 us (22%)
  blocking collectives  11.8 us (16%)
  local copies, waits for them, and re-layouts  9.8 us (14%)
  other arithmetic  8.41 us (12%)
  matrix products  4.4 us (6%)
  between operations  1 us (1%)
    ppermute x4, starting transfers between devices, from_behind(): lax.ppermute(value, axis, [(source, source + steps) for source in range(l...  12.7 us
    ppermute x4, waiting for transfers between devices, from_behind(): lax.ppermute(value, axis, [(source, source + steps) for source in range(l...  12.6 us
    all_to_all x1, blocking collectives, sum_at_owner(): lax.all_to_all(tiles, axis, split_axis=0, concat_axis=0, tiled=True)  11.8 us
    all_to_all x1, waiting for transfers between devices, copy_for_each(): return lax.all_to_all(copies, axis, split_axis=0, concat_axis=0, tiled=True)  6.82 us
    all_to_all x1, starting transfers between devices, copy_for_each(): return lax.all_to_all(copies, axis, split_axis=0, concat_axis=0, tiled=True)  3.41 us
    unnamed x16, local copies, waits for them, and re-layouts  2.07 us
    slice x1, local copies, waits for them, and re-layouts, body(): adjoint_init[:, slab_depth - back_margin:]  1.51 us
    concatenate x1, other arithmetic, body(): jnp.concatenate([adjoint_init[:, slab_depth - back_margin:]] + [dense[1][...  1.5 us
  transfers between devices with their start and end apart: 5, of which 4 were waited for; matrix products, arithmetic and copies ran while one was open for 11% of the time, Pallas kernels for 0%

commit v1 on v0

v1 whole, which is shorter than its diff:
```python
import functools

import jax
import jax.numpy as jnp
from jax import lax
from jax.experimental import pallas as pl
from jax.experimental.pallas import tpu as pltpu
from jax.sharding import PartitionSpec as P

LANES = 128
FAR = float(1 << 20)
TINY = 16
VMEM = pltpu.VMEM
F32 = jnp.float32


def dot(a, b, contract):
    return lax.dot_general(
        a, b, ((contract[:1], contract[1:]), ((), ())),
        precision=lax.Precision.HIGHEST, preferred_element_type=F32,
    )


def edge_masks(shape):
    row = lax.broadcasted_iota(jnp.int32, shape, 0)
    col = lax.broadcasted_iota(jnp.int32, shape, 1)
    return row > 0, row < shape[0] - 1, col > 0, col < shape[1] - 1


def plane_weights(vel, masks):
    low_x, high_x, low_y, high_y = masks
    xp = jnp.where(high_x, vel, 0.0)
    xm = jnp.where(low_x, pltpu.roll(vel, 1, 0), 0.0)
    yp = jnp.where(high_y, vel, 0.0)
    ym = jnp.where(low_y, pltpu.roll(vel, 1, 1), 0.0)
    return xp, xm, yp, ym, 2.0 * vel + xm + ym


def plane_part(u, weights):
    xp, xm, yp, ym, centre = weights
    rows, cols = u.shape
    return (
        xp * pltpu.roll(u, rows - 1, 0) + xm * pltpu.roll(u, 1, 0)
        + yp * pltpu.roll(u, cols - 1, 1) + ym * pltpu.roll(u, 1, 1)
        - centre * u
    )


def pick_columns(cols, width):
    return (lax.broadcasted_iota(jnp.int32, (width, cols.shape[1]), 0) == cols).astype(F32)


def pick_rows(rows, count):
    return (lax.broadcasted_iota(jnp.int32, (count, rows.shape[1]), 0) == rows).astype(F32)


def split_cells(cells, width_x, width_y):
    whole = cells.astype(jnp.int32)
    plane = lax.div(whole, width_x * width_y)
    row = lax.div(whole, width_y)
    return plane, row, row - plane * width_x, whole - row * width_y


def edge_kernel(
    p0, adj_low, adj_high, density, speed, admittance, mask, aux,
    first, up, down, vel_s, pd_s, stack,
):
    shots, depth, width_x, width_y = p0.shape
    masks = edge_masks((width_x, width_y))
    last = depth - 1

    def weights(z):
        return plane_weights(vel_s[z], masks)

    for z in range(depth):
        dens = density[z]
        vel = 0.5 / dens
        spd = speed[z]
        pres = 0.5 * dens * spd * spd
        vel_s[z] = vel
        damp = 1.0 - admittance[z] * mask[z].astype(F32)
        pd_s[z] = pres * damp
        w = plane_weights(vel, masks)
        for s in range(shots):
            here = p0[s, z]
            total = plane_part(here, w)
            if z < last:
                total += vel * (p0[s, z + 1] - here)
            if z > 0:
                total -= vel_s[z - 1] * (here - p0[s, z - 1])
            first[s, z] = here + pres * total

    def damp_of(z):
        return 1.0 - admittance[z] * mask[z].astype(F32)

    plane, _, row_x, col = split_cells(aux[0:1, :], width_x, width_y)
    for side in range(2):
        if side == 0:
            out, near, far, third, adj = down, 0, 1, 2, adj_low
            vel_out = vel_s[0]
        else:
            out, near, far, third, adj = up, last, last - 1, last - 2, adj_high
            vel_out = vel_s[last - 1]
        damp_near, damp_far = damp_of(near), damp_of(far)
        pd_near, pd_far = pd_s[near], pd_s[far]
        vel_near = vel_s[near]
        w_far = weights(far)
        beyond = vel_s[far] if side == 0 else vel_s[third]
        damp_third = damp_of(third)
        base = side * 7 * width_x

        def put(k, value):
            stack[base + k * width_x : base + (k + 1) * width_x, :] = value

        for s in range(shots):
            out[s * width_x : (s + 1) * width_x, :] = p0[s, near]
            out[(2 + s) * width_x : (3 + s) * width_x, :] = damp_near * first[s, near]
            out[(4 + s) * width_x : (5 + s) * width_x, :] = pd_near * adj[s, 0]
            p1_far = damp_far * first[s, far]
            q_far = p0[s, far] + p1_far
            q_third = p0[s, third] + damp_third * first[s, third]
            total = plane_part(q_far, w_far) + beyond * (q_third - q_far) - vel_out * q_far
            put(s, pd_near * vel_out * q_far)
            put(4 + s, damp_far * p1_far + pd_far * total)
        out[6 * width_x : 7 * width_x, :] = vel_near
        out[7 * width_x : 8 * width_x, :] = pd_near
        put(2, damp_near)
        put(3, pd_near * vel_out)
        put(6, pd_far * vel_out)
    columns = pick_columns(col, width_y)
    rows = pick_rows(row_x, width_x)
    found = dot(stack[...], columns, (1, 0))
    for side in range(2):
        out, near, far = (down, 0, 1) if side == 0 else (up, last, last - 1)
        is_near = (plane == near).astype(F32)
        is_far = (plane == far).astype(F32)

        def got(k):
            start = (side * 7 + k) * width_x
            return jnp.sum(found[start : start + width_x, :] * rows, axis=0, keepdims=True)

        tiny = [is_near * got(s) + is_far * got(4 + s) for s in range(shots)]
        tiny += [
            is_near * got(2), is_far * got(6) - is_near * got(3), is_near,
            row_x.astype(F32), col.astype(F32), aux[1:2, :], aux[4:5, :], aux[5:6, :],
        ]
        tiny.append(jnp.zeros((TINY - len(tiny), LANES), F32))
        start = 8 * width_x
        out[start : start + TINY, :] = jnp.zeros((TINY, width_y), F32)
        out[start : start + TINY, 0:LANES] = jnp.concatenate(tiny, axis=0)


def main_kernel(
    core, p0, adj, first, density, speed, admittance, mask, below, above, aux, bd,
    keep, send, coded,
    vel_s, pres_s, damp_s, q_s, p1_s, b2_s, p2_s, w_s, halo_s, src_s, grad_s, b1_edge,
):
    shots, depth, width_x, width_y = p0.shape
    masks = edge_masks((width_x, width_y))
    last = depth - 1
    plane_cells = depth * width_x
    encode = bd[...]
    for z in range(depth):
        dens = density[z]
        spd = speed[z]
        vel_s[z] = 0.5 / dens
        pres_s[z] = 0.5 * dens * spd * spd
        damp_s[z] = 1.0 - admittance[z] * mask[z].astype(F32)

    def halo(ref, k):
        return ref[k * width_x : (k + 1) * width_x, :]

    q_halo, flux = [], []
    for side, (ref, edge, sign) in enumerate(((below, 0, 1.0), (above, last, -1.0))):
        vel_h, pd_h = halo(ref, 6), halo(ref, 7)
        w_h = plane_weights(vel_h, masks)
        vel_b = vel_h if side == 0 else vel_s[last]
        for s in range(shots):
            here, out = p0[s, edge], halo(ref, s)
            step = vel_b * (here - out)
            fixed = first[s, edge] - pres_s[edge] * step
            p1_h = halo(ref, 2 + s) + pd_h * step
            q_h = out + p1_h
            q_edge = here + damp_s[edge] * fixed
            step2 = vel_b * (q_edge - q_h)
            x_h = pd_h * (plane_part(q_h, w_h) + step2)
            base = side * 6 * width_x
            halo_s[base + s * width_x : base + (s + 1) * width_x, :] = p1_h
            halo_s[base + (2 + s) * width_x : base + (3 + s) * width_x, :] = q_h
            halo_s[base + (4 + s) * width_x : base + (5 + s) * width_x, :] = x_h
            b1_edge[s, side] = fixed
            flux.append(step2)
    def b1_of(s, z):
        return b1_edge[s, min(z, 1)] if z in (0, last) else first[s, z]

    for s in range(shots):
        for z in range(depth):
            p1 = damp_s[z] * b1_of(s, z)
            row = s * plane_cells + z * width_x
            p1_s[row : row + width_x, :] = p1
            q_s[s, z] = p0[s, z] + p1
    for z in range(depth):
        vel = vel_s[z]
        w = plane_weights(vel, masks)
        for s in range(shots):
            row = s * plane_cells + z * width_x
            here = q_s[s, z]
            total = plane_part(here, w)
            if z < last:
                total += vel * (q_s[s, z + 1] - here)
            else:
                total -= flux[shots + s]
            if z > 0:
                total -= vel_s[z - 1] * (here - q_s[s, z - 1])
            else:
                total -= flux[s]
            b2 = p1_s[row : row + width_x, :] + pres_s[z] * total
            b2_s[s, z] = b2
            p2_s[row : row + width_x, :] = damp_s[z] * b2
    plane, row, _, col = split_cells(aux[0:1, :], width_x, width_y)
    columns = pick_columns(col, width_y)
    rows = pick_rows(row, plane_cells)
    live = aux[1:2, :]
    for n, field in enumerate((p1_s, p2_s)):
        found = dot(field[...], columns, (1, 0))
        lines = [
            jnp.sum(found[s * plane_cells : (s + 1) * plane_cells, :] * rows, axis=0, keepdims=True)
            for s in range(shots)
        ]
        got = jnp.concatenate(lines + [jnp.zeros((8 - shots, LANES), F32)], axis=0)
        signals = dot(got, encode, (1, 0)) * live
        coded[n * 8 : (n + 1) * 8, :] = signals
        goal = jnp.concatenate(
            [aux[2 + 2 * n : 4 + 2 * n, :], jnp.zeros((8 - shots, LANES), F32)], axis=0
        )
        source = dot(signals - goal, encode, (1, 1))
        spread = jnp.concatenate([rows * source[s : s + 1, :] for s in range(shots)], axis=0)
        src_s[n] = dot(spread, columns, (1, 1))
    w_halo = []
    for side, ref in enumerate((below, above)):
        start = 8 * width_x
        tiny = ref[start : start + TINY, 0:LANES]
        near = tiny[4:5, :]
        rows_h = pick_rows(tiny[5:6, :].astype(jnp.int32), width_x)
        columns_h = pick_columns(tiny[6:7, :].astype(jnp.int32), width_y)
        base = side * 6 * width_x
        found = dot(halo_s[base : base + 6 * width_x, :], columns_h, (1, 0))

        def got_h(k):
            return jnp.sum(found[k * width_x : (k + 1) * width_x, :] * rows_h, axis=0, keepdims=True)

        lines = [
            tiny[s : s + 1, :] + tiny[2:3, :] * got_h(s) + tiny[3:4, :] * got_h(2 + s) + near * got_h(4 + s)
            for s in range(shots)
        ]
        got = jnp.concatenate(lines + [jnp.zeros((8 - shots, LANES), F32)], axis=0)
        goal = jnp.concatenate([tiny[8:10, :], jnp.zeros((8 - shots, LANES), F32)], axis=0)
        misfit = dot(got, encode, (1, 0)) * tiny[7:8, :] - goal
        source = dot(misfit, encode, (1, 1)) * near
        spread = jnp.concatenate([rows_h * source[s : s + 1, :] for s in range(shots)], axis=0)
        placed = dot(spread, columns_h, (1, 1))
        pd_h = halo(ref, 7)
        for s in range(shots):
            w_halo.append(halo(ref, 4 + s) + pd_h * placed[s * width_x : (s + 1) * width_x, :])
    for s in range(shots):
        for z in range(depth):
            row = s * plane_cells + z * width_x
            scaled = damp_s[z] * (adj[s, z] + src_s[1, row : row + width_x, :])
            q_s[s, z] = scaled
            w_s[s, z] = pres_s[z] * scaled
    for z in range(depth):
        vel = vel_s[z]
        w = plane_weights(vel, masks)
        grad = jnp.zeros((width_x, width_y), F32)
        for s in range(shots):
            row = s * plane_cells + z * width_x
            here = w_s[s, z]
            above_w = w_s[s, z + 1] if z < last else w_halo[shots + s]
            total = plane_part(here, w) + vel * (above_w - here)
            if z > 0:
                total -= vel_s[z - 1] * (here - w_s[s, z - 1])
            else:
                total -= halo(below, 6) * (here - w_halo[s])
            back = q_s[s, z] + total + src_s[0, row : row + width_x, :]
            adj1 = adj[s, z] + src_s[1, row : row + width_x, :]
            grad += b2_s[s, z] * adj1 + b1_of(s, z) * back
        grad_s[z] = -(mask[z].astype(F32) * grad)
    half = depth // 2
    mine = core[0] * half
    other = half - mine
    for z in range(half):
        keep[z] = grad_s[mine + z]
        send[z] = grad_s[other + z]


def whole(shape):
    return pl.BlockSpec(shape, lambda i: (0,) * len(shape))


def body(
    pressure_init, adjoint_init, density, speed, admittance, bound_mask,
    rec_cells, rec_live, encoder, target,
):
    shots, depth, width_x, width_y = pressure_init.shape
    slots, capsules = rec_cells.shape
    steps, channels = target.shape[2:]
    slabs, peers = lax.axis_size("slab"), lax.axis_size("shot")
    field = (shots, depth, width_x, width_y)
    slab = (depth, width_x, width_y)
    plane_rows = width_x
    message = (8 * plane_rows + TINY, width_y)

    spare = LANES - slots * capsules
    cells = jnp.pad(rec_cells.reshape(1, -1).astype(F32), ((0, 0), (0, spare)), constant_values=FAR)
    live = rec_live.astype(F32)[:, None]
    live_row = jnp.pad(jnp.broadcast_to(live, (slots, capsules)).reshape(1, -1), ((0, 0), (0, spare)))
    goal = jnp.transpose(target * live[:, :, None, None], (2, 1, 0, 3))
    goal = jnp.pad(goal, ((0, 0),) * 3 + ((0, capsules - channels),)).reshape(steps * shots, -1)
    goal = jnp.pad(goal, ((0, 2), (0, spare)))
    aux = jnp.concatenate([cells, live_row, goal], axis=0)
    padded = jnp.pad(encoder, ((0, 0), (0, capsules - channels)))
    bd = jnp.einsum("ab,ck->acbk", jnp.eye(slots, dtype=F32), padded)
    bd = jnp.pad(bd.reshape(slots * capsules, -1), ((0, spare), (0, spare)))

    edge_plane = (shots, 1, width_x, width_y)
    first, up, down = pl.pallas_call(
        edge_kernel,
        grid=(1,),
        in_specs=[
            whole(field),
            pl.BlockSpec(edge_plane, lambda i: (0, 0, 0, 0)),
            pl.BlockSpec(edge_plane, lambda i: (0, depth - 1, 0, 0)),
            whole(slab), whole(slab), whole(slab), whole(slab), whole(aux.shape),
        ],
        out_specs=[whole(field), whole(message), whole(message)],
        out_shape=[
            jax.ShapeDtypeStruct(field, F32),
            jax.ShapeDtypeStruct(message, F32),
            jax.ShapeDtypeStruct(message, F32),
        ],
        scratch_shapes=[VMEM(slab, F32), VMEM(slab, F32), VMEM((14 * plane_rows, width_y), F32)],
        name="edge",
    )(pressure_init, adjoint_init, adjoint_init, density, speed, admittance, bound_mask, aux)

    below = lax.ppermute(up, "slab", [(i, i + 1) for i in range(slabs - 1)])
    above = lax.ppermute(down, "slab", [(i + 1, i) for i in range(slabs - 1)])

    place = lax.axis_index("shot")
    core = lax.rem(place, 2)
    half = (depth // 2, width_x, width_y)
    flat = (shots * depth * width_x, width_y)
    keep, send, coded = pl.pallas_call(
        main_kernel,
        grid=(1,),
        in_specs=[
            pl.BlockSpec(memory_space=pltpu.SMEM),
            whole(field), whole(field), whole(field),
            whole(slab), whole(slab), whole(slab), whole(slab),
            whole(message), whole(message), whole(aux.shape), whole(bd.shape),
        ],
        out_specs=[whole(half), whole(half), whole((8 * steps, LANES))],
        out_shape=[
            jax.ShapeDtypeStruct(half, F32),
            jax.ShapeDtypeStruct(half, F32),
            jax.ShapeDtypeStruct((8 * steps, LANES), F32),
        ],
        scratch_shapes=[
            VMEM(slab, F32), VMEM(slab, F32), VMEM(slab, F32),
            VMEM(field, F32), VMEM(flat, F32), VMEM(field, F32), VMEM(flat, F32), VMEM(field, F32),
            VMEM((12 * plane_rows, width_y), F32), VMEM((steps, *flat), F32), VMEM(slab, F32),
            VMEM((shots, 2, width_x, width_y), F32),
        ],
        name="main",
    )(
        core[None], pressure_init, adjoint_init, first, density, speed, admittance, bound_mask,
        below, above, aux, bd,
    )

    pairs = [(i, i ^ 1) for i in range(peers)]
    groups = [list(range(c, peers, 2)) for c in range(2)]
    total = keep + lax.ppermute(send, "shot", pairs)
    copies = jnp.broadcast_to(total, (peers // 2, *half))
    total = lax.all_to_all(
        copies, "shot", split_axis=0, concat_axis=0, tiled=True, axis_index_groups=groups
    ).sum(axis=0)
    other = lax.ppermute(total, "shot", pairs)
    gradient = jnp.where(
        core == 0, jnp.concatenate([total, other], 0), jnp.concatenate([other, total], 0)
    )
    signals = coded.reshape(steps, 8, LANES)[:, :shots, : slots * capsules]
    signals = signals.reshape(steps, shots, slots, capsules)[..., :channels]
    return jnp.transpose(signals, (2, 1, 0, 3)), gradient


def solution(mesh):
    placed = (
        P("shot", "slab", None, None), P("shot", "slab", None, None),
        P("slab", None, None), P("slab", None, None), P("slab", None, None), P("slab", None, None),
        P("slab", None), P("slab"), P(), P("slab", "shot", None, None),
    )
    return jax.shard_map(
        body, mesh=mesh, in_specs=placed,
        out_specs=(P("slab", "shot", None, None), P("slab", None, None)),
        check_vma=False,
    )
```

time: 71.7 us -> 58.6 us (0.82)
  the two profiles are of different devices: /device:TPU:230 before, /device:TPU:103 now
where the time goes in v1:
time: 58.6 us; the launch traced here: 58.1 us
  waiting for transfers between devices  19.5 us (33%)
  starting transfers between devices  18 us (31%)
  Pallas kernels  11.5 us (20%)
  local copies, waits for them, and re-layouts  4.57 us (8%)
  other arithmetic  3.82 us (7%)
  between operations  0.72 us (1%)
    all_to_all x1, waiting for transfers between devices, body(): lax.all_to_all(copies, 'shot', split_axis=0, concat_axis=0, tiled=True, a...  8.15 us
    pallas_call x1, Pallas kernels, body(): pl.pallas_call(main_kernel, grid=(1,), in_specs=[pl.BlockSpec(memory_spac...  8.1 us
    ppermute x1, waiting for transfers between devices, body(): above = lax.ppermute(down, 'slab', [(i + 1, i) for i in range(slabs - 1)])  7.05 us
    ppermute x1, starting transfers between devices, body(): below = lax.ppermute(up, 'slab', [(i, i + 1) for i in range(slabs - 1)])  4.79 us
    all_to_all x1, starting transfers between devices, body(): lax.all_to_all(copies, 'shot', split_axis=0, concat_axis=0, tiled=True, a...  4.19 us
    ppermute x1, starting transfers between devices, body(): total = keep + lax.ppermute(send, 'shot', pairs)  3.7 us
    ppermute x1, starting transfers between devices, body(): other = lax.ppermute(total, 'shot', pairs)  3.41 us
    pallas_call x1, Pallas kernels, body(): pl.pallas_call(edge_kernel, grid=(1,), in_specs=[whole(field), pl.BlockSp...  3.38 us
  transfers between devices with their start and end apart: 5, of which 5 were waited for; matrix products, arithmetic and copies ran while one was open for 4% of the time, Pallas kernels for 0%

profile of v1, /device:TPU:103, one launch (start us, length us, event | category | flops | bytes accessed | tf_op | source)
XLA Modules:
  0.0 58.1 jit_solution(8759136191331093959)
XLA Ops:
  0.6 0.7 %convert_element_type.30 = f32[3]{0:T(128)S(1)} convert(s32[3]{0:T(128)} %param.17) | non-fusion elementwise | flops 3 | bytes 24 | tf_op jit(solution)/shard_map/convert_element_type | solution.py:315
  1.3 0.8 %multiply_bitcast_fusion.1 = f32[2,2,3,25]{3,0,1,2:T(2,128)S(1)} fusion(f32[3,2,2,25]{3,2,1,0:T(2,128)} %param.19, f32[3]{0:T(128)S(1)} %convert_element_type.30), kind=kLoop, calls=%fused_computation.5 | loop fusion | flops 300 | bytes 2412 | tf_op jit(solution)/shard_map/transpose | solution.py:317
  2.1 0.1 reshape.36
  2.2 0.0 copy-start.3
  2.2 0.1 broadcast_in_dim.13
  2.2 0.1 reshape.35
  2.3 0.5 copy-done.3
  2.8 0.1 convert_element_type.29
  2.9 0.6 %select_maximum_fusion.aux = f32[8,128]{1,0:T(8,128)} fusion(f32[4,96]{1,0:T(4,128)S(1)} %reshape.36, f32[1,96]{1,0:T(1,128)S(1)} %reshape.35, f32[1,96]{1,0:T(1,128)S(1)} %convert_element_type.29), kind=kLoop, calls=%fused_computation.6 | loop fusion | flops 10240 | bytes 6400 | tf_op jit(solution)/shard_map/concatenate | solution.py:320
  3.5 3.4 %edge.1 = (f32[2,8,32,256]{3,2,1,0:T(8,128)}, f32[272,256]{1,0:T(8,128)}, f32[272,256]{1,0:T(8,128)}) custom-call(f32[2,8,32,256]{3,2,1,0:T(8,128)} %p0.3, f32[2,8,32,256]{3,2,1,0:T(8,128)} %adj.1, f32[2,8,32,256]{3,2,1,0:T(8,128)} %adj.1, f32[8,32,256]{2,1,0:T(8,128)} %density.3, f32[8,32,256]{2,1,0:T(8,128)} %speed.3, f32[8,32,256]{2,1,0:T(8,128)} %admittance.3, ...), custom_call_target="tpu_custom_call" | custom-call | tf_op jit(solution)/shard_map/edge/pallas_call | solution.py:326
  6.9 0.0 copy-start.2
  6.9 4.8 %collective-permute-start = (f32[272,256]{1,0:T(8,128)}, f32[272,256]{1,0:T(8,128)S(1)}, u32[]{:S(2)}, u32[]{:S(2)}) collective-permute-start(f32[272,256]{1,0:T(8,128)} %get-tuple-element.9), channel_id=1, source_target_pairs={{0,8},{8,16},{16,24},{24,32},{32,40},{40,48},{48,56},{56,64},{64,7... | collective-permute-start | bytes 835592 | tf_op jit(solution)/shard_map/ppermute | solution.py:345
  11.7 1.9 %collective-permute-start.1 = (f32[272,256]{1,0:T(8,128)}, f32[272,256]{1,0:T(8,128)S(1)}, u32[]{:S(2)}, u32[]{:S(2)}) collective-permute-start(f32[272,256]{1,0:T(8,128)} %get-tuple-element.10), channel_id=1, source_target_pairs={{8,0},{16,8},{24,16},{32,24},{40,32},{48,40},{56,48},{64,56},{72,6... | collective-permute-start | bytes 835592 | tf_op jit(solution)/shard_map/ppermute | solution.py:346
  13.7 0.0 copy-done.2
  13.7 0.1 multiply_bitcast_fusion
  13.8 0.1 reshape.37
  13.9 0.6 %pad.29.bd = f32[128,128]{1,0:T(8,128)} pad(f32[96,96]{1,0:T(8,128)S(1)} %reshape.37, f32[]{:T(128)} %constant.14.clone.1), padding=0_32x0_32 | pad | bytes 102404 | tf_op jit(solution)/shard_map/jit(_pad)/pad | solution.py:323
  14.5 2.8 %collective-permute-done.below = f32[272,256]{1,0:T(8,128)S(1)} collective-permute-done((f32[272,256]{1,0:T(8,128)}, f32[272,256]{1,0:T(8,128)S(1)}, u32[]{:S(2)}, u32[]{:S(2)}) %collective-permute-start) | collective-permute-done | bytes 278560 | tf_op jit(solution)/shard_map/ppermute | solution.py:345
  17.3 0.0 copy-start
  17.3 7.0 %collective-permute-done.1.above = f32[272,256]{1,0:T(8,128)S(1)} collective-permute-done((f32[272,256]{1,0:T(8,128)}, f32[272,256]{1,0:T(8,128)S(1)}, u32[]{:S(2)}, u32[]{:S(2)}) %collective-permute-start.1) | collective-permute-done | bytes 278560 | tf_op jit(solution)/shard_map/ppermute | solution.py:346
  24.4 0.0 copy-start.1
  24.4 0.0 copy-done
  24.4 0.7 %copy-done.1 = f32[272,256]{1,0:T(8,128)} copy-done((f32[272,256]{1,0:T(8,128)}, f32[272,256]{1,0:T(8,128)S(1)}, u32[]{:S(2)}) %copy-start.1) | copy-done | bytes 278552
  25.1 8.1 %main.1 = (f32[4,32,256]{2,1,0:T(8,128)}, f32[4,32,256]{2,1,0:T(8,128)}, f32[16,128]{1,0:T(8,128)}) custom-call(s32[1]{0:T(128)} %bitcast.core, f32[2,8,32,256]{3,2,1,0:T(8,128)} %p0.3, f32[2,8,32,256]{3,2,1,0:T(8,128)} %adj.1, f32[2,8,32,256]{3,2,1,0:T(8,128)} %get-tuple-element.8.first, f32[8,32,256]{2,1,0:T(8,128)} %density.3, f32[8,32,256]{2,1,0:T(8,128)} %speed.3, ...), custom_call_target="tpu_custom_call" | custom-call | tf_op jit(solution)/shard_map/main/pallas_call | solution.py:352
  33.2 3.7 %collective-permute-start.2 = (f32[4,32,256]{2,1,0:T(8,128)}, f32[4,32,256]{2,1,0:T(8,128)S(1)}, u32[]{:S(2)}, u32[]{:S(2)}) collective-permute-start(f32[4,32,256]{2,1,0:T(8,128)} %get-tuple-element.13), channel_id=1, source_target_pairs={{0,1},{1,0},{2,3},{3,2},{4,5},{5,4},{6,7},{7,6},{8,9},{9,8},{10,11... | collective-permute-start | bytes 393224 | tf_op jit(solution)/shard_map/ppermute | solution.py:381
  36.9 1.2 %collective-permute-done.2 = f32[4,32,256]{2,1,0:T(8,128)S(1)} collective-permute-done((f32[4,32,256]{2,1,0:T(8,128)}, f32[4,32,256]{2,1,0:T(8,128)S(1)}, u32[]{:S(2)}, u32[]{:S(2)}) %collective-permute-start.2) | collective-permute-done | bytes 131104 | tf_op jit(solution)/shard_map/ppermute | solution.py:381
  38.1 0.9 %add.15 = f32[4,32,256]{2,1,0:T(8,128)S(1)} add(f32[4,32,256]{2,1,0:T(8,128)} %get-tuple-element.12, f32[4,32,256]{2,1,0:T(8,128)S(1)} %collective-permute-done.2) | non-fusion elementwise | flops 32768 | bytes 393216 | tf_op jit(solution)/shard_map/add | solution.py:381
  39.0 0.8 %broadcast_in_dim.14 = f32[4,4,32,256]{3,2,1,0:T(8,128)} broadcast(f32[4,32,256]{2,1,0:T(8,128)S(1)} %add.15), dimensions={1,2,3} | broadcast | bytes 655360 | tf_op jit(solution)/shard_map/broadcast_in_dim | solution.py:382
  39.9 4.2 %all-to-all-start = ((f32[4,4,32,256]{3,2,1,0:T(8,128)}), f32[4,4,32,256]{3,2,1,0:T(8,128)S(1)}, u32[]{:S(2)}, u32[]{:S(2)}) async-start(f32[4,4,32,256]{3,2,1,0:T(8,128)} %broadcast_in_dim.14), calls=%async_computation | async-start | bytes 1048576 | tf_op jit(solution)/shard_map/all_to_all | solution.py:383
  44.1 0.7 %slice.8 = f32[2,2,96]{2,1,0:T(2,128)S(1)} slice(f32[2,8,128]{2,1,0:T(8,128)} %bitcast.8), slice={[0:2], [0:2], [0:96]} | slice | bytes 3072 | tf_op jit(solution)/shard_map/slice | solution.py:390
  44.8 0.1 reshape.39
  44.8 8.2 %all-to-all-done = f32[4,4,32,256]{3,2,1,0:T(8,128)S(1)} async-done(((f32[4,4,32,256]{3,2,1,0:T(8,128)}), f32[4,4,32,256]{3,2,1,0:T(8,128)S(1)}, u32[]{:S(2)}, u32[]{:S(2)}) %all-to-all-start) | async-done | bytes 524320 | tf_op jit(solution)/shard_map/all_to_all | solution.py:383
  53.0 3.4 %collective-permute-start.3 = (f32[4,32,256]{2,1,0:T(8,128)S(1)}, f32[4,32,256]{2,1,0:T(8,128)S(1)}, u32[]{:S(2)}, u32[]{:S(2)}) collective-permute-start(f32[4,32,256]{2,1,0:T(8,128)S(1)} %reduce_sum.9), channel_id=1, source_target_pairs={{0,1},{1,0},{2,3},{3,2},{4,5},{5,4},{6,7},{7,6},{8,9},{9,8},{10,11... | collective-permute-start | bytes 393224 | tf_op jit(solution)/shard_map/ppermute | solution.py:386
  56.5 0.6 %copy.16 = f32[3,2,2,25]{3,2,1,0:T(2,128)} copy(f32[3,2,2,25]{3,0,1,2:T(4,128)S(1)} %slice_bitcast_fusion) | data formatting | bytes 2400
  57.1 0.4 collective-permute-done.3
  57.4 0.7 %maximum_select_fusion = f32[8,32,256]{2,1,0:T(8,128)} fusion(f32[4,32,256]{2,1,0:T(8,128)S(1)} %collective-permute-done.3, f32[4,32,256]{2,1,0:T(8,128)S(1)} %reduce_sum.9, pred[]{:T(512)S(6)} %eq.7), kind=kLoop, calls=%fused_computation | loop fusion | flops 196608 | bytes 524289 | tf_op jit(solution)/shard_map/jit(_where)/select_n | solution.py:387
  (7 shorter events, 0.1 us)
Async XLA Ops:
  2.2 0.7 %copy-start.3 = (s32[3,32]{1,0:T(4,128)S(1)}, s32[3,32]{1,0:T(4,128)}, u32[]{:S(2)}) copy-start(s32[3,32]{1,0:T(4,128)} %param.16) | copy-start | bytes 1156
  6.9 6.7 %copy-start.2 = (f32[32,25]{1,0:T(8,128)S(1)}, f32[32,25]{1,0:T(8,128)}, u32[]{:S(2)}) copy-start(f32[32,25]{1,0:T(8,128)} %param.18) | copy-start | bytes 9604
  6.9 10.4 %collective-permute-start = (f32[272,256]{1,0:T(8,128)}, f32[272,256]{1,0:T(8,128)S(1)}, u32[]{:S(2)}, u32[]{:S(2)}) collective-permute-start(f32[272,256]{1,0:T(8,128)} %get-tuple-element.9), channel_id=1, source_target_pairs={{0,8},{8,16},{16,24},{24,32},{32,40},{40,48},{48,56},{56,64},{64,7... | collective-permute-start | bytes 835592 | tf_op jit(solution)/shard_map/ppermute | solution.py:345
  11.7 12.7 %collective-permute-start.1 = (f32[272,256]{1,0:T(8,128)}, f32[272,256]{1,0:T(8,128)S(1)}, u32[]{:S(2)}, u32[]{:S(2)}) collective-permute-start(f32[272,256]{1,0:T(8,128)} %get-tuple-element.10), channel_id=1, source_target_pairs={{8,0},{16,8},{24,16},{32,24},{40,32},{48,40},{56,48},{64,56},{72,6... | collective-permute-start | bytes 835592 | tf_op jit(solution)/shard_map/ppermute | solution.py:346
  17.3 7.1 %copy-start = (f32[272,256]{1,0:T(8,128)}, f32[272,256]{1,0:T(8,128)S(1)}, u32[]{:S(2)}) copy-start(f32[272,256]{1,0:T(8,128)S(1)} %collective-permute-done.below) | copy-start | bytes 835588
  24.4 0.7 %copy-start.1 = (f32[272,256]{1,0:T(8,128)}, f32[272,256]{1,0:T(8,128)S(1)}, u32[]{:S(2)}) copy-start(f32[272,256]{1,0:T(8,128)S(1)} %collective-permute-done.1.above) | copy-start | bytes 835588
  33.2 4.9 %collective-permute-start.2 = (f32[4,32,256]{2,1,0:T(8,128)}, f32[4,32,256]{2,1,0:T(8,128)S(1)}, u32[]{:S(2)}, u32[]{:S(2)}) collective-permute-start(f32[4,32,256]{2,1,0:T(8,128)} %get-tuple-element.13), channel_id=1, source_target_pairs={{0,1},{1,0},{2,3},{3,2},{4,5},{5,4},{6,7},{7,6},{8,9},{9,8},{10,11... | collective-permute-start | bytes 393224 | tf_op jit(solution)/shard_map/ppermute | solution.py:381
  39.9 13.1 %all-to-all-start = ((f32[4,4,32,256]{3,2,1,0:T(8,128)}), f32[4,4,32,256]{3,2,1,0:T(8,128)S(1)}, u32[]{:S(2)}, u32[]{:S(2)}) async-start(f32[4,4,32,256]{3,2,1,0:T(8,128)} %broadcast_in_dim.14), calls=%async_computation | async-start | bytes 1048576 | tf_op jit(solution)/shard_map/all_to_all | solution.py:383
  53.0 4.4 %collective-permute-start.3 = (f32[4,32,256]{2,1,0:T(8,128)S(1)}, f32[4,32,256]{2,1,0:T(8,128)S(1)}, u32[]{:S(2)}, u32[]{:S(2)}) collective-permute-start(f32[4,32,256]{2,1,0:T(8,128)S(1)} %reduce_sum.9), channel_id=1, source_target_pairs={{0,1},{1,0},{2,3},{3,2},{4,5},{5,4},{6,7},{7,6},{8,9},{9,8},{10,11... | collective-permute-start | bytes 393224 | tf_op jit(solution)/shard_map/ppermute | solution.py:386

commit v2 on v1

v2 whole, which is shorter than its diff:
```python
import functools

import jax
import jax.numpy as jnp
from jax import lax
from jax.experimental import pallas as pl
from jax.experimental.pallas import tpu as pltpu
from jax.sharding import PartitionSpec as P

LANES = 128
FAR = float(1 << 20)
WINDOW = 16
VMEM_LIMIT = 20 << 20
EDGE_LIMIT = 62 << 20
TINY = 16
VMEM = pltpu.VMEM
F32 = jnp.float32


def dot(a, b, contract):
    return lax.dot_general(
        a, b, ((contract[:1], contract[1:]), ((), ())), preferred_element_type=F32
    )


def halves(a):
    high = a.astype(jnp.bfloat16)
    return high, (a - high.astype(F32)).astype(jnp.bfloat16)


def pick(a, onehot, contract):
    high, low = halves(a)
    return dot(high, onehot, contract) + dot(low, onehot, contract)


def edge_masks(shape):
    row = lax.broadcasted_iota(jnp.int32, shape, 0)
    col = lax.broadcasted_iota(jnp.int32, shape, 1)
    return row > 0, row < shape[0] - 1, col > 0, col < shape[1] - 1


def plane_weights(vel, masks):
    low_x, high_x, low_y, high_y = masks
    xp = jnp.where(high_x, vel, 0.0)
    xm = jnp.where(low_x, pltpu.roll(vel, 1, 0), 0.0)
    yp = jnp.where(high_y, vel, 0.0)
    ym = jnp.where(low_y, pltpu.roll(vel, 1, 1), 0.0)
    return xp, xm, yp, ym, 2.0 * vel + xm + ym


def plane_part(u, weights):
    xp, xm, yp, ym, centre = weights
    rows, cols = u.shape
    return (
        xp * pltpu.roll(u, rows - 1, 0) + xm * pltpu.roll(u, 1, 0)
        + yp * pltpu.roll(u, cols - 1, 1) + ym * pltpu.roll(u, 1, 1)
        - centre * u
    )


def pick_columns(cols, width):
    return (lax.broadcasted_iota(jnp.int32, (width, cols.shape[1]), 0) == cols).astype(jnp.bfloat16)


def pick_rows(rows, count):
    return (lax.broadcasted_iota(jnp.int32, (count, rows.shape[1]), 0) == rows).astype(F32)


def split_cells(cells, width_x, width_y):
    plane = lax.div(cells, width_x * width_y)
    row = lax.div(cells, width_y)
    return plane, row, row - plane * width_x, cells - row * width_y


def in_lanes(pieces, width, fill=0.0):
    parts = []
    for piece in pieces:
        parts.append(piece)
        if piece.shape[1] < width:
            parts.append(jnp.full((1, width - piece.shape[1]), fill, piece.dtype))
    used = width * len(pieces)
    parts.append(jnp.full((1, LANES - used), fill, pieces[0].dtype))
    return jnp.concatenate(parts, axis=1)


def live_lanes(rec_live, slots, capsules):
    slot = lax.div(lax.broadcasted_iota(jnp.int32, (1, LANES), 1), capsules)
    row = jnp.zeros((1, LANES), F32)
    for r in range(slots):
        row = jnp.where(slot == r, rec_live[r].astype(F32), row)
    return row


def cell_lanes(rec_cells):
    slots, capsules = rec_cells.shape
    return in_lanes([rec_cells[r : r + 1, :] for r in range(slots)], capsules, int(FAR))


def goal_lanes(target, s, n, capsules):
    return in_lanes([target[r, s, n : n + 1, :] for r in range(target.shape[0])], capsules)


def edge_kernel(
    rec_live, rec_cells, target, p0_h, adj_h, density_h, speed_h, admittance_h, mask_h,
    up, down, p0, adj, density, speed, admittance, mask, vel_s, pd_s, stack, sems,
):
    shots, depth, width_x, width_y = p0.shape
    slots, capsules = rec_cells.shape
    half = depth // 2
    last = depth - 1
    copies = []
    for side in range(2):
        some = pl.ds(side * half, half)
        pairs = [(h.at[some], v.at[some]) for h, v in (
            (density_h, density), (speed_h, speed), (admittance_h, admittance), (mask_h, mask))]
        pairs.insert(0, (p0_h.at[:, some], p0.at[:, some]))
        pairs.append((adj_h.at[:, pl.ds(side * last, 1)], adj.at[:, pl.ds(side, 1)]))
        copies.append([
            pltpu.make_async_copy(a, b, sems.at[side, k]) for k, (a, b) in enumerate(pairs)
        ])
    for copy in copies[0] + copies[1]:
        copy.start()
    masks = edge_masks((width_x, width_y))
    plane, _, row_x, col = split_cells(cell_lanes(rec_cells), width_x, width_y)
    live = live_lanes(rec_live, slots, capsules)
    columns = pick_columns(col, width_y)
    rows = pick_rows(row_x, width_x)
    for side in range(2):
        for copy in copies[side]:
            copy.wait()
        if side == 0:
            out, planes, lowest, inward = down, (0, 1, 2), 0, 1
        else:
            out, planes, lowest, inward = up, (last, last - 1, last - 2), half, -1
        near, far, third = planes
        span = range(lowest, lowest + half)
        weights, pres, damp = {}, {}, {}
        for z in span:
            vel_s[z] = 0.5 / density[z]
        for z in planes:
            spd = speed[z]
            pres[z] = 0.5 * density[z] * spd * spd
            damp[z] = 1.0 - admittance[z] * mask[z].astype(F32)
            weights[z] = plane_weights(vel_s[z], masks)
        for z in (near, far):
            pd_s[z] = pres[z] * damp[z]
        wall_low = min(near, far)
        base = side * 7 * width_x

        def put(k, value):
            stack[base + k * width_x : base + (k + 1) * width_x, :] = value

        for s in range(shots):
            first = {}
            for z in planes:
                here = p0[s, z]
                total = plane_part(here, weights[z])
                if z + 1 in span:
                    total += vel_s[z] * (p0[s, z + 1] - here)
                if z - 1 in span:
                    total -= vel_s[z - 1] * (here - p0[s, z - 1])
                first[z] = damp[z] * (here + pres[z] * total)
            out[s * width_x : (s + 1) * width_x, :] = p0[s, near]
            out[(2 + s) * width_x : (3 + s) * width_x, :] = first[near]
            out[(4 + s) * width_x : (5 + s) * width_x, :] = pd_s[near] * adj[s, side]
            q_far = p0[s, far] + first[far]
            q_third = p0[s, third] + first[third]
            beyond = vel_s[min(far, third)]
            total = plane_part(q_far, weights[far]) + beyond * (q_third - q_far)
            total -= vel_s[wall_low] * q_far
            put(s, pd_s[near] * vel_s[wall_low] * q_far)
            put(4 + s, damp[far] * first[far] + pd_s[far] * total)
        out[6 * width_x : 7 * width_x, :] = vel_s[near]
        out[7 * width_x : 8 * width_x, :] = pd_s[near]
        put(2, damp[near])
        put(3, pd_s[near] * vel_s[wall_low])
        put(6, pd_s[far] * vel_s[wall_low])
        found = pick(stack[base : base + 7 * width_x, :], columns, (1, 0))
        is_near = (plane == near).astype(F32)
        is_far = (plane == far).astype(F32)

        def got(k):
            return jnp.sum(found[k * width_x : (k + 1) * width_x, :] * rows, axis=0, keepdims=True)

        tiny = [is_near * got(s) + is_far * got(4 + s) for s in range(shots)]
        tiny += [
            is_near * got(2), is_far * got(6) - is_near * got(3), is_near,
            row_x.astype(F32), col.astype(F32), live,
        ]
        tiny += [live * goal_lanes(target, s, 1, capsules) for s in range(shots)]
        tiny.append(jnp.zeros((TINY - len(tiny), LANES), F32))
        start = 8 * width_x
        out[start : start + TINY, :] = jnp.zeros((TINY, width_y), F32)
        out[start : start + TINY, 0:LANES] = jnp.concatenate(tiny, axis=0)


def middle_kernel(
    rec_live, rec_cells, target, encoder, p0, adj, density, speed, admittance, mask,
    b1, b2, vel_s, pres_s, damp_s, pd_s, back_e, grad, rows_out, code_high, code_low,
    q_s, w_s,
):
    shots, depth, width_x, width_y = p0.shape
    slots, capsules = rec_cells.shape
    steps, channels = target.shape[2:]
    masks = edge_masks((width_x, width_y))
    last = depth - 1
    edges = (0, 1, last - 1, last)
    for z in range(depth):
        dens = density[z]
        spd = speed[z]
        vel = 0.5 / dens
        pres = 0.5 * dens * spd * spd
        damp = 1.0 - admittance[z] * mask[z].astype(F32)
        vel_s[z] = vel
        pres_s[z] = pres
        damp_s[z] = damp
        pd_s[z] = pres * damp
        w = plane_weights(vel, masks)
        for s in range(shots):
            here = p0[s, z]
            total = plane_part(here, w)
            if z < last:
                total += vel * (p0[s, z + 1] - here)
            if z > 0:
                total -= vel_s[z - 1] * (here - p0[s, z - 1])
            value = here + pres * total
            b1[s, z] = value
            q_s[s, z] = here + damp * value
            w_s[s, z] = pd_s[z] * adj[s, z]
    for z in range(depth):
        vel = vel_s[z]
        w = plane_weights(vel, masks)
        sums = jnp.zeros((width_x, width_y), F32)
        for s in range(shots):
            here, weighted = q_s[s, z], w_s[s, z]
            total = plane_part(here, w)
            back = plane_part(weighted, w)
            if z < last:
                total += vel * (q_s[s, z + 1] - here)
                back += vel * (w_s[s, z + 1] - weighted)
            if z > 0:
                total -= vel_s[z - 1] * (here - q_s[s, z - 1])
                back -= vel_s[z - 1] * (weighted - w_s[s, z - 1])
            value = damp_s[z] * b1[s, z] + pres_s[z] * total
            b2[s, z] = value
            back += damp_s[z] * adj[s, z]
            if z in edges:
                back_e[s, edges.index(z)] = back
            else:
                sums += value * adj[s, z] + b1[s, z] * back
        grad[z] = -(mask[z].astype(F32) * sums)
    lane = lax.broadcasted_iota(jnp.int32, (LANES, LANES), 1)
    line = lax.broadcasted_iota(jnp.int32, (LANES, LANES), 0)
    same = (lax.div(lane, capsules) == lax.div(line, capsules)) & (line < slots * capsules)
    code = jnp.concatenate([encoder[...], jnp.zeros((capsules, capsules - channels), F32)], axis=1)
    code = jnp.concatenate([code] * (LANES // capsules), axis=1)
    code = jnp.where(same, jnp.concatenate([code] * (LANES // capsules), axis=0), 0.0)
    square = lax.dot_general(
        code, code, (((1,), (1,)), ((), ())),
        precision=lax.Precision.HIGHEST, preferred_element_type=F32,
    )
    both = jnp.concatenate([code, square], axis=1)
    code_high[...], code_low[...] = halves(both)
    live = live_lanes(rec_live, slots, capsules)
    goal = [live * goal_lanes(target, s, n, capsules) for n in range(steps) for s in range(shots)]
    goal = jnp.concatenate(goal + [jnp.zeros((8 - len(goal), LANES), F32)], axis=0)
    rows_out[0:8, :] = lax.dot_general(
        goal, code, (((1,), (1,)), ((), ())),
        precision=lax.Precision.HIGHEST, preferred_element_type=F32,
    )
    rows_out[8:16, :] = jnp.concatenate(
        [cell_lanes(rec_cells).astype(F32), live, jnp.zeros((6, LANES), F32)], axis=0
    )


def window_part(u, vel, masks):
    low_x, high_x, low_y, high_y = masks
    rows, cols = u.shape
    flow_x = vel * (jnp.where(high_x, pltpu.roll(u, rows - 1, 0), 0.0) - u)
    flow_y = vel * (jnp.where(high_y, pltpu.roll(u, cols - 1, 1), 0.0) - u)
    fall_x = flow_x - jnp.where(low_x, pltpu.roll(flow_x, 1, 0), 0.0)
    return fall_x + flow_y - jnp.where(low_y, pltpu.roll(flow_y, 1, 1), 0.0)


def last_kernel(
    capsules, core, corners, below, above, p0, adj, mask, vel_s, pres_s, damp_s, pd_s, back_e,
    rows_in, code_high, code_low, b1_in, b2_in, grad_in,
    keep, send, coded, b1, b2, grad,
    halo_s, stack, spread,
):
    shots, depth, width_x, width_y = p0.shape
    slots = corners.shape[0]
    masks = edge_masks((width_x, width_y))
    last = depth - 1
    edges = (0, 1, last - 1, last)
    sides = ((below, 0, 1), (above, last, last - 1))
    blank = jnp.zeros((1, LANES), F32)

    def halo(ref, k):
        return ref[k * width_x : (k + 1) * width_x, :]

    def rows_of(array, k, count):
        return array[k * count : (k + 1) * count, :]

    for side, (ref, edge, inner) in enumerate(sides):
        vel_h, pd_h = halo(ref, 6), halo(ref, 7)
        vel_b = vel_h if side == 0 else vel_s[last]
        vel_in = vel_s[min(edge, inner)]
        w_h = plane_weights(vel_h, masks)
        w_e = plane_weights(vel_s[edge], masks)
        for s in range(shots):
            here, out = p0[s, edge], halo(ref, s)
            step = vel_b * (here - out)
            p1_h = halo(ref, 2 + s) + pd_h * step
            q_h = out + p1_h
            fixed = b1[s, edge] - pres_s[edge] * step
            change = -(pd_s[edge] * step)
            step2 = vel_b * (here + damp_s[edge] * fixed - q_h)
            base = side * 6
            halo_s[(base + s) * width_x : (base + s + 1) * width_x, :] = p1_h
            halo_s[(base + 2 + s) * width_x : (base + 3 + s) * width_x, :] = q_h
            halo_s[(base + 4 + s) * width_x : (base + 5 + s) * width_x, :] = pd_h * (
                plane_part(q_h, w_h) + step2
            )
            b1[s, edge] = fixed
            total = plane_part(change, w_e) - vel_in * change - step2
            b2[s, edge] = b2[s, edge] + change + pres_s[edge] * total
            b2[s, inner] = b2[s, inner] + pres_s[inner] * (vel_in * change)

    places = []
    for r in range(slots):
        z0 = jnp.clip(lax.div(corners[r], width_x * width_y), 0, depth - 2)
        x0 = lax.rem(lax.div(corners[r], width_y), width_x)
        start = jnp.minimum(lax.div(jnp.maximum(x0 - 1, 0), 8) * 8, width_x - WINDOW)
        places.append((z0, pl.multiple_of(start, 8)))
    _, row, _, col = split_cells(rows_in[8:9, :].astype(jnp.int32), width_x, width_y)
    live = rows_in[9:10, :]
    columns = pick_columns(col, width_y)
    slot_of = lax.div(lax.broadcasted_iota(jnp.int32, (1, LANES), 1), capsules)
    line = lax.broadcasted_iota(jnp.int32, (WINDOW, LANES), 0)
    found_rows = {}
    for r, (z0, start) in enumerate(places):
        own = jnp.where(slot_of == r, row, -1)
        for dz in range(2):
            first_row = (z0 + dz) * width_x + start
            found_rows[r, dz] = (line + first_row == own).astype(F32)
    index = {}
    for n, field in enumerate((b1, b2)):
        for r, (z0, start) in enumerate(places):
            for dz in range(2):
                damp = damp_s[z0 + dz, pl.ds(start, WINDOW), :]
                for s in range(shots):
                    k = index[n, r, dz, s] = len(index)
                    stack[k * WINDOW : (k + 1) * WINDOW, :] = (
                        damp * field[s, z0 + dz, pl.ds(start, WINDOW), :]
                    )
    found = pick(stack[...], columns, (1, 0))
    lines, lives, goals = [], [live] * 4, [blank] * 4
    for n in range(2):
        for s in range(shots):
            total = jnp.zeros((WINDOW, LANES), F32)
            for key, picked in found_rows.items():
                total += picked * rows_of(found, index[(n, *key, s)], WINDOW)
            lines.append(jnp.sum(total, axis=0, keepdims=True))
    columns_h, rows_h = [], []
    for side, (ref, _, _) in enumerate(sides):
        tiny = ref[8 * width_x : 8 * width_x + TINY, 0:LANES]
        near = tiny[4:5, :]
        picked = pick_rows(tiny[5:6, :].astype(jnp.int32), width_x).astype(F32)
        columns_h.append(pick_columns(tiny[6:7, :].astype(jnp.int32), width_y))
        rows_h.append(picked * near)
        found = pick(
            halo_s[side * 6 * width_x : (side + 1) * 6 * width_x, :], columns_h[side], (1, 0)
        )
        for s in range(shots):
            total = picked * (
                tiny[2:3, :] * rows_of(found, s, width_x)
                + tiny[3:4, :] * rows_of(found, 2 + s, width_x)
                + near * rows_of(found, 4 + s, width_x)
            )
            lines.append(tiny[s : s + 1, :] + jnp.sum(total, axis=0, keepdims=True))
            lives.append(tiny[7:8, :])
            goals.append(tiny[8 + s : 9 + s, :])
    goal_high, goal_low = halves(jnp.concatenate(goals, axis=0))
    high, low = code_high[:, 0:LANES], code_low[:, 0:LANES]
    known = rows_in[0:8, :] + (
        dot(goal_high, high, (1, 1)) + dot(goal_low, high, (1, 1)) + dot(goal_high, low, (1, 1))
    )
    got_high, got_low = halves(jnp.concatenate(lines, axis=0))
    both = (
        dot(got_high, code_high[...], (1, 0)) + dot(got_low, code_high[...], (1, 0))
        + dot(got_high, code_low[...], (1, 0))
    )
    lives = jnp.concatenate(lives, axis=0)
    coded[...] = both[:, 0:LANES] * lives
    source = both[:, LANES:] * lives - known

    parts = [None] * len(index)
    for (n, r, dz, s), k in index.items():
        line_of = n * shots + s
        parts[k] = found_rows[r, dz] * source[line_of : line_of + 1, :]
    spread[...] = pick(jnp.concatenate(parts, axis=0), columns, (1, 1))
    for side, (ref, edge, inner) in enumerate(sides):
        lines = [
            rows_h[side] * source[4 + 2 * side + s : 5 + 2 * side + s, :] for s in range(shots)
        ]
        placed = pick(jnp.concatenate(lines, axis=0), columns_h[side], (1, 1))
        vel_b = halo(ref, 6) if side == 0 else vel_s[last]
        sums = jnp.zeros((width_x, width_y), F32)
        sums_in = jnp.zeros((width_x, width_y), F32)
        for s in range(shots):
            w_h = halo(ref, 4 + s) + halo(ref, 7) * rows_of(placed, s, width_x)
            start = adj[s, edge]
            back = back_e[s, edges.index(edge)] - vel_b * (pd_s[edge] * start - w_h)
            sums += b2[s, edge] * start + b1[s, edge] * back
            sums_in += b2[s, inner] * adj[s, inner] + b1[s, inner] * back_e[s, edges.index(inner)]
        grad[edge] = -(mask[edge].astype(F32) * sums)
        grad[inner] = -(mask[inner].astype(F32) * sums_in)

    near_masks = edge_masks((WINDOW, width_y))
    for r, (z0, start) in enumerate(places):
        window = pl.ds(start, WINDOW)
        lower, upper = jnp.maximum(z0 - 1, 0), jnp.minimum(z0 + 2, last)
        vel_low = jnp.where(
            z0 > 0, vel_s[lower, window, :], below[pl.ds(6 * width_x + start, WINDOW), :]
        )
        vel = [vel_s[z0 + dz, window, :] for dz in range(2)]
        sums = [jnp.zeros((WINDOW, width_y), F32) for _ in range(4)]
        for s in range(shots):
            now, before = [
                [rows_of(spread, index[n, r, dz, s], WINDOW) for dz in range(2)] for n in (1, 0)
            ]
            w = [pd_s[z0 + dz, window, :] * now[dz] for dz in range(2)]
            between = vel[0] * (w[1] - w[0])
            outer = [vel_low * w[0], vel[1] * w[1]]
            for dz in range(2):
                total = window_part(w[dz], vel[dz], near_masks) - outer[dz]
                total += between if dz == 0 else -between
                total += damp_s[z0 + dz, window, :] * now[dz] + before[dz]
                sums[1 + dz] += (
                    b2[s, z0 + dz, window, :] * now[dz] + b1[s, z0 + dz, window, :] * total
                )
            sums[0] += b1[s, lower, window, :] * outer[0]
            sums[3] += b1[s, upper, window, :] * outer[1]
        inside = (jnp.where(z0 > 0, 1.0, 0.0), 1.0, 1.0, jnp.where(z0 + 2 < depth, 1.0, 0.0))
        for z, total, factor in zip((lower, z0, z0 + 1, upper), sums, inside):
            wall = mask[z, window, :].astype(F32)
            grad[z, window, :] = grad[z, window, :] - factor * (wall * total)
    half = depth // 2
    mine = core[0] * half
    for z in range(half):
        keep[z] = grad[mine + z]
        send[z] = grad[half - mine + z]


def body(
    pressure_init, adjoint_init, density, speed, admittance, bound_mask,
    rec_cells, rec_live, encoder, target,
):
    shots, depth, width_x, width_y = pressure_init.shape
    slots, capsules = rec_cells.shape
    steps, channels = target.shape[2:]
    slabs, peers = lax.axis_size("slab"), lax.axis_size("shot")
    field = (shots, depth, width_x, width_y)
    slab = (depth, width_x, width_y)
    half = (depth // 2, width_x, width_y)
    message = (8 * width_x + TINY, width_y)

    def ins(count, scalars=0, far=0):
        kinds = [pltpu.SMEM] * scalars + [VMEM] * (count - scalars - far) + [pltpu.HBM] * far
        return [pl.BlockSpec(memory_space=kind) for kind in kinds]

    def outs(*shapes):
        return [
            shape if isinstance(shape, jax.ShapeDtypeStruct) else jax.ShapeDtypeStruct(shape, F32)
            for shape in shapes
        ]

    params = pltpu.CompilerParams(vmem_limit_bytes=VMEM_LIMIT)
    up, down = pl.pallas_call(
        edge_kernel,
        in_specs=ins(9, 1, 6),
        out_specs=ins(2),
        out_shape=outs(message, message),
        scratch_shapes=[
            VMEM(field, F32), VMEM((shots, 2, width_x, width_y), F32),
            VMEM(slab, F32), VMEM(slab, F32), VMEM(slab, F32), VMEM(slab, jnp.int32),
            VMEM(slab, F32), VMEM(slab, F32), VMEM((14 * width_x, width_y), F32),
            pltpu.SemaphoreType.DMA((2, 6)),
        ],
        compiler_params=pltpu.CompilerParams(vmem_limit_bytes=EDGE_LIMIT),
        name="edge",
    )(
        rec_live, rec_cells, target, pressure_init, adjoint_init, density, speed, admittance,
        bound_mask,
    )

    below = lax.ppermute(up, "slab", [(i, i + 1) for i in range(slabs - 1)])
    above = lax.ppermute(down, "slab", [(i + 1, i) for i in range(slabs - 1)])

    table = jax.ShapeDtypeStruct((LANES, 2 * LANES), jnp.bfloat16)
    b1, b2, vel, pres, damp, pd, back, grad, rows, high, low = pl.pallas_call(
        middle_kernel,
        in_specs=ins(10, 1),
        out_specs=ins(11),
        out_shape=outs(
            field, field, slab, slab, slab, slab, (shots, 4, width_x, width_y), slab,
            (16, LANES), table, table,
        ),
        scratch_shapes=[VMEM(field, F32), VMEM(field, F32)],
        compiler_params=params,
        cost_estimate=pl.CostEstimate(flops=20_000_000, bytes_accessed=6_000_000, transcendentals=0),
        name="middle",
    )(
        rec_live, rec_cells, target, encoder, pressure_init, adjoint_init, density, speed,
        admittance, bound_mask,
    )

    core = lax.rem(lax.axis_index("shot"), 2)
    corners = jnp.min(rec_cells, axis=1)
    windows = steps * slots * 2 * shots * WINDOW
    keep, send, coded, _, _, _ = pl.pallas_call(
        functools.partial(last_kernel, capsules),
        in_specs=ins(18, 2),
        out_specs=ins(6),
        out_shape=outs(half, half, (8, LANES), field, field, slab),
        scratch_shapes=[
            VMEM((12 * width_x, width_y), F32), VMEM((windows, width_y), F32),
            VMEM((windows, width_y), F32),
        ],
        input_output_aliases={15: 3, 16: 4, 17: 5},
        compiler_params=params,
        name="last",
    )(
        core[None], corners, below, above, pressure_init, adjoint_init, bound_mask, vel, pres,
        damp, pd, back, rows, high, low, b1, b2, grad,
    )

    pairs = [(i, i ^ 1) for i in range(peers)]
    groups = [list(range(c, peers, 2)) for c in range(2)]
    total = keep + lax.ppermute(send, "shot", pairs)
    copies = jnp.broadcast_to(total, (peers // 2, *half))
    total = lax.all_to_all(
        copies, "shot", split_axis=0, concat_axis=0, tiled=True, axis_index_groups=groups
    ).sum(axis=0)
    other = lax.ppermute(total, "shot", pairs)
    gradient = jnp.where(
        core == 0, jnp.concatenate([total, other], 0), jnp.concatenate([other, total], 0)
    )
    signals = coded[: steps * shots, : slots * capsules]
    signals = signals.reshape(steps, shots, slots, capsules)[..., :channels]
    return jnp.transpose(signals, (2, 1, 0, 3)), gradient


def solution(mesh):
    placed = (
        P("shot", "slab", None, None), P("shot", "slab", None, None),
        P("slab", None, None), P("slab", None, None), P("slab", None, None), P("slab", None, None),
        P("slab", None), P("slab"), P(), P("slab", "shot", None, None),
    )
    return jax.shard_map(
        body, mesh=mesh, in_specs=placed,
        out_specs=(P("slab", "shot", None, None), P("slab", None, None)),
        check_vma=False,
    )
```

time: 58.6 us -> 47.9 us (0.82)
  Pallas kernels: 11.5 us -> 7.77 us
  waiting for transfers between devices: 19.5 us -> 16.4 us
  other arithmetic: 3.82 us -> 0.9 us
  local copies, waits for them, and re-layouts: 4.57 us -> 3.67 us
    pallas_call x2 -> x3, Pallas kernels: 11.5 us -> 7.77 us  [the longest x1 3.67 us: body(): pl.pallas_call(edge_kernel, in_specs=ins(9, 1, 6), out_specs=ins(2), out_...]
    ppermute x1, waiting for transfers between devices: 2.81 us -> 0.01 us  [body(): below = lax.ppermute(up, 'slab', [(i, i + 1) for i in range(slabs - 1)])]
    add x1, other arithmetic: 0.92 us -> 0.02 us  [body(): total = keep + lax.ppermute(send, 'shot', pairs)]
    unnamed x10 -> x21, local copies, waits for them, and re-layouts: 1.84 us -> 2.73 us
    transpose x2 -> x0, other arithmetic: 0.86 us -> none  [the longest x1 0.76 us: body(): goal = jnp.transpose(target * live[:, :, None, None], (2, 1, 0, 3))]
    ppermute x1, waiting for transfers between devices: 7.05 us -> 6.27 us  [body(): above = lax.ppermute(down, 'slab', [(i + 1, i) for i in range(slabs - 1)])]
    all_to_all x1, waiting for transfers between devices: 8.15 us -> 8.85 us  [body(): lax.all_to_all(copies, 'shot', split_axis=0, concat_axis=0, tiled=True, a...]
    slice x1, local copies, waits for them, and re-layouts: 0.7 us -> 0.01 us  [body(): signals = coded[:steps * shots, :slots * capsules]]
  transfers between devices with their start and end apart: 5 -> 5, of which waited for: 5 -> 4; matrix products, arithmetic and copies ran while one was open for 4% -> 2% of each run, Pallas kernels for 0% -> 5%
where the time goes in v2:
time: 47.9 us; the launch traced here: 47.5 us
  starting transfers between devices  17.9 us (37%)
  waiting for transfers between devices  16.4 us (34%)
  Pallas kernels  7.77 us (16%)
  local copies, waits for them, and re-layouts  3.67 us (8%)
  other arithmetic  0.9 us (2%)
  between operations  0.83 us (2%)
    all_to_all x1, waiting for transfers between devices, body(): lax.all_to_all(copies, 'shot', split_axis=0, concat_axis=0, tiled=True, a...  8.85 us
    ppermute x1, waiting for transfers between devices, body(): above = lax.ppermute(down, 'slab', [(i + 1, i) for i in range(slabs - 1)])  6.27 us
    ppermute x1, starting transfers between devices, body(): below = lax.ppermute(up, 'slab', [(i, i + 1) for i in range(slabs - 1)])  4.67 us
    all_to_all x1, starting transfers between devices, body(): lax.all_to_all(copies, 'shot', split_axis=0, concat_axis=0, tiled=True, a...  4.18 us
    ppermute x1, starting transfers between devices, body(): total = keep + lax.ppermute(send, 'shot', pairs)  3.72 us
    pallas_call x1, Pallas kernels, body(): pl.pallas_call(edge_kernel, in_specs=ins(9, 1, 6), out_specs=ins(2), out_...  3.67 us
    ppermute x1, starting transfers between devices, body(): other = lax.ppermute(total, 'shot', pairs)  3.41 us
    unnamed x21, local copies, waits for them, and re-layouts  2.73 us
  transfers between devices with their start and end apart: 5, of which 4 were waited for; matrix products, arithmetic and copies ran while one was open for 2% of the time, Pallas kernels for 5%

profile of v2, /device:TPU:103, one launch (start us, length us, event | category | flops | bytes accessed | tf_op | source)
XLA Modules:
  0.0 47.5 jit_solution(16982971737600711532)
XLA Ops:
  0.6 0.0 copy-start
  0.6 0.0 copy-start.1
  0.7 0.0 copy-start.3
  0.7 0.0 copy-start.4
  0.7 0.0 copy-start.2
  0.7 0.0 copy-start.8
  0.7 3.7 %edge.1 = (f32[272,256]{1,0:T(8,128)}, f32[272,256]{1,0:T(8,128)}) custom-call(s32[3]{0:T(128)} %rec_live.3, s32[3,32]{1,0:T(4,128)} %rec_cells.3, f32[3,2,2,25]{3,2,1,0:T(2,128)} %target.3, f32[2,8,32,256]{3,2,1,0:T(8,128)} %p0.3, f32[2,8,32,256]{3,2,1,0:T(8,128)} %adj.3, f32[8,32,256]{2,1,0:T(8,128)} %density.1, f32[8,32,256]{2,1,0:T(8,128)} %speed.1, ...), custom_call_target="tpu_custom_call" | custom-call | tf_op jit(solution)/shard_map/edge/pallas_call | solution.py:480
  4.4 4.7 %collective-permute-start = (f32[272,256]{1,0:T(8,128)}, f32[272,256]{1,0:T(8,128)S(1)}, u32[]{:S(2)}, u32[]{:S(2)}) collective-permute-start(f32[272,256]{1,0:T(8,128)} %get-tuple-element.18), channel_id=1, source_target_pairs={{0,8},{8,16},{16,24},{24,32},{32,40},{40,48},{48,56},{56,64},{64,7... | collective-permute-start | bytes 835592 | tf_op jit(solution)/shard_map/ppermute | solution.py:498
  9.0 1.9 %collective-permute-start.1 = (f32[272,256]{1,0:T(8,128)}, f32[272,256]{1,0:T(8,128)S(1)}, u32[]{:S(2)}, u32[]{:S(2)}) collective-permute-start(f32[272,256]{1,0:T(8,128)} %get-tuple-element.19), channel_id=1, source_target_pairs={{8,0},{16,8},{24,16},{32,24},{40,32},{48,40},{56,48},{64,56},{72,6... | collective-permute-start | bytes 835592 | tf_op jit(solution)/shard_map/ppermute | solution.py:499
  11.0 0.0 copy-start.6
  11.0 0.0 copy-start.7
  11.0 0.7 %copy-done.7 = s32[3,32]{1,0:T(4,128)S(1)} copy-done((s32[3,32]{1,0:T(4,128)S(1)}, s32[3,32]{1,0:T(4,128)}, u32[]{:S(2)}) %copy-start.7) | copy-done | bytes 408
  11.7 0.0 copy-start.9
  11.7 0.1 reduce_min.9.corners
  11.8 0.0 copy-done
  11.8 0.0 copy-done.1
  11.8 0.0 copy-done.3
  11.8 0.0 copy-done.4
  11.8 0.0 copy-done.2
  11.8 0.0 copy-done.8
  11.9 0.0 copy-done.6
  11.9 0.5 copy-done.9
  12.3 0.0 copy-start.5
  12.3 0.9 %copy-done.5 = f32[8,32,256]{2,1,0:T(8,128)S(1)} copy-done((f32[8,32,256]{2,1,0:T(8,128)S(1)}, f32[8,32,256]{2,1,0:T(8,128)}, u32[]{:S(2)}) %copy-start.5) | copy-done | bytes 262168
  13.3 2.2 %middle.1 = (f32[2,8,32,256]{3,2,1,0:T(8,128)S(1)}, f32[2,8,32,256]{3,2,1,0:T(8,128)S(1)}, f32[8,32,256]{2,1,0:T(8,128)S(1)}, f32[8,32,256]{2,1,0:T(8,128)S(1)},...) custom-call(s32[3]{0:T(128)S(1)} %copy-done.9, ...), custom_call_target="tpu_custom_call" | custom-call | flops 20000000 | bytes 6000000 | tf_op jit(solution)/shard_map/middle/pallas_call | solution.py:502
  15.5 0.0 collective-permute-done.below
  15.5 6.3 %collective-permute-done.1.above = f32[272,256]{1,0:T(8,128)S(1)} collective-permute-done((f32[272,256]{1,0:T(8,128)}, f32[272,256]{1,0:T(8,128)S(1)}, u32[]{:S(2)}, u32[]{:S(2)}) %collective-permute-start.1) | collective-permute-done | bytes 278560 | tf_op jit(solution)/shard_map/ppermute | solution.py:499
  21.7 1.9 %last.1 = (f32[4,32,256]{2,1,0:T(8,128)S(1)}, f32[4,32,256]{2,1,0:T(8,128)S(1)}, f32[8,128]{1,0:T(8,128)S(1)}, f32[2,8,32,256]{3,2,1,0:T(8,128)S(1)}, f32[2,8,32...) custom-call(s32[1]{0:T(128)} %bitcast.core, ...), custom_call_target="tpu_custom_call", output_to_operand_aliasing={{3}: (15, {}), {4}: (16, {}), {5}: (17, {})} | custom-call | tf_op jit(solution)/shard_map/last/pallas_call | solution.py:522
  23.7 3.7 %collective-permute-start.2 = (f32[4,32,256]{2,1,0:T(8,128)S(1)}, f32[4,32,256]{2,1,0:T(8,128)S(1)}, u32[]{:S(2)}, u32[]{:S(2)}) collective-permute-start(f32[4,32,256]{2,1,0:T(8,128)S(1)} %get-tuple-element.33), channel_id=1, source_target_pairs={{0,1},{1,0},{2,3},{3,2},{4,5},{5,4},{6,7},{7,6},{8,9},{9,8},{10,11... | collective-permute-start | bytes 393224 | tf_op jit(solution)/shard_map/ppermute | solution.py:541
  27.4 1.0 %collective-permute-done.2 = f32[4,32,256]{2,1,0:T(8,128)S(1)} collective-permute-done((f32[4,32,256]{2,1,0:T(8,128)S(1)}, f32[4,32,256]{2,1,0:T(8,128)S(1)}, u32[]{:S(2)}, u32[]{:S(2)}) %collective-permute-start.2) | collective-permute-done | bytes 131104 | tf_op jit(solution)/shard_map/ppermute | solution.py:541
  28.4 0.8 %broadcast_in_dim.7 = f32[4,4,32,256]{3,2,1,0:T(8,128)} broadcast(f32[4,32,256]{2,1,0:T(8,128)S(1)} %add.3), dimensions={1,2,3} | broadcast | bytes 655360 | tf_op jit(solution)/shard_map/broadcast_in_dim | solution.py:542
  29.2 4.2 %all-to-all-start = ((f32[4,4,32,256]{3,2,1,0:T(8,128)}), f32[4,4,32,256]{3,2,1,0:T(8,128)S(1)}, u32[]{:S(2)}, u32[]{:S(2)}) async-start(f32[4,4,32,256]{3,2,1,0:T(8,128)} %broadcast_in_dim.7), calls=%async_computation | async-start | bytes 1048576 | tf_op jit(solution)/shard_map/all_to_all | solution.py:543
  33.4 0.1 reshape.7
  33.5 8.8 %all-to-all-done = f32[4,4,32,256]{3,2,1,0:T(8,128)S(1)} async-done(((f32[4,4,32,256]{3,2,1,0:T(8,128)}), f32[4,4,32,256]{3,2,1,0:T(8,128)S(1)}, u32[]{:S(2)}, u32[]{:S(2)}) %all-to-all-start) | async-done | bytes 524320 | tf_op jit(solution)/shard_map/all_to_all | solution.py:543
  42.4 3.4 %collective-permute-start.3 = (f32[4,32,256]{2,1,0:T(8,128)S(1)}, f32[4,32,256]{2,1,0:T(8,128)S(1)}, u32[]{:S(2)}, u32[]{:S(2)}) collective-permute-start(f32[4,32,256]{2,1,0:T(8,128)S(1)} %reduce_sum.9), channel_id=1, source_target_pairs={{0,1},{1,0},{2,3},{3,2},{4,5},{5,4},{6,7},{7,6},{8,9},{9,8},{10,11... | collective-permute-start | bytes 393224 | tf_op jit(solution)/shard_map/ppermute | solution.py:546
  45.8 0.6 %copy.17 = f32[3,2,2,25]{3,2,1,0:T(2,128)} copy(f32[3,2,2,25]{3,0,1,2:T(4,128)S(1)} %slice_bitcast_fusion) | data formatting | bytes 2400
  46.4 0.4 collective-permute-done.3
  46.8 0.7 %maximum_select_fusion = f32[8,32,256]{2,1,0:T(8,128)} fusion(f32[4,32,256]{2,1,0:T(8,128)S(1)} %collective-permute-done.3, f32[4,32,256]{2,1,0:T(8,128)S(1)} %reduce_sum.9, pred[]{:T(512)S(6)} %eq.3), kind=kLoop, calls=%fused_computation | loop fusion | flops 196608 | bytes 524289 | tf_op jit(solution)/shard_map/jit(_where)/select_n | solution.py:547
  (4 shorter events, 0.1 us)
Async XLA Ops:
  0.6 11.2 %copy-start = (f32[2,8,32,256]{3,2,1,0:T(8,128)S(1)}, f32[2,8,32,256]{3,2,1,0:T(8,128)}, u32[]{:S(2)}) copy-start(f32[2,8,32,256]{3,2,1,0:T(8,128)} %p0.3) | copy-start | bytes 1572868
  0.6 11.2 %copy-start.1 = (f32[2,8,32,256]{3,2,1,0:T(8,128)S(1)}, f32[2,8,32,256]{3,2,1,0:T(8,128)}, u32[]{:S(2)}) copy-start(f32[2,8,32,256]{3,2,1,0:T(8,128)} %adj.3) | copy-start | bytes 1572868
  0.7 11.2 %copy-start.3 = (f32[8,32,256]{2,1,0:T(8,128)S(1)}, f32[8,32,256]{2,1,0:T(8,128)}, u32[]{:S(2)}) copy-start(f32[8,32,256]{2,1,0:T(8,128)} %density.1) | copy-start | bytes 786436
  0.7 11.2 %copy-start.4 = (f32[8,32,256]{2,1,0:T(8,128)S(1)}, f32[8,32,256]{2,1,0:T(8,128)}, u32[]{:S(2)}) copy-start(f32[8,32,256]{2,1,0:T(8,128)} %speed.1) | copy-start | bytes 786436
  0.7 11.2 %copy-start.2 = (s32[8,32,256]{2,1,0:T(8,128)S(1)}, s32[8,32,256]{2,1,0:T(8,128)}, u32[]{:S(2)}) copy-start(s32[8,32,256]{2,1,0:T(8,128)} %mask.3) | copy-start | bytes 786436
  0.7 11.2 %copy-start.8 = (f32[32,25]{1,0:T(8,128)S(1)}, f32[32,25]{1,0:T(8,128)}, u32[]{:S(2)}) copy-start(f32[32,25]{1,0:T(8,128)} %encoder.1) | copy-start | bytes 9604
  4.4 11.1 %collective-permute-start = (f32[272,256]{1,0:T(8,128)}, f32[272,256]{1,0:T(8,128)S(1)}, u32[]{:S(2)}, u32[]{:S(2)}) collective-permute-start(f32[272,256]{1,0:T(8,128)} %get-tuple-element.18), channel_id=1, source_target_pairs={{0,8},{8,16},{16,24},{24,32},{32,40},{40,48},{48,56},{56,64},{64,7... | collective-permute-start | bytes 835592 | tf_op jit(solution)/shard_map/ppermute | solution.py:498
  9.0 12.7 %collective-permute-start.1 = (f32[272,256]{1,0:T(8,128)}, f32[272,256]{1,0:T(8,128)S(1)}, u32[]{:S(2)}, u32[]{:S(2)}) collective-permute-start(f32[272,256]{1,0:T(8,128)} %get-tuple-element.19), channel_id=1, source_target_pairs={{8,0},{16,8},{24,16},{32,24},{40,32},{48,40},{56,48},{64,56},{72,6... | collective-permute-start | bytes 835592 | tf_op jit(solution)/shard_map/ppermute | solution.py:499
  11.0 0.9 %copy-start.6 = (f32[3,2,2,25]{3,2,1,0:T(2,128)S(1)}, f32[3,2,2,25]{3,2,1,0:T(2,128)}, u32[]{:S(2)}) copy-start(f32[3,2,2,25]{3,2,1,0:T(2,128)} %target.3) | copy-start | bytes 3604
  11.0 0.7 %copy-start.7 = (s32[3,32]{1,0:T(4,128)S(1)}, s32[3,32]{1,0:T(4,128)}, u32[]{:S(2)}) copy-start(s32[3,32]{1,0:T(4,128)} %rec_cells.3) | copy-start | bytes 1156
  11.7 0.7 %copy-start.9 = (s32[3]{0:T(128)S(1)}, s32[3]{0:T(128)}, u32[]{:S(2)}) copy-start(s32[3]{0:T(128)} %rec_live.3) | copy-start | bytes 40
  12.3 0.9 %copy-start.5 = (f32[8,32,256]{2,1,0:T(8,128)S(1)}, f32[8,32,256]{2,1,0:T(8,128)}, u32[]{:S(2)}) copy-start(f32[8,32,256]{2,1,0:T(8,128)} %admittance.1) | copy-start | bytes 786436
  23.7 4.7 %collective-permute-start.2 = (f32[4,32,256]{2,1,0:T(8,128)S(1)}, f32[4,32,256]{2,1,0:T(8,128)S(1)}, u32[]{:S(2)}, u32[]{:S(2)}) collective-permute-start(f32[4,32,256]{2,1,0:T(8,128)S(1)} %get-tuple-element.33), channel_id=1, source_target_pairs={{0,1},{1,0},{2,3},{3,2},{4,5},{5,4},{6,7},{7,6},{8,9},{9,8},{10,11... | collective-permute-start | bytes 393224 | tf_op jit(solution)/shard_map/ppermute | solution.py:541
  29.2 13.1 %all-to-all-start = ((f32[4,4,32,256]{3,2,1,0:T(8,128)}), f32[4,4,32,256]{3,2,1,0:T(8,128)S(1)}, u32[]{:S(2)}, u32[]{:S(2)}) async-start(f32[4,4,32,256]{3,2,1,0:T(8,128)} %broadcast_in_dim.7), calls=%async_computation | async-start | bytes 1048576 | tf_op jit(solution)/shard_map/all_to_all | solution.py:543
  42.4 4.4 %collective-permute-start.3 = (f32[4,32,256]{2,1,0:T(8,128)S(1)}, f32[4,32,256]{2,1,0:T(8,128)S(1)}, u32[]{:S(2)}, u32[]{:S(2)}) collective-permute-start(f32[4,32,256]{2,1,0:T(8,128)S(1)} %reduce_sum.9), channel_id=1, source_target_pairs={{0,1},{1,0},{2,3},{3,2},{4,5},{5,4},{6,7},{7,6},{8,9},{9,8},{10,11... | collective-permute-start | bytes 393224 | tf_op jit(solution)/shard_map/ppermute | solution.py:546

commit v3 on v2

--- a/solution.py
+++ b/solution.py
@@ -11,7 +11,6 @@
 FAR = float(1 << 20)
 WINDOW = 16
 VMEM_LIMIT = 20 << 20
-EDGE_LIMIT = 62 << 20
 TINY = 16
 VMEM = pltpu.VMEM
 F32 = jnp.float32
@@ -101,8 +100,9 @@
 
 
 def edge_kernel(
-    rec_live, rec_cells, target, p0_h, adj_h, density_h, speed_h, admittance_h, mask_h,
-    up, down, p0, adj, density, speed, admittance, mask, vel_s, pd_s, stack, sems,
+    live_h, cells_h, target_h, p0_h, adj_h, density_h, speed_h, admittance_h, mask_h,
+    up, down, p0, adj, density, speed, admittance, mask, vel_s, pd_s, stack,
+    rec_live, rec_cells, target, sems, small_sems,
 ):
     shots, depth, width_x, width_y = p0.shape
     slots, capsules = rec_cells.shape
@@ -114,13 +114,21 @@
         pairs = [(h.at[some], v.at[some]) for h, v in (
             (density_h, density), (speed_h, speed), (admittance_h, admittance), (mask_h, mask))]
         pairs.insert(0, (p0_h.at[:, some], p0.at[:, some]))
-        pairs.append((adj_h.at[:, pl.ds(side * last, 1)], adj.at[:, pl.ds(side, 1)]))
+        pairs.append((adj_h.at[:, some], adj.at[:, some]))
         copies.append([
             pltpu.make_async_copy(a, b, sems.at[side, k]) for k, (a, b) in enumerate(pairs)
         ])
     for copy in copies[0] + copies[1]:
         copy.start()
+    smalls = [
+        pltpu.make_async_copy(a, b, small_sems.at[k])
+        for k, (a, b) in enumerate(((live_h, rec_live), (cells_h, rec_cells), (target_h, target)))
+    ]
+    for copy in smalls:
+        copy.start()
     masks = edge_masks((width_x, width_y))
+    for copy in smalls:
+        copy.wait()
     plane, _, row_x, col = split_cells(cell_lanes(rec_cells), width_x, width_y)
     live = live_lanes(rec_live, slots, capsules)
     columns = pick_columns(col, width_y)
@@ -162,7 +170,7 @@
                 first[z] = damp[z] * (here + pres[z] * total)
             out[s * width_x : (s + 1) * width_x, :] = p0[s, near]
             out[(2 + s) * width_x : (3 + s) * width_x, :] = first[near]
-            out[(4 + s) * width_x : (5 + s) * width_x, :] = pd_s[near] * adj[s, side]
+            out[(4 + s) * width_x : (5 + s) * width_x, :] = pd_s[near] * adj[s, near]
             q_far = p0[s, far] + first[far]
             q_third = p0[s, third] + first[third]
             beyond = vel_s[min(far, third)]
@@ -477,26 +485,41 @@
         ]
 
     params = pltpu.CompilerParams(vmem_limit_bytes=VMEM_LIMIT)
-    up, down = pl.pallas_call(
+    up, down, p0, adj, density, speed, admittance, bound_mask = pl.pallas_call(
         edge_kernel,
-        in_specs=ins(9, 1, 6),
-        out_specs=ins(2),
-        out_shape=outs(message, message),
+        in_specs=ins(9, 0, 9),
+        out_specs=ins(8),
+        out_shape=[
+            VMEM(message, F32), VMEM(message, F32), VMEM(field, F32), VMEM(field, F32),
+            VMEM(slab, F32), VMEM(slab, F32), VMEM(slab, F32), VMEM(slab, jnp.int32),
+        ],
         scratch_shapes=[
-            VMEM(field, F32), VMEM((shots, 2, width_x, width_y), F32),
-            VMEM(slab, F32), VMEM(slab, F32), VMEM(slab, F32), VMEM(slab, jnp.int32),
             VMEM(slab, F32), VMEM(slab, F32), VMEM((14 * width_x, width_y), F32),
-            pltpu.SemaphoreType.DMA((2, 6)),
+            pltpu.SMEM(rec_live.shape, jnp.int32), VMEM(rec_cells.shape, jnp.int32),
+            VMEM(target.shape, F32),
+            pltpu.SemaphoreType.DMA((2, 6)), pltpu.SemaphoreType.DMA((3,)),
         ],
-        compiler_params=pltpu.CompilerParams(vmem_limit_bytes=EDGE_LIMIT),
+        compiler_params=params,
         name="edge",
     )(
-        rec_live, rec_cells, target, pressure_init, adjoint_init, density, speed, admittance,
-        bound_mask,
-    )
-
-    below = lax.ppermute(up, "slab", [(i, i + 1) for i in range(slabs - 1)])
-    above = lax.ppermute(down, "slab", [(i + 1, i) for i in range(slabs - 1)])
+        *[
+            pltpu.with_memory_space_constraint(array, pltpu.HBM)
+            for array in (
+                rec_live, rec_cells, target,
+                pressure_init, adjoint_init, density, speed, admittance, bound_mask,
+            )
+        ],
+    )
+
+    even = lax.rem(lax.axis_index("slab"), 2) == 0
+
+    def exchange(value, first):
+        pairs = [(i, i + 1) for i in range(first, slabs - 1, 2)]
+        return lax.ppermute(value, "slab", pairs + [(b, a) for a, b in pairs])
+
+    inner = exchange(jnp.where(even, up, down), 0)
+    outer = exchange(jnp.where(even, down, up), 1)
+    below, above = jnp.where(even, outer, inner), jnp.where(even, inner, outer)
 
     table = jax.ShapeDtypeStruct((LANES, 2 * LANES), jnp.bfloat16)
     b1, b2, vel, pres, damp, pd, back, grad, rows, high, low = pl.pallas_call(
@@ -512,8 +535,7 @@
         cost_estimate=pl.CostEstimate(flops=20_000_000, bytes_accessed=6_000_000, transcendentals=0),
         name="middle",
     )(
-        rec_live, rec_cells, target, encoder, pressure_init, adjoint_init, density, speed,
-        admittance, bound_mask,
+        rec_live, rec_cells, target, encoder, p0, adj, density, speed, admittance, bound_mask,
     )
 
     core = lax.rem(lax.axis_index("shot"), 2)
@@ -532,8 +554,7 @@
         compiler_params=params,
         name="last",
     )(
-        core[None], corners, below, above, pressure_init, adjoint_init, bound_mask, vel, pres,
-        damp, pd, back, rows, high, low, b1, b2, grad,
+        core[None], corners, below, above, p0, adj, bound_mask, vel, pres, damp, pd, back, rows, high, low, b1, b2, grad,
     )
 
     pairs = [(i, i ^ 1) for i in range(peers)]
@@ -543,9 +564,10 @@
     total = lax.all_to_all(
         copies, "shot", split_axis=0, concat_axis=0, tiled=True, axis_index_groups=groups
     ).sum(axis=0)
+    total, coded, later = lax.optimization_barrier((total, coded, core))
     other = lax.ppermute(total, "shot", pairs)
     gradient = jnp.where(
-        core == 0, jnp.concatenate([total, other], 0), jnp.concatenate([other, total], 0)
+        later == 0, jnp.concatenate([total, other], 0), jnp.concatenate([other, total], 0)
     )
     signals = coded[: steps * shots, : slots * capsules]
     signals = signals.reshape(steps, shots, slots, capsules)[..., :channels]

time: 47.9 us -> 44.1 us (0.921)
  the two profiles are of different devices: /device:TPU:103 before, /device:TPU:385 now
where the time goes in v3:
time: 44.1 us; the launch traced here: 43.7 us
  starting transfers between devices  15.9 us (36%)
  blocking collectives  12.6 us (29%)
  Pallas kernels  6.58 us (15%)
  waiting for transfers between devices  4.73 us (11%)
  local copies, waits for them, and re-layouts  2.08 us (5%)
  other arithmetic  0.98 us (2%)
  between operations  0.8 us (2%)
    all_to_all x1, blocking collectives, body(): lax.all_to_all(copies, 'shot', split_axis=0, concat_axis=0, tiled=True, a...  12.6 us
    ppermute x2, starting transfers between devices, exchange(): return lax.ppermute(value, 'slab', pairs + [(b, a) for a, b in pairs])  8.5 us
    ppermute x1, starting transfers between devices, body(): total = keep + lax.ppermute(send, 'shot', pairs)  3.72 us
    ppermute x1, starting transfers between devices, body(): other = lax.ppermute(total, 'shot', pairs)  3.69 us
    ppermute x2, waiting for transfers between devices, exchange(): return lax.ppermute(value, 'slab', pairs + [(b, a) for a, b in pairs])  3.41 us
    pallas_call x1, Pallas kernels, body(): pl.pallas_call(edge_kernel, in_specs=ins(9, 0, 9), out_specs=ins(8), out_...  2.47 us
    pallas_call x1, Pallas kernels, body(): pl.pallas_call(middle_kernel, in_specs=ins(10, 1), out_specs=ins(11), out...  2.17 us
    unnamed x9, local copies, waits for them, and re-layouts  1.95 us
  transfers between devices with their start and end apart: 4, of which 3 were waited for; matrix products, arithmetic and copies ran while one was open for 2% of the time, Pallas kernels for 5%

profile of v3, /device:TPU:385, one launch (start us, length us, event | category | flops | bytes accessed | tf_op | source)
XLA Modules:
  0.0 43.7 jit_solution(979837200282660366)
XLA Ops:
  0.6 2.5 %edge.1 = (f32[272,256]{1,0:T(8,128)S(1)}, f32[272,256]{1,0:T(8,128)S(1)}, f32[2,8,32,256]{3,2,1,0:T(8,128)S(1)}, f32[2,8,32,256]{3,2,1,0:T(8,128)S(1)}, f32[8,3...) custom-call(s32[3]{0:T(128)} %rec_live.1, ...), custom_call_target="tpu_custom_call" | custom-call | tf_op jit(solution)/shard_map/edge/pallas_call | solution.py:488
  3.2 0.0 copy-start.2
  3.2 3.1 %collective-permute-start.1 = (f32[272,256]{1,0:T(8,128)S(1)}, f32[272,256]{1,0:T(8,128)S(1)}, u32[]{:S(2)}, u32[]{:S(2)}) collective-permute-start(f32[272,256]{1,0:T(8,128)S(1)} %get-tuple-element.58), channel_id=1, source_target_pairs={{0,8},{16,24},{32,40},{48,56},{64,72},{80,88},{96,104},{112,120},{... | collective-permute-start | bytes 835592 | tf_op jit(solution)/shard_map/ppermute | solution.py:518
  6.3 5.4 %collective-permute-start = (f32[272,256]{1,0:T(8,128)S(1)}, f32[272,256]{1,0:T(8,128)S(1)}, u32[]{:S(2)}, u32[]{:S(2)}) collective-permute-start(f32[272,256]{1,0:T(8,128)S(1)} %get-tuple-element.59), channel_id=1, source_target_pairs={{8,16},{24,32},{40,48},{56,64},{72,80},{88,96},{104,112},{120,128}... | collective-permute-start | bytes 835592 | tf_op jit(solution)/shard_map/ppermute | solution.py:518
  11.7 0.0 copy-start.1
  11.7 0.7 %copy-done.1 = s32[3,32]{1,0:T(4,128)S(1)} copy-done((s32[3,32]{1,0:T(4,128)S(1)}, s32[3,32]{1,0:T(4,128)}, u32[]{:S(2)}) %copy-start.1) | copy-done | bytes 408
  12.4 0.1 reduce_min.9.corners
  12.5 0.0 copy-start
  12.5 0.0 copy-start.3
  12.5 0.0 copy-done.2
  12.5 0.7 %copy-done = f32[3,2,2,25]{3,2,1,0:T(2,128)S(1)} copy-done((f32[3,2,2,25]{3,2,1,0:T(2,128)S(1)}, f32[3,2,2,25]{3,2,1,0:T(2,128)}, u32[]{:S(2)}) %copy-start) | copy-done | bytes 1224
  13.2 0.0 copy-done.3
  13.2 2.2 %middle.1 = (f32[2,8,32,256]{3,2,1,0:T(8,128)S(1)}, f32[2,8,32,256]{3,2,1,0:T(8,128)S(1)}, f32[8,32,256]{2,1,0:T(8,128)S(1)}, f32[8,32,256]{2,1,0:T(8,128)S(1)},...) custom-call(s32[3]{0:T(128)S(1)} %copy-done.3, ...), custom_call_target="tpu_custom_call" | custom-call | flops 20000000 | bytes 6000000 | tf_op jit(solution)/shard_map/middle/pallas_call | solution.py:525
  15.4 0.0 collective-permute-done.1
  15.4 3.4 %collective-permute-done = f32[272,256]{1,0:T(8,128)S(1)} collective-permute-done((f32[272,256]{1,0:T(8,128)S(1)}, f32[272,256]{1,0:T(8,128)S(1)}, u32[]{:S(2)}, u32[]{:S(2)}) %collective-permute-start) | collective-permute-done | bytes 278560 | tf_op jit(solution)/shard_map/ppermute | solution.py:518
  18.8 1.9 %last.1 = (f32[4,32,256]{2,1,0:T(8,128)S(1)}, f32[4,32,256]{2,1,0:T(8,128)S(1)}, f32[8,128]{1,0:T(8,128)S(1)}, f32[2,8,32,256]{3,2,1,0:T(8,128)S(1)}, f32[2,8,32...) custom-call(s32[1]{0:T(128)} %bitcast.core, ...), custom_call_target="tpu_custom_call", output_to_operand_aliasing={{3}: (15, {}), {4}: (16, {}), {5}: (17, {})} | custom-call | tf_op jit(solution)/shard_map/last/pallas_call | solution.py:544
  20.8 3.7 %collective-permute-start.2 = (f32[4,32,256]{2,1,0:T(8,128)S(1)}, f32[4,32,256]{2,1,0:T(8,128)S(1)}, u32[]{:S(2)}, u32[]{:S(2)}) collective-permute-start(f32[4,32,256]{2,1,0:T(8,128)S(1)} %get-tuple-element.47), channel_id=1, source_target_pairs={{0,1},{1,0},{2,3},{3,2},{4,5},{5,4},{6,7},{7,6},{8,9},{9,8},{10,11... | collective-permute-start | bytes 393224 | tf_op jit(solution)/shard_map/ppermute | solution.py:562
  24.5 1.0 %collective-permute-done.2 = f32[4,32,256]{2,1,0:T(8,128)S(1)} collective-permute-done((f32[4,32,256]{2,1,0:T(8,128)S(1)}, f32[4,32,256]{2,1,0:T(8,128)S(1)}, u32[]{:S(2)}, u32[]{:S(2)}) %collective-permute-start.2) | collective-permute-done | bytes 131104 | tf_op jit(solution)/shard_map/ppermute | solution.py:562
  25.5 12.6 %all_to_all.5 = f32[4,4,32,256]{3,2,1,0:T(8,128)S(1)} all-to-all(f32[4,4,32,256]{3,2,1,0:T(8,128)S(1)} %broadcast_in_dim.7), channel_id=1, replica_groups={{0,2,4,6},{1,3,5,7},{8,10,12,14},{9,11,13,15},{16,18,20,22},{17,19,21,2..., dimensions={0} | all-to-all | bytes 1048576 | tf_op jit(solution)/shard_map/all_to_all | solution.py:564
  38.2 0.1 reshape.7
  38.3 3.7 %collective-permute-start.3 = (f32[4,32,256]{2,1,0:T(8,128)S(1)}, f32[4,32,256]{2,1,0:T(8,128)S(1)}, u32[]{:S(2)}, u32[]{:S(2)}) collective-permute-start(f32[4,32,256]{2,1,0:T(8,128)S(1)} %reduce_sum.9), channel_id=1, source_target_pairs={{0,1},{1,0},{2,3},{3,2},{4,5},{5,4},{6,7},{7,6},{8,9},{9,8},{10,11... | collective-permute-start | bytes 393224 | tf_op jit(solution)/shard_map/ppermute | solution.py:568
  42.0 0.6 %copy.17 = f32[3,2,2,25]{3,2,1,0:T(2,128)} copy(f32[3,2,2,25]{3,0,1,2:T(4,128)S(1)} %slice_bitcast_fusion) | data formatting | bytes 2400
  42.6 0.4 collective-permute-done.3
  43.0 0.7 %maximum_select_fusion = f32[8,32,256]{2,1,0:T(8,128)} fusion(f32[4,32,256]{2,1,0:T(8,128)S(1)} %collective-permute-done.3, f32[4,32,256]{2,1,0:T(8,128)S(1)} %reduce_sum.9, pred[]{:T(512)S(6)} %eq.7), kind=kLoop, calls=%fused_computation | loop fusion | flops 196608 | bytes 524289 | tf_op jit(solution)/shard_map/jit(_where)/select_n | solution.py:569
  (7 shorter events, 0.2 us)
Async XLA Ops:
  3.2 9.4 %copy-start.2 = (f32[32,25]{1,0:T(8,128)S(1)}, f32[32,25]{1,0:T(8,128)}, u32[]{:S(2)}) copy-start(f32[32,25]{1,0:T(8,128)} %encoder.1) | copy-start | bytes 9604
  3.2 12.2 %collective-permute-start.1 = (f32[272,256]{1,0:T(8,128)S(1)}, f32[272,256]{1,0:T(8,128)S(1)}, u32[]{:S(2)}, u32[]{:S(2)}) collective-permute-start(f32[272,256]{1,0:T(8,128)S(1)} %get-tuple-element.58), channel_id=1, source_target_pairs={{0,8},{16,24},{32,40},{48,56},{64,72},{80,88},{96,104},{112,120},{... | collective-permute-start | bytes 835592 | tf_op jit(solution)/shard_map/ppermute | solution.py:518
  6.3 12.5 %collective-permute-start = (f32[272,256]{1,0:T(8,128)S(1)}, f32[272,256]{1,0:T(8,128)S(1)}, u32[]{:S(2)}, u32[]{:S(2)}) collective-permute-start(f32[272,256]{1,0:T(8,128)S(1)} %get-tuple-element.59), channel_id=1, source_target_pairs={{8,16},{24,32},{40,48},{56,64},{72,80},{88,96},{104,112},{120,128}... | collective-permute-start | bytes 835592 | tf_op jit(solution)/shard_map/ppermute | solution.py:518
  11.7 0.7 %copy-start.1 = (s32[3,32]{1,0:T(4,128)S(1)}, s32[3,32]{1,0:T(4,128)}, u32[]{:S(2)}) copy-start(s32[3,32]{1,0:T(4,128)} %rec_cells.1) | copy-start | bytes 1156
  12.5 0.7 %copy-start = (f32[3,2,2,25]{3,2,1,0:T(2,128)S(1)}, f32[3,2,2,25]{3,2,1,0:T(2,128)}, u32[]{:S(2)}) copy-start(f32[3,2,2,25]{3,2,1,0:T(2,128)} %target.1) | copy-start | bytes 3604
  12.5 0.7 %copy-start.3 = (s32[3]{0:T(128)S(1)}, s32[3]{0:T(128)}, u32[]{:S(2)}) copy-start(s32[3]{0:T(128)} %rec_live.1) | copy-start | bytes 40
  20.8 4.7 %collective-permute-start.2 = (f32[4,32,256]{2,1,0:T(8,128)S(1)}, f32[4,32,256]{2,1,0:T(8,128)S(1)}, u32[]{:S(2)}, u32[]{:S(2)}) collective-permute-start(f32[4,32,256]{2,1,0:T(8,128)S(1)} %get-tuple-element.47), channel_id=1, source_target_pairs={{0,1},{1,0},{2,3},{3,2},{4,5},{5,4},{6,7},{7,6},{8,9},{9,8},{10,11... | collective-permute-start | bytes 393224 | tf_op jit(solution)/shard_map/ppermute | solution.py:562
  38.3 4.7 %collective-permute-start.3 = (f32[4,32,256]{2,1,0:T(8,128)S(1)}, f32[4,32,256]{2,1,0:T(8,128)S(1)}, u32[]{:S(2)}, u32[]{:S(2)}) collective-permute-start(f32[4,32,256]{2,1,0:T(8,128)S(1)} %reduce_sum.9), channel_id=1, source_target_pairs={{0,1},{1,0},{2,3},{3,2},{4,5},{5,4},{6,7},{7,6},{8,9},{9,8},{10,11... | collective-permute-start | bytes 393224 | tf_op jit(solution)/shard_map/ppermute | solution.py:568

commit v4 on v3

--- a/solution.py
+++ b/solution.py
@@ -6,6 +6,7 @@
 from jax.experimental import pallas as pl
 from jax.experimental.pallas import tpu as pltpu
 from jax.sharding import PartitionSpec as P
+
 
 LANES = 128
 FAR = float(1 << 20)
@@ -114,17 +115,18 @@
         pairs = [(h.at[some], v.at[some]) for h, v in (
             (density_h, density), (speed_h, speed), (admittance_h, admittance), (mask_h, mask))]
         pairs.insert(0, (p0_h.at[:, some], p0.at[:, some]))
-        pairs.append((adj_h.at[:, some], adj.at[:, some]))
+        face = pl.ds(side * last, 1)
+        pairs.append((adj_h.at[:, face], adj.at[:, face]))
         copies.append([
             pltpu.make_async_copy(a, b, sems.at[side, k]) for k, (a, b) in enumerate(pairs)
         ])
-    for copy in copies[0] + copies[1]:
-        copy.start()
+    inside = pl.ds(1, depth - 2)
+    rest = pltpu.make_async_copy(adj_h.at[:, inside], adj.at[:, inside], small_sems.at[3])
     smalls = [
         pltpu.make_async_copy(a, b, small_sems.at[k])
         for k, (a, b) in enumerate(((live_h, rec_live), (cells_h, rec_cells), (target_h, target)))
     ]
-    for copy in smalls:
+    for copy in smalls + copies[0] + copies[1] + [rest]:
         copy.start()
     masks = edge_masks((width_x, width_y))
     for copy in smalls:
@@ -137,9 +139,9 @@
         for copy in copies[side]:
             copy.wait()
         if side == 0:
-            out, planes, lowest, inward = down, (0, 1, 2), 0, 1
+            out, planes, lowest = down, (0, 1, 2), 0
         else:
-            out, planes, lowest, inward = up, (last, last - 1, last - 2), half, -1
+            out, planes, lowest = up, (last, last - 1, last - 2), half
         near, far, third = planes
         span = range(lowest, lowest + half)
         weights, pres, damp = {}, {}, {}
@@ -200,6 +202,7 @@
         start = 8 * width_x
         out[start : start + TINY, :] = jnp.zeros((TINY, width_y), F32)
         out[start : start + TINY, 0:LANES] = jnp.concatenate(tiny, axis=0)
+    rest.wait()
 
 
 def middle_kernel(
@@ -461,6 +464,19 @@
         send[z] = grad[half - mine + z]
 
 
+def join_kernel(core, mine, other, out, sems):
+    half = mine.shape[0]
+    start = core[0] * half
+    copies = [
+        pltpu.make_async_copy(mine, out.at[pl.ds(start, half)], sems.at[0]),
+        pltpu.make_async_copy(other, out.at[pl.ds(half - start, half)], sems.at[1]),
+    ]
+    for copy in copies:
+        copy.start()
+    for copy in copies:
+        copy.wait()
+
+
 def body(
     pressure_init, adjoint_init, density, speed, admittance, bound_mask,
     rec_cells, rec_live, encoder, target,
@@ -497,7 +513,7 @@
             VMEM(slab, F32), VMEM(slab, F32), VMEM((14 * width_x, width_y), F32),
             pltpu.SMEM(rec_live.shape, jnp.int32), VMEM(rec_cells.shape, jnp.int32),
             VMEM(target.shape, F32),
-            pltpu.SemaphoreType.DMA((2, 6)), pltpu.SemaphoreType.DMA((3,)),
+            pltpu.SemaphoreType.DMA((2, 6)), pltpu.SemaphoreType.DMA((4,)),
         ],
         compiler_params=params,
         name="edge",
@@ -517,8 +533,8 @@
         pairs = [(i, i + 1) for i in range(first, slabs - 1, 2)]
         return lax.ppermute(value, "slab", pairs + [(b, a) for a, b in pairs])
 
+    outer = exchange(jnp.where(even, down, up), 1)
     inner = exchange(jnp.where(even, up, down), 0)
-    outer = exchange(jnp.where(even, down, up), 1)
     below, above = jnp.where(even, outer, inner), jnp.where(even, inner, outer)
 
     table = jax.ShapeDtypeStruct((LANES, 2 * LANES), jnp.bfloat16)
@@ -566,9 +582,15 @@
     ).sum(axis=0)
     total, coded, later = lax.optimization_barrier((total, coded, core))
     other = lax.ppermute(total, "shot", pairs)
-    gradient = jnp.where(
-        later == 0, jnp.concatenate([total, other], 0), jnp.concatenate([other, total], 0)
-    )
+    gradient = pl.pallas_call(
+        join_kernel,
+        in_specs=ins(3, 1),
+        out_specs=pl.BlockSpec(memory_space=pltpu.HBM),
+        out_shape=pltpu.HBM(slab, F32),
+        scratch_shapes=[pltpu.SemaphoreType.DMA((2,))],
+        compiler_params=params,
+        name="join",
+    )(later[None], total, other)
     signals = coded[: steps * shots, : slots * capsules]
     signals = signals.reshape(steps, shots, slots, capsules)[..., :channels]
     return jnp.transpose(signals, (2, 1, 0, 3)), gradient

time: 44.1 us -> 43.9 us (level)
  other arithmetic: 0.98 us -> 0.25 us
  Pallas kernels: 6.58 us -> 7.17 us
    select_n x1 -> x0, other arithmetic: 0.73 us -> none  [body(): jnp.where(later == 0, jnp.concatenate([total, other], 0), jnp.concatenate...]
    pallas_call x0 -> x1, Pallas kernels: none -> 0.71 us  [body(): pl.pallas_call(join_kernel, in_specs=ins(3, 1), out_specs=pl.BlockSpec(me...]
where the time goes in v4:
time: 43.9 us; the launch traced here: 43.5 us
  starting transfers between devices  15.9 us (36%)
  blocking collectives  12.6 us (29%)
  Pallas kernels  7.17 us (16%)
  waiting for transfers between devices  4.72 us (11%)
  local copies, waits for them, and re-layouts  2.08 us (5%)
  between operations  0.79 us (2%)
    all_to_all x1, blocking collectives, body(): lax.all_to_all(copies, 'shot', split_axis=0, concat_axis=0, tiled=True, a...  12.6 us
    ppermute x2, starting transfers between devices, exchange(): return lax.ppermute(value, 'slab', pairs + [(b, a) for a, b in pairs])  8.5 us
    ppermute x1, starting transfers between devices, body(): total = keep + lax.ppermute(send, 'shot', pairs)  3.71 us
    ppermute x1, starting transfers between devices, body(): other = lax.ppermute(total, 'shot', pairs)  3.69 us
    ppermute x2, waiting for transfers between devices, exchange(): return lax.ppermute(value, 'slab', pairs + [(b, a) for a, b in pairs])  3.41 us
    pallas_call x1, Pallas kernels, body(): pl.pallas_call(edge_kernel, in_specs=ins(9, 0, 9), out_specs=ins(8), out_...  2.34 us
    pallas_call x1, Pallas kernels, body(): pl.pallas_call(middle_kernel, in_specs=ins(10, 1), out_specs=ins(11), out...  2.17 us
    unnamed x9, local copies, waits for them, and re-layouts  1.95 us
  transfers between devices with their start and end apart: 4, of which 3 were waited for; matrix products, arithmetic and copies ran while one was open for 2% of the time, Pallas kernels for 5%

profile of v4, /device:TPU:385, one launch (start us, length us, event | category | flops | bytes accessed | tf_op | source)
XLA Modules:
  0.0 43.5 jit_solution(9300069178906492187)
XLA Ops:
  0.6 2.3 %edge.1 = (f32[272,256]{1,0:T(8,128)S(1)}, f32[272,256]{1,0:T(8,128)S(1)}, f32[2,8,32,256]{3,2,1,0:T(8,128)S(1)}, f32[2,8,32,256]{3,2,1,0:T(8,128)S(1)}, f32[8,3...) custom-call(s32[3]{0:T(128)} %rec_live.1, ...), custom_call_target="tpu_custom_call" | custom-call | tf_op jit(solution)/shard_map/edge/pallas_call | solution.py:504
  3.0 0.0 copy-start.2
  3.1 3.1 %collective-permute-start.1 = (f32[272,256]{1,0:T(8,128)S(1)}, f32[272,256]{1,0:T(8,128)S(1)}, u32[]{:S(2)}, u32[]{:S(2)}) collective-permute-start(f32[272,256]{1,0:T(8,128)S(1)} %get-tuple-element.58), channel_id=1, source_target_pairs={{0,8},{16,24},{32,40},{48,56},{64,72},{80,88},{96,104},{112,120},{... | collective-permute-start | bytes 835592 | tf_op jit(solution)/shard_map/ppermute | solution.py:534
  6.2 5.4 %collective-permute-start = (f32[272,256]{1,0:T(8,128)S(1)}, f32[272,256]{1,0:T(8,128)S(1)}, u32[]{:S(2)}, u32[]{:S(2)}) collective-permute-start(f32[272,256]{1,0:T(8,128)S(1)} %get-tuple-element.59), channel_id=1, source_target_pairs={{8,16},{24,32},{40,48},{56,64},{72,80},{88,96},{104,112},{120,128}... | collective-permute-start | bytes 835592 | tf_op jit(solution)/shard_map/ppermute | solution.py:534
  11.6 0.0 copy-start.1
  11.6 0.7 %copy-done.1 = s32[3,32]{1,0:T(4,128)S(1)} copy-done((s32[3,32]{1,0:T(4,128)S(1)}, s32[3,32]{1,0:T(4,128)}, u32[]{:S(2)}) %copy-start.1) | copy-done | bytes 408
  12.3 0.1 reduce_min.9.corners
  12.4 0.0 copy-start
  12.4 0.0 copy-start.3
  12.4 0.0 copy-done.2
  12.4 0.7 %copy-done = f32[3,2,2,25]{3,2,1,0:T(2,128)S(1)} copy-done((f32[3,2,2,25]{3,2,1,0:T(2,128)S(1)}, f32[3,2,2,25]{3,2,1,0:T(2,128)}, u32[]{:S(2)}) %copy-start) | copy-done | bytes 1224
  13.1 0.0 copy-done.3
  13.1 2.2 %middle.1 = (f32[2,8,32,256]{3,2,1,0:T(8,128)S(1)}, f32[2,8,32,256]{3,2,1,0:T(8,128)S(1)}, f32[8,32,256]{2,1,0:T(8,128)S(1)}, f32[8,32,256]{2,1,0:T(8,128)S(1)},...) custom-call(s32[3]{0:T(128)S(1)} %copy-done.3, ...), custom_call_target="tpu_custom_call" | custom-call | flops 20000000 | bytes 6000000 | tf_op jit(solution)/shard_map/middle/pallas_call | solution.py:541
  15.2 0.0 collective-permute-done.1
  15.3 3.4 %collective-permute-done = f32[272,256]{1,0:T(8,128)S(1)} collective-permute-done((f32[272,256]{1,0:T(8,128)S(1)}, f32[272,256]{1,0:T(8,128)S(1)}, u32[]{:S(2)}, u32[]{:S(2)}) %collective-permute-start) | collective-permute-done | bytes 278560 | tf_op jit(solution)/shard_map/ppermute | solution.py:534
  18.7 1.9 %last.1 = (f32[4,32,256]{2,1,0:T(8,128)S(1)}, f32[4,32,256]{2,1,0:T(8,128)S(1)}, f32[8,128]{1,0:T(8,128)S(1)}, f32[2,8,32,256]{3,2,1,0:T(8,128)S(1)}, f32[2,8,32...) custom-call(s32[1]{0:T(128)} %bitcast.core, ...), custom_call_target="tpu_custom_call", output_to_operand_aliasing={{3}: (15, {}), {4}: (16, {}), {5}: (17, {})} | custom-call | tf_op jit(solution)/shard_map/last/pallas_call | solution.py:560
  20.6 3.7 %collective-permute-start.2 = (f32[4,32,256]{2,1,0:T(8,128)S(1)}, f32[4,32,256]{2,1,0:T(8,128)S(1)}, u32[]{:S(2)}, u32[]{:S(2)}) collective-permute-start(f32[4,32,256]{2,1,0:T(8,128)S(1)} %get-tuple-element.47), channel_id=1, source_target_pairs={{0,1},{1,0},{2,3},{3,2},{4,5},{5,4},{6,7},{7,6},{8,9},{9,8},{10,11... | collective-permute-start | bytes 393224 | tf_op jit(solution)/shard_map/ppermute | solution.py:578
  24.4 1.0 %collective-permute-done.2 = f32[4,32,256]{2,1,0:T(8,128)S(1)} collective-permute-done((f32[4,32,256]{2,1,0:T(8,128)S(1)}, f32[4,32,256]{2,1,0:T(8,128)S(1)}, u32[]{:S(2)}, u32[]{:S(2)}) %collective-permute-start.2) | collective-permute-done | bytes 131104 | tf_op jit(solution)/shard_map/ppermute | solution.py:578
  25.4 12.6 %all_to_all.5 = f32[4,4,32,256]{3,2,1,0:T(8,128)S(1)} all-to-all(f32[4,4,32,256]{3,2,1,0:T(8,128)S(1)} %broadcast_in_dim.10), channel_id=1, replica_groups={{0,2,4,6},{1,3,5,7},{8,10,12,14},{9,11,13,15},{16,18,20,22},{17,19,21,2..., dimensions={0} | all-to-all | bytes 1048576 | tf_op jit(solution)/shard_map/all_to_all | solution.py:580
  38.1 0.1 reshape.7
  38.2 3.7 %collective-permute-start.3 = (f32[4,32,256]{2,1,0:T(8,128)S(1)}, f32[4,32,256]{2,1,0:T(8,128)S(1)}, u32[]{:S(2)}, u32[]{:S(2)}) collective-permute-start(f32[4,32,256]{2,1,0:T(8,128)S(1)} %reduce_sum.9.mine), channel_id=1, source_target_pairs={{0,1},{1,0},{2,3},{3,2},{4,5},{5,4},{6,7},{7,6},{8,9},{9,8},{10,11... | collective-permute-start | bytes 393224 | tf_op jit(solution)/shard_map/ppermute | solution.py:584
  41.9 0.6 %copy.17 = f32[3,2,2,25]{3,2,1,0:T(2,128)} copy(f32[3,2,2,25]{3,0,1,2:T(4,128)S(1)} %slice_bitcast_fusion) | data formatting | bytes 2400
  42.5 0.4 collective-permute-done.3.other
  42.8 0.7 %join.1 = f32[8,32,256]{2,1,0:T(8,128)} custom-call(s32[1]{0:T(128)} %bitcast.2.core, f32[4,32,256]{2,1,0:T(8,128)S(1)} %reduce_sum.9.mine, f32[4,32,256]{2,1,0:T(8,128)S(1)} %collective-permute-done.3.other), custom_call_target="tpu_custom_call" | custom-call | tf_op jit(solution)/shard_map/join/pallas_call | solution.py:585
  (7 shorter events, 0.2 us)
Async XLA Ops:
  3.0 9.4 %copy-start.2 = (f32[32,25]{1,0:T(8,128)S(1)}, f32[32,25]{1,0:T(8,128)}, u32[]{:S(2)}) copy-start(f32[32,25]{1,0:T(8,128)} %encoder.1) | copy-start | bytes 9604
  3.1 12.2 %collective-permute-start.1 = (f32[272,256]{1,0:T(8,128)S(1)}, f32[272,256]{1,0:T(8,128)S(1)}, u32[]{:S(2)}, u32[]{:S(2)}) collective-permute-start(f32[272,256]{1,0:T(8,128)S(1)} %get-tuple-element.58), channel_id=1, source_target_pairs={{0,8},{16,24},{32,40},{48,56},{64,72},{80,88},{96,104},{112,120},{... | collective-permute-start | bytes 835592 | tf_op jit(solution)/shard_map/ppermute | solution.py:534
  6.2 12.5 %collective-permute-start = (f32[272,256]{1,0:T(8,128)S(1)}, f32[272,256]{1,0:T(8,128)S(1)}, u32[]{:S(2)}, u32[]{:S(2)}) collective-permute-start(f32[272,256]{1,0:T(8,128)S(1)} %get-tuple-element.59), channel_id=1, source_target_pairs={{8,16},{24,32},{40,48},{56,64},{72,80},{88,96},{104,112},{120,128}... | collective-permute-start | bytes 835592 | tf_op jit(solution)/shard_map/ppermute | solution.py:534
  11.6 0.7 %copy-start.1 = (s32[3,32]{1,0:T(4,128)S(1)}, s32[3,32]{1,0:T(4,128)}, u32[]{:S(2)}) copy-start(s32[3,32]{1,0:T(4,128)} %rec_cells.1) | copy-start | bytes 1156
  12.4 0.7 %copy-start = (f32[3,2,2,25]{3,2,1,0:T(2,128)S(1)}, f32[3,2,2,25]{3,2,1,0:T(2,128)}, u32[]{:S(2)}) copy-start(f32[3,2,2,25]{3,2,1,0:T(2,128)} %target.1) | copy-start | bytes 3604
  12.4 0.7 %copy-start.3 = (s32[3]{0:T(128)S(1)}, s32[3]{0:T(128)}, u32[]{:S(2)}) copy-start(s32[3]{0:T(128)} %rec_live.1) | copy-start | bytes 40
  20.6 4.7 %collective-permute-start.2 = (f32[4,32,256]{2,1,0:T(8,128)S(1)}, f32[4,32,256]{2,1,0:T(8,128)S(1)}, u32[]{:S(2)}, u32[]{:S(2)}) collective-permute-start(f32[4,32,256]{2,1,0:T(8,128)S(1)} %get-tuple-element.47), channel_id=1, source_target_pairs={{0,1},{1,0},{2,3},{3,2},{4,5},{5,4},{6,7},{7,6},{8,9},{9,8},{10,11... | collective-permute-start | bytes 393224 | tf_op jit(solution)/shard_map/ppermute | solution.py:578
  38.2 4.7 %collective-permute-start.3 = (f32[4,32,256]{2,1,0:T(8,128)S(1)}, f32[4,32,256]{2,1,0:T(8,128)S(1)}, u32[]{:S(2)}, u32[]{:S(2)}) collective-permute-start(f32[4,32,256]{2,1,0:T(8,128)S(1)} %reduce_sum.9.mine), channel_id=1, source_target_pairs={{0,1},{1,0},{2,3},{3,2},{4,5},{5,4},{6,7},{7,6},{8,9},{9,8},{10,11... | collective-permute-start | bytes 393224 | tf_op jit(solution)/shard_map/ppermute | solution.py:584

commit v5 on v4

v5 whole, which is shorter than its diff:
```python
import functools

import jax
import jax.numpy as jnp
from jax import lax
from jax.experimental import pallas as pl
from jax.experimental.pallas import tpu as pltpu
from jax.sharding import PartitionSpec as P


LANES = 128
FAR = float(1 << 20)
WINDOW = 16
VMEM_LIMIT = 20 << 20
TINY = 16
VMEM = pltpu.VMEM
F32 = jnp.float32


def dot(a, b, contract):
    return lax.dot_general(
        a, b, ((contract[:1], contract[1:]), ((), ())), preferred_element_type=F32
    )


def halves(a):
    high = a.astype(jnp.bfloat16)
    return high, (a - high.astype(F32)).astype(jnp.bfloat16)


def pick(a, onehot, contract):
    high, low = halves(a)
    return dot(high, onehot, contract) + dot(low, onehot, contract)


def edge_masks(shape):
    row = lax.broadcasted_iota(jnp.int32, shape, 0)
    col = lax.broadcasted_iota(jnp.int32, shape, 1)
    return row > 0, row < shape[0] - 1, col > 0, col < shape[1] - 1


def plane_weights(vel, masks):
    low_x, high_x, low_y, high_y = masks
    xp = jnp.where(high_x, vel, 0.0)
    xm = jnp.where(low_x, pltpu.roll(vel, 1, 0), 0.0)
    yp = jnp.where(high_y, vel, 0.0)
    ym = jnp.where(low_y, pltpu.roll(vel, 1, 1), 0.0)
    return xp, xm, yp, ym, 2.0 * vel + xm + ym


def plane_part(u, weights):
    xp, xm, yp, ym, centre = weights
    rows, cols = u.shape
    return (
        xp * pltpu.roll(u, rows - 1, 0) + xm * pltpu.roll(u, 1, 0)
        + yp * pltpu.roll(u, cols - 1, 1) + ym * pltpu.roll(u, 1, 1)
        - centre * u
    )


def pick_columns(cols, width):
    return (lax.broadcasted_iota(jnp.int32, (width, cols.shape[1]), 0) == cols).astype(jnp.bfloat16)


def pick_rows(rows, count):
    return (lax.broadcasted_iota(jnp.int32, (count, rows.shape[1]), 0) == rows).astype(F32)


def split_cells(cells, width_x, width_y):
    plane = lax.div(cells, width_x * width_y)
    row = lax.div(cells, width_y)
    return plane, row, row - plane * width_x, cells - row * width_y


def in_lanes(pieces, width, fill=0.0):
    parts = []
    for piece in pieces:
        parts.append(piece)
        if piece.shape[1] < width:
            parts.append(jnp.full((1, width - piece.shape[1]), fill, piece.dtype))
    used = width * len(pieces)
    parts.append(jnp.full((1, LANES - used), fill, pieces[0].dtype))
    return jnp.concatenate(parts, axis=1)


def live_lanes(rec_live, slots, capsules):
    slot = lax.div(lax.broadcasted_iota(jnp.int32, (1, LANES), 1), capsules)
    row = jnp.zeros((1, LANES), F32)
    for r in range(slots):
        row = jnp.where(slot == r, rec_live[r].astype(F32), row)
    return row


def cell_lanes(rec_cells):
    slots, capsules = rec_cells.shape
    return in_lanes([rec_cells[r : r + 1, :] for r in range(slots)], capsules, int(FAR))


def goal_lanes(target, s, n, capsules):
    return in_lanes([target[r, s, n : n + 1, :] for r in range(target.shape[0])], capsules)


def edge_kernel(
    core_ref, live_h, cells_h, target_h, p0_h, adj_h, density_h, speed_h, admittance_h, mask_h,
    face, sent, fields, density, speed, admittance, mask, vel_s, pd_s, stack,
    both, rec_live, rec_cells, target, sems, small_sems,
):
    p0, adj = fields.at[0], fields.at[1]
    shots, depth, width_x, width_y = p0.shape
    slots, capsules = rec_cells.shape
    half = depth // 2
    last = depth - 1
    copies = []
    for side in range(2):
        some = pl.ds(side * half, half)
        pairs = [(h.at[some], v.at[some]) for h, v in (
            (density_h, density), (speed_h, speed), (admittance_h, admittance), (mask_h, mask))]
        pairs.insert(0, (p0_h.at[:, some], p0.at[:, some]))
        outmost = pl.ds(side * last, 1)
        pairs.append((adj_h.at[:, outmost], adj.at[:, outmost]))
        copies.append([
            pltpu.make_async_copy(a, b, sems.at[side, k]) for k, (a, b) in enumerate(pairs)
        ])
    inside = pl.ds(1, depth - 2)
    rest = pltpu.make_async_copy(adj_h.at[:, inside], adj.at[:, inside], small_sems.at[3])
    smalls = [
        pltpu.make_async_copy(a, b, small_sems.at[k])
        for k, (a, b) in enumerate(((live_h, rec_live), (cells_h, rec_cells), (target_h, target)))
    ]
    for copy in smalls + copies[0] + copies[1] + [rest]:
        copy.start()
    masks = edge_masks((width_x, width_y))
    for copy in smalls:
        copy.wait()
    plane, _, row_x, col = split_cells(cell_lanes(rec_cells), width_x, width_y)
    live = live_lanes(rec_live, slots, capsules)
    columns = pick_columns(col, width_y)
    rows = pick_rows(row_x, width_x)
    for side in range(2):
        for copy in copies[side]:
            copy.wait()
        out = both.at[side]
        if side == 0:
            planes, lowest = (0, 1, 2), 0
        else:
            planes, lowest = (last, last - 1, last - 2), half
        near, far, third = planes
        span = range(lowest, lowest + half)
        weights, pres, damp = {}, {}, {}
        for z in span:
            vel_s[z] = 0.5 / density[z]
        for z in planes:
            spd = speed[z]
            pres[z] = 0.5 * density[z] * spd * spd
            damp[z] = 1.0 - admittance[z] * mask[z].astype(F32)
            weights[z] = plane_weights(vel_s[z], masks)
        for z in (near, far):
            pd_s[z] = pres[z] * damp[z]
        wall_low = min(near, far)
        base = side * 7 * width_x

        def put(k, value):
            stack[base + k * width_x : base + (k + 1) * width_x, :] = value

        for s in range(shots):
            first = {}
            for z in planes:
                here = p0[s, z]
                total = plane_part(here, weights[z])
                if z + 1 in span:
                    total += vel_s[z] * (p0[s, z + 1] - here)
                if z - 1 in span:
                    total -= vel_s[z - 1] * (here - p0[s, z - 1])
                first[z] = damp[z] * (here + pres[z] * total)
            out[s * width_x : (s + 1) * width_x, :] = p0[s, near]
            out[(2 + s) * width_x : (3 + s) * width_x, :] = first[near]
            out[(4 + s) * width_x : (5 + s) * width_x, :] = pd_s[near] * adj[s, near]
            q_far = p0[s, far] + first[far]
            q_third = p0[s, third] + first[third]
            beyond = vel_s[min(far, third)]
            total = plane_part(q_far, weights[far]) + beyond * (q_third - q_far)
            total -= vel_s[wall_low] * q_far
            put(s, pd_s[near] * vel_s[wall_low] * q_far)
            put(4 + s, damp[far] * first[far] + pd_s[far] * total)
        out[6 * width_x : 7 * width_x, :] = vel_s[near]
        out[7 * width_x : 8 * width_x, :] = pd_s[near]
        put(2, damp[near])
        put(3, pd_s[near] * vel_s[wall_low])
        put(6, pd_s[far] * vel_s[wall_low])
        found = pick(stack[base : base + 7 * width_x, :], columns, (1, 0))
        is_near = (plane == near).astype(F32)
        is_far = (plane == far).astype(F32)

        def got(k):
            return jnp.sum(found[k * width_x : (k + 1) * width_x, :] * rows, axis=0, keepdims=True)

        tiny = [is_near * got(s) + is_far * got(4 + s) for s in range(shots)]
        tiny += [
            is_near * got(2), is_far * got(6) - is_near * got(3), is_near,
            row_x.astype(F32), col.astype(F32), live,
        ]
        tiny += [live * goal_lanes(target, s, n, capsules) for n in (1, 0) for s in range(shots)]
        tiny.append(cell_lanes(rec_cells).astype(F32))
        tiny.append(jnp.zeros((TINY - len(tiny), LANES), F32))
        start = 8 * width_x
        out[start : start + TINY, :] = jnp.zeros((TINY, width_y), F32)
        out[start : start + TINY, 0:LANES] = jnp.concatenate(tiny, axis=0)
    core = core_ref[0]
    moves = [
        pltpu.make_async_copy(both.at[core], face.at[pl.ds(0, both.shape[1])], small_sems.at[4]),
        pltpu.make_async_copy(both.at[1 - core], sent, small_sems.at[5]),
    ]
    for copy in moves:
        copy.start()
    for copy in [*moves, rest]:
        copy.wait()


def pack_kernel(got, face_in, face, sems):
    planes = got.shape[0] - TINY
    width_x = planes // 8
    second = got.shape[0]
    copies = [
        pltpu.make_async_copy(
            got.at[pl.ds(0, 6 * width_x)], face.at[pl.ds(second, 6 * width_x)], sems.at[0]
        ),
        pltpu.make_async_copy(
            got.at[pl.ds(planes, TINY)], face.at[pl.ds(second + 6 * width_x, TINY)], sems.at[1]
        ),
    ]
    for copy in copies:
        copy.start()
    for copy in copies:
        copy.wait()


def middle_kernel(
    capsules, core_ref, message, encoder, others, fields,
    density, speed, admittance, mask,
    b1, b2, vel_s, pres_s, damp_s, pd_s, back_e, grad, rows_out, code_high, code_low, corners,
    q_s, w_s,
):
    _, pair, depth, width_x, width_y = fields.shape
    shots = 2 * pair
    slots, steps, channels = corners.shape[0], 2, encoder.shape[1]
    masks = edge_masks((width_x, width_y))
    core = core_ref[0]
    half = depth // 2

    def plane_at(d):
        return d + core * (depth - 1 - 2 * d)

    def coupling(d):
        return vel_s[d + core * (depth - 2 - 2 * d)]

    def value_of(kind, s, z):
        return (others if s < pair else fields)[kind, s % pair, z]

    for z in range(depth):
        dens = density[z]
        spd = speed[z]
        pres = 0.5 * dens * spd * spd
        damp = 1.0 - admittance[z] * mask[z].astype(F32)
        vel_s[z] = 0.5 / dens
        pres_s[z] = pres
        damp_s[z] = damp
        pd_s[z] = pres * damp
    for d in range(depth - 1):
        z = plane_at(d)
        w = plane_weights(vel_s[z], masks)
        inwards, outwards = coupling(d), coupling(d - 1) if d > 0 else None
        for s in range(shots):
            here = value_of(0, s, z)
            total = plane_part(here, w) + inwards * (value_of(0, s, plane_at(d + 1)) - here)
            if d > 0:
                total += outwards * (value_of(0, s, plane_at(d - 1)) - here)
            value = here + pres_s[z] * total
            b1[s, z] = value
            q_s[s, d] = here + damp_s[z] * value
            if d <= half:
                w_s[s, d] = pd_s[z] * value_of(1, s, z)
    for d in range(depth - 2):
        z = plane_at(d)
        w = plane_weights(vel_s[z], masks)
        inwards, outwards = coupling(d), coupling(d - 1) if d > 0 else None
        sums = jnp.zeros((width_x, width_y), F32)
        for s in range(shots):
            here = q_s[s, d]
            total = plane_part(here, w) + inwards * (q_s[s, d + 1] - here)
            if d > 0:
                total += outwards * (q_s[s, d - 1] - here)
            value = damp_s[z] * b1[s, z] + pres_s[z] * total
            b2[s, z] = value
            if d >= half:
                continue
            weighted, start = w_s[s, d], value_of(1, s, z)
            back = plane_part(weighted, w) + inwards * (w_s[s, d + 1] - weighted)
            if d > 0:
                back += outwards * (w_s[s, d - 1] - weighted)
            back += damp_s[z] * start
            if d < 2:
                back_e[s, d] = back
            else:
                sums += value * start + b1[s, z] * back
        if d < half:
            grad[z] = -(mask[z].astype(F32) * sums)
        else:
            grad[z] = sums
    grad[plane_at(depth - 2)] = jnp.zeros((width_x, width_y), F32)
    lane = lax.broadcasted_iota(jnp.int32, (LANES, LANES), 1)
    line = lax.broadcasted_iota(jnp.int32, (LANES, LANES), 0)
    same = (lax.div(lane, capsules) == lax.div(line, capsules)) & (line < slots * capsules)
    code = jnp.concatenate([encoder[...], jnp.zeros((capsules, capsules - channels), F32)], axis=1)
    code = jnp.concatenate([code] * (LANES // capsules), axis=1)
    code = jnp.where(same, jnp.concatenate([code] * (LANES // capsules), axis=0), 0.0)
    square = lax.dot_general(
        code, code, (((1,), (1,)), ((), ())),
        precision=lax.Precision.HIGHEST, preferred_element_type=F32,
    )
    both = jnp.concatenate([code, square], axis=1)
    code_high[...], code_low[...] = halves(both)
    own = message[8 * width_x : 8 * width_x + TINY, 0:LANES]
    start = message.shape[0] - TINY
    other = message[start : start + TINY, 0:LANES]
    goal = []
    for n in range(steps):
        first = 10 if n == 0 else 8
        goal += [tiny[first : first + pair, :] for tiny in (other, own)]
    cells = own[12:13, :]
    slot_of = lax.div(lax.broadcasted_iota(jnp.int32, (1, LANES), 1), capsules)
    for r in range(slots):
        corners[r] = jnp.min(jnp.where(slot_of == r, cells, FAR)).astype(jnp.int32)
    goal = jnp.concatenate(goal, axis=0)
    rows_out[0:8, :] = lax.dot_general(
        goal, code, (((1,), (1,)), ((), ())),
        precision=lax.Precision.HIGHEST, preferred_element_type=F32,
    )
    rows_out[8:16, :] = jnp.concatenate(
        [cells, own[7:8, :], jnp.zeros((6, LANES), F32)], axis=0
    )


def window_part(u, vel, masks):
    low_x, high_x, low_y, high_y = masks
    rows, cols = u.shape
    flow_x = vel * (jnp.where(high_x, pltpu.roll(u, rows - 1, 0), 0.0) - u)
    flow_y = vel * (jnp.where(high_y, pltpu.roll(u, cols - 1, 1), 0.0) - u)
    fall_x = flow_x - jnp.where(low_x, pltpu.roll(flow_x, 1, 0), 0.0)
    return fall_x + flow_y - jnp.where(low_y, pltpu.roll(flow_y, 1, 1), 0.0)


def last_kernel(
    capsules, core_ref, corners, halo, others, fields, mask, vel_s, pres_s, damp_s, pd_s, back_e,
    rows_in, code_high, code_low, b1_in, b2_in, grad_in,
    out, coded, coded_other, b1, b2, grad,
    halo_s, stack, spread,
):
    _, pair, depth, width_x, width_y = fields.shape
    shots = 2 * pair
    slots = corners.shape[0]
    masks = edge_masks((width_x, width_y))
    core = core_ref[0]
    half = depth // 2
    last = depth - 1
    edge, inner = core * last, 1 + core * (last - 2)
    second = 8 * width_x + TINY

    def value_of(kind, s, z):
        return (others if s < pair else fields)[kind, s % pair, z]

    def face(k, s):
        start = (second if s >= pair else 0) + (k + s % pair) * width_x
        return halo[start : start + width_x, :]

    def rows_of(array, k, count):
        return array[k * count : (k + 1) * count, :]

    vel_h, pd_h = rows_of(halo, 6, width_x), rows_of(halo, 7, width_x)
    vel_b = jnp.where(core == 0, vel_h, vel_s[last])
    vel_in = vel_s[core * (depth - 2)]
    w_h = plane_weights(vel_h, masks)
    w_e = plane_weights(vel_s[edge], masks)
    for s in range(shots):
        here, beyond = value_of(0, s, edge), face(0, s)
        step = vel_b * (here - beyond)
        p1_h = face(2, s) + pd_h * step
        q_h = beyond + p1_h
        fixed = b1[s, edge] - pres_s[edge] * step
        change = -(pd_s[edge] * step)
        step2 = vel_b * (here + damp_s[edge] * fixed - q_h)
        halo_s[s * width_x : (s + 1) * width_x, :] = p1_h
        halo_s[(shots + s) * width_x : (shots + s + 1) * width_x, :] = q_h
        halo_s[(2 * shots + s) * width_x : (2 * shots + s + 1) * width_x, :] = pd_h * (
            plane_part(q_h, w_h) + step2
        )
        b1[s, edge] = fixed
        total = plane_part(change, w_e) - vel_in * change - step2
        b2[s, edge] = b2[s, edge] + change + pres_s[edge] * total
        b2[s, inner] = b2[s, inner] + pres_s[inner] * (vel_in * change)

    places = []
    low, high = 2 * core, 4 + 2 * core
    for r in range(slots):
        z0 = jnp.clip(lax.div(corners[r], width_x * width_y), low, high)
        x0 = lax.rem(lax.div(corners[r], width_y), width_x)
        start = jnp.minimum(lax.div(jnp.maximum(x0 - 1, 0), 8) * 8, width_x - WINDOW)
        places.append((z0, pl.multiple_of(start, 8)))
    _, row, _, col = split_cells(rows_in[8:9, :].astype(jnp.int32), width_x, width_y)
    live = rows_in[9:10, :]
    columns = pick_columns(col, width_y)
    slot_of = lax.div(lax.broadcasted_iota(jnp.int32, (1, LANES), 1), capsules)
    line = lax.broadcasted_iota(jnp.int32, (WINDOW, LANES), 0)
    mine = jnp.zeros((1, LANES), F32)
    found_rows = {}
    for r, (z0, start) in enumerate(places):
        own = jnp.where(slot_of == r, row, -1)
        upper = jnp.where(lax.div(corners[r], width_x * width_y) >= half, 1, 0)
        mine = jnp.where(slot_of == r, jnp.where(upper == core, 1.0, 0.0), mine)
        for dz in range(2):
            first_row = (z0 + dz) * width_x + start
            found_rows[r, dz] = (line + first_row == own).astype(F32)
    index = {}
    for n, field in enumerate((b1, b2)):
        for r, (z0, start) in enumerate(places):
            for dz in range(2):
                damp = damp_s[z0 + dz, pl.ds(start, WINDOW), :]
                for s in range(shots):
                    k = index[n, r, dz, s] = len(index)
                    stack[k * WINDOW : (k + 1) * WINDOW, :] = (
                        damp * field[s, z0 + dz, pl.ds(start, WINDOW), :]
                    )
    found = pick(stack[...], columns, (1, 0))
    blank = jnp.zeros((1, LANES), F32)
    lines, goals = [], []
    for n in range(2):
        for s in range(shots):
            total = jnp.zeros((WINDOW, LANES), F32)
            for key, picked in found_rows.items():
                total += picked * rows_of(found, index[(n, *key, s)], WINDOW)
            lines.append(jnp.sum(total, axis=0, keepdims=True))
    start = 8 * width_x
    tiny = halo[start : start + TINY, 0:LANES]
    start = second + 6 * width_x
    tiny_second = halo[start : start + TINY, 0:LANES]
    near = tiny[4:5, :]
    picked = pick_rows(tiny[5:6, :].astype(jnp.int32), width_x).astype(F32)
    columns_h = pick_columns(tiny[6:7, :].astype(jnp.int32), width_y)
    rows_h = picked * near
    found = pick(halo_s[...], columns_h, (1, 0))
    for s in range(shots):
        own_tiny = tiny if s < pair else tiny_second
        total = picked * (
            tiny[2:3, :] * rows_of(found, s, width_x)
            + tiny[3:4, :] * rows_of(found, shots + s, width_x)
            + near * rows_of(found, 2 * shots + s, width_x)
        )
        k = s % pair
        lines.append(own_tiny[k : k + 1, :] + jnp.sum(total, axis=0, keepdims=True))
        goals.append(own_tiny[8 + k : 9 + k, :])
    lines += [blank] * 4
    goal_high, goal_low = halves(jnp.concatenate(goals + [blank] * 4, axis=0))
    high, low = code_high[:, 0:LANES], code_low[:, 0:LANES]
    known = jnp.concatenate([
        rows_in[0:8, :],
        dot(goal_high, high, (1, 1)) + dot(goal_low, high, (1, 1)) + dot(goal_high, low, (1, 1)),
    ], axis=0)
    got_high, got_low = halves(jnp.concatenate(lines, axis=0))
    both = (
        dot(got_high, code_high[...], (1, 0)) + dot(got_low, code_high[...], (1, 0))
        + dot(got_high, code_low[...], (1, 0))
    )
    lives = jnp.concatenate([live] * 8 + [tiny[7:8, :]] * 8, axis=0)
    signals = both[0:8, 0:LANES] * (live * mine)
    for ref, first in ((coded_other, 0), (coded, pair)):
        ref[...] = jnp.zeros(ref.shape, F32)
        for n in range(2):
            ref[n * pair : (n + 1) * pair, 0:LANES] = (
                signals[n * shots + first : n * shots + first + pair, :]
            )
    source = both[:, LANES:] * lives - known

    parts = [None] * len(index)
    for (n, r, dz, s), k in index.items():
        line_of = n * shots + s
        parts[k] = found_rows[r, dz] * source[line_of : line_of + 1, :]
    spread[...] = pick(jnp.concatenate(parts, axis=0), columns, (1, 1))
    lines = [rows_h * source[8 + s : 9 + s, :] for s in range(shots)]
    placed = pick(jnp.concatenate(lines, axis=0), columns_h, (1, 1))
    sums = jnp.zeros((width_x, width_y), F32)
    sums_in = jnp.zeros((width_x, width_y), F32)
    for s in range(shots):
        weighted = face(4, s) + pd_h * rows_of(placed, s, width_x)
        start = value_of(1, s, edge)
        back = back_e[s, 0] - vel_b * (pd_s[edge] * start - weighted)
        sums += b2[s, edge] * start + b1[s, edge] * back
        sums_in += b2[s, inner] * value_of(1, s, inner) + b1[s, inner] * back_e[s, 1]
    grad[edge] = -(mask[edge].astype(F32) * sums)
    grad[inner] = -(mask[inner].astype(F32) * sums_in)

    near_masks = edge_masks((WINDOW, width_y))
    for r, (z0, start) in enumerate(places):
        window = pl.ds(start, WINDOW)
        lower, upper = jnp.maximum(z0 - 1, 0), jnp.minimum(z0 + 2, last)
        vel_low = jnp.where(
            z0 > 0, vel_s[lower, window, :], halo[pl.ds(6 * width_x + start, WINDOW), :]
        )
        vel = [vel_s[z0 + dz, window, :] for dz in range(2)]
        sums = [jnp.zeros((WINDOW, width_y), F32) for _ in range(4)]
        for s in range(shots):
            now, before = [
                [rows_of(spread, index[n, r, dz, s], WINDOW) for dz in range(2)] for n in (1, 0)
            ]
            w = [pd_s[z0 + dz, window, :] * now[dz] for dz in range(2)]
            between = vel[0] * (w[1] - w[0])
            outer = [vel_low * w[0], vel[1] * w[1]]
            for dz in range(2):
                total = window_part(w[dz], vel[dz], near_masks) - outer[dz]
                total += between if dz == 0 else -between
                total += damp_s[z0 + dz, window, :] * now[dz] + before[dz]
                sums[1 + dz] += (
                    b2[s, z0 + dz, window, :] * now[dz] + b1[s, z0 + dz, window, :] * total
                )
            sums[0] += b1[s, lower, window, :] * outer[0]
            sums[3] += b1[s, upper, window, :] * outer[1]
        inside = (jnp.where(z0 > 0, 1.0, 0.0), 1.0, 1.0, jnp.where(z0 + 2 < depth, 1.0, 0.0))
        for z, total, factor in zip((lower, z0, z0 + 1, upper), sums, inside):
            wall = mask[z, window, :].astype(F32)
            grad[z, window, :] = grad[z, window, :] - factor * (wall * total)
    for z in range(half):
        out[z * width_x : (z + 1) * width_x, :] = grad[core * half + z]


def join_kernel(core, mine, other, coded, out, signals, signals_s, sems):
    half = mine.shape[0]
    start = core[0] * half
    slots, shots, steps, channels = signals_s.shape
    copies = [
        pltpu.make_async_copy(mine, out.at[pl.ds(start, half)], sems.at[0]),
        pltpu.make_async_copy(
            other.at[pl.ds(0, half)], out.at[pl.ds(half - start, half)], sems.at[1]
        ),
    ]
    for copy in copies:
        copy.start()
    total = coded[...] + other[half : half + 8, :]
    for r in range(slots):
        for s in range(shots):
            for n in range(steps):
                line = n * shots + s
                signals_s[r, s, n : n + 1, :] = total[line : line + 1, r * 32 : r * 32 + channels]
    copies.append(pltpu.make_async_copy(signals_s, signals, sems.at[2]))
    copies[-1].start()
    for copy in copies:
        copy.wait()


def body(
    pressure_init, adjoint_init, density, speed, admittance, bound_mask,
    rec_cells, rec_live, encoder, target,
):
    shots, depth, width_x, width_y = pressure_init.shape
    slots, capsules = rec_cells.shape
    steps, channels = target.shape[2:]
    slabs, peers = lax.axis_size("slab"), lax.axis_size("shot")
    field = (shots, depth, width_x, width_y)
    slab = (depth, width_x, width_y)
    message = (8 * width_x + TINY, width_y)

    def ins(count, scalars=0, far=0):
        kinds = [pltpu.SMEM] * scalars + [VMEM] * (count - scalars - far) + [pltpu.HBM] * far
        return [pl.BlockSpec(memory_space=kind) for kind in kinds]

    def outs(*shapes):
        return [
            shape if isinstance(shape, jax.ShapeDtypeStruct) else jax.ShapeDtypeStruct(shape, F32)
            for shape in shapes
        ]

    params = pltpu.CompilerParams(vmem_limit_bytes=VMEM_LIMIT)
    core = lax.rem(lax.axis_index("shot"), 2)
    longer = (message[0] + 6 * width_x + TINY, width_y)
    face, sent, fields, density, speed, admittance, bound_mask = pl.pallas_call(
        edge_kernel,
        in_specs=ins(10, 1, 9),
        out_specs=ins(7),
        out_shape=[
            VMEM(longer, F32), VMEM(message, F32), VMEM((2, *field), F32),
            VMEM(slab, F32), VMEM(slab, F32), VMEM(slab, F32), VMEM(slab, jnp.int32),
        ],
        scratch_shapes=[
            VMEM(slab, F32), VMEM(slab, F32), VMEM((14 * width_x, width_y), F32),
            VMEM((2, *message), F32),
            pltpu.SMEM(rec_live.shape, jnp.int32), VMEM(rec_cells.shape, jnp.int32),
            VMEM(target.shape, F32),
            pltpu.SemaphoreType.DMA((2, 6)), pltpu.SemaphoreType.DMA((6,)),
        ],
        compiler_params=params,
        name="edge",
    )(
        core[None],
        *[
            pltpu.with_memory_space_constraint(array, pltpu.HBM)
            for array in (
                rec_live, rec_cells, target,
                pressure_init, adjoint_init, density, speed, admittance, bound_mask,
            )
        ],
    )

    pairs = [(i, i ^ 1) for i in range(peers)]
    facing = []
    for i in range(slabs - 1):
        for j in range(0, peers, 2):
            ends = (i * peers + j + 1, (i + 1) * peers + j)
            facing += [ends, ends[::-1]]
    got = lax.ppermute(sent, "shot", pairs)
    others = lax.ppermute(fields, "shot", pairs)
    face = pl.pallas_call(
        pack_kernel,
        in_specs=ins(2),
        out_specs=pl.BlockSpec(memory_space=VMEM),
        out_shape=VMEM(longer, F32),
        scratch_shapes=[pltpu.SemaphoreType.DMA((2,))],
        input_output_aliases={1: 0},
        compiler_params=params,
        name="pack",
    )(got, face)
    halo = lax.ppermute(face, ("slab", "shot"), facing)

    table = jax.ShapeDtypeStruct((LANES, 2 * LANES), jnp.bfloat16)
    four = (2 * shots, *slab)
    rows_plane = (width_x, width_y)
    b1, b2, vel, pres, damp, pd, back, grad, rows, high, low, corners = pl.pallas_call(
        functools.partial(middle_kernel, capsules),
        in_specs=ins(9, 1),
        out_specs=[*ins(11), *ins(1, 1)],
        out_shape=outs(
            four, four, slab, slab, slab, slab, (2 * shots, 2, *rows_plane), slab,
            (16, LANES), table, table, jax.ShapeDtypeStruct((slots,), jnp.int32),
        ),
        scratch_shapes=[
            VMEM((2 * shots, depth - 1, *rows_plane), F32),
            VMEM((2 * shots, depth // 2 + 1, *rows_plane), F32),
        ],
        compiler_params=params,
        cost_estimate=pl.CostEstimate(flops=30_000_000, bytes_accessed=9_000_000, transcendentals=0),
        name="middle",
    )(
        core[None], face, encoder, others, fields, density, speed, admittance, bound_mask,
    )

    windows = steps * slots * 2 * 2 * shots * WINDOW
    half = (depth // 2 * width_x, width_y)
    line = (8, width_y)
    total, coded, coded_other, _, _, _ = pl.pallas_call(
        functools.partial(last_kernel, capsules),
        in_specs=ins(17, 2),
        out_specs=ins(6),
        out_shape=outs(half, line, line, four, four, slab),
        scratch_shapes=[
            VMEM((6 * shots * width_x, width_y), F32), VMEM((windows, width_y), F32),
            VMEM((windows, width_y), F32),
        ],
        input_output_aliases={14: 3, 15: 4, 16: 5},
        compiler_params=params,
        name="last",
    )(
        core[None], corners, halo, others, fields, bound_mask, vel, pres, damp, pd, back,
        rows, high, low, b1, b2, grad,
    )

    groups = [list(range(c, peers, 2)) for c in range(2)]
    copies = jnp.broadcast_to(total, (peers // 2, *half))
    total = lax.all_to_all(
        copies, "shot", split_axis=0, concat_axis=0, tiled=True, axis_index_groups=groups
    ).reshape(peers // 2, *half).sum(axis=0)
    total, coded, coded_other, later = lax.optimization_barrier((total, coded, coded_other, core))
    other = lax.ppermute(jnp.concatenate([total, coded_other], axis=0), "shot", pairs)
    gradient, recording = pl.pallas_call(
        join_kernel,
        in_specs=ins(4, 1),
        out_specs=[pl.BlockSpec(memory_space=pltpu.HBM)] * 2,
        out_shape=[
            pltpu.HBM((depth * width_x, width_y), F32),
            pltpu.HBM((slots, shots, steps, channels), F32),
        ],
        scratch_shapes=[
            VMEM((slots, shots, steps, channels), F32), pltpu.SemaphoreType.DMA((3,)),
        ],
        compiler_params=params,
        name="join",
    )(later[None], total, other, coded)
    return recording, gradient.reshape(slab)


def solution(mesh):
    placed = (
        P("shot", "slab", None, None), P("shot", "slab", None, None),
        P("slab", None, None), P("slab", None, None), P("slab", None, None), P("slab", None, None),
        P("slab", None), P("slab"), P(), P("slab", "shot", None, None),
    )
    return jax.shard_map(
        body, mesh=mesh, in_specs=placed,
        out_specs=(P("slab", "shot", None, None), P("slab", None, None)),
        check_vma=False,
    )
```

time: 43.9 us -> 41.9 us (0.954)
  the two profiles are of different devices: /device:TPU:385 before, /device:TPU:1 now
where the time goes in v5:
time: 41.9 us; the launch traced here: 41.6 us
  starting transfers between devices  14.5 us (35%)
  blocking collectives  9.33 us (22%)
  Pallas kernels  8.85 us (21%)
  waiting for transfers between devices  8.12 us (19%)
  between operations  0.74 us (2%)
    all_to_all x1, blocking collectives, body(): lax.all_to_all(copies, 'shot', split_axis=0, concat_axis=0, tiled=True, a...  9.33 us
    ppermute x1, starting transfers between devices, body(): others = lax.ppermute(fields, 'shot', pairs)  8.75 us
    ppermute x1, waiting for transfers between devices, body(): halo = lax.ppermute(face, ('slab', 'shot'), facing)  5.27 us
    pallas_call x1, Pallas kernels, body(): pl.pallas_call(functools.partial(middle_kernel, capsules), in_specs=ins(9...  2.92 us
    pallas_call x1, Pallas kernels, body(): pl.pallas_call(functools.partial(last_kernel, capsules), in_specs=ins(17,...  2.47 us
    pallas_call x1, Pallas kernels, body(): pl.pallas_call(edge_kernel, in_specs=ins(10, 1, 9), out_specs=ins(7), out...  2.46 us
    ppermute x1, starting transfers between devices, body(): lax.ppermute(jnp.concatenate([total, coded_other], axis=0), 'shot', pairs)  1.92 us
    ppermute x1, starting transfers between devices, body(): got = lax.ppermute(sent, 'shot', pairs)  1.92 us
  transfers between devices with their start and end apart: 4, of which 3 were waited for; matrix products, arithmetic and copies ran while one was open for 0% of the time, Pallas kernels for 8%

profile of v5, /device:TPU:1, one launch (start us, length us, event | category | flops | bytes accessed | tf_op | source)
XLA Modules:
  0.0 41.6 jit_solution(424907379685921698)
XLA Ops:
  0.6 2.5 %edge.1 = (f32[480,256]{1,0:T(8,128)S(1)}, f32[272,256]{1,0:T(8,128)S(1)}, f32[2,2,8,32,256]{4,3,2,1,0:T(8,128)S(1)}, f32[8,32,256]{2,1,0:T(8,128)S(1)}, f32[8,3...) custom-call(s32[1]{0:T(128)} %bitcast.core_ref, s32[3]{0:T(128)} %live_h.1, ...), custom_call_target="tpu_custom_call" | custom-call | tf_op jit(solution)/shard_map/edge/pallas_call | solution.py:582
  3.1 8.7 %collective-permute-start.1 = (f32[2,2,8,32,256]{4,3,2,1,0:T(8,128)S(1)}, f32[2,2,8,32,256]{4,3,2,1,0:T(8,128)S(1)}, u32[]{:S(2)}, u32[]{:S(2)}) collective-permute-start(f32[2,2,8,32,256]{4,3,2,1,0:T(8,128)S(1)} %get-tuple-element.32.fields), channel_id=1, source_target_pairs={{0,1},{1,0},{2,3},{3,2},{4,5},{5,4},{6,7},{7,6},{8,9},{9,8},{10,11... | collective-permute-start | bytes 3145736 | tf_op jit(solution)/shard_map/ppermute | solution.py:617
  11.9 1.9 %collective-permute-start = (f32[272,256]{1,0:T(8,128)S(1)}, f32[272,256]{1,0:T(8,128)S(1)}, u32[]{:S(2)}, u32[]{:S(2)}) collective-permute-start(f32[272,256]{1,0:T(8,128)S(1)} %get-tuple-element.30), channel_id=1, source_target_pairs={{0,1},{1,0},{2,3},{3,2},{4,5},{5,4},{6,7},{7,6},{8,9},{9,8},{10,11... | collective-permute-start | bytes 835592 | tf_op jit(solution)/shard_map/ppermute | solution.py:616
  13.8 1.5 %collective-permute-done.got = f32[272,256]{1,0:T(8,128)S(1)} collective-permute-done((f32[272,256]{1,0:T(8,128)S(1)}, f32[272,256]{1,0:T(8,128)S(1)}, u32[]{:S(2)}, u32[]{:S(2)}) %collective-permute-start) | collective-permute-done | bytes 278560 | tf_op jit(solution)/shard_map/ppermute | solution.py:616
  15.3 0.0 copy-start
  15.3 0.3 pack.1.message
  15.6 1.9 %collective-permute-start.2 = (f32[480,256]{1,0:T(8,128)S(1)}, f32[480,256]{1,0:T(8,128)S(1)}, u32[]{:S(2)}, u32[]{:S(2)}) collective-permute-start(f32[480,256]{1,0:T(8,128)S(1)} %pack.1.message), channel_id=1, source_target_pairs={{1,8},{8,1},{3,10},{10,3},{5,12},{12,5},{7,14},{14,7},{9,16},{16,9... | collective-permute-start | bytes 1474568 | tf_op jit(solution)/shard_map/ppermute | solution.py:628
  17.5 0.0 collective-permute-done.1.others
  17.5 0.0 copy-done
  17.5 2.9 %middle.1 = (f32[4,8,32,256]{3,2,1,0:T(8,128)S(1)}, f32[4,8,32,256]{3,2,1,0:T(8,128)S(1)}, f32[8,32,256]{2,1,0:T(8,128)S(1)}, f32[8,32,256]{2,1,0:T(8,128)S(1)},...) custom-call(s32[1]{0:T(128)} %bitcast.core_ref, ...), custom_call_target="tpu_custom_call" | custom-call | flops 30000000 | bytes 9000000 | tf_op jit(solution)/shard_map/middle/pallas_call | solution.py:633
  20.5 5.3 %collective-permute-done.2.halo = f32[480,256]{1,0:T(8,128)S(1)} collective-permute-done((f32[480,256]{1,0:T(8,128)S(1)}, f32[480,256]{1,0:T(8,128)S(1)}, u32[]{:S(2)}, u32[]{:S(2)}) %collective-permute-start.2) | collective-permute-done | bytes 491552 | tf_op jit(solution)/shard_map/ppermute | solution.py:628
  25.7 2.5 %last.1 = (f32[128,256]{1,0:T(8,128)S(1)}, f32[8,256]{1,0:T(8,128)S(1)}, f32[8,256]{1,0:T(8,128)S(1)}, f32[4,8,32,256]{3,2,1,0:T(8,128)S(1)}, f32[4,8,32,256]{3,2,1,0:T(8,128)S(1)}, /*index=5*/f32[8,32,256]{2,1,0:T(8,128)S(1)}) custom-call(s32[1]{0:T(128)} %bitcast.core_ref, ...), custom_call_target="tpu_custom_call", output_to_operand_aliasing={{3}: (14, {}), {4}: (15, {}), {5}: (16, {})} | custom-call | tf_op jit(solution)/shard_map/last/pallas_call | solution.py:655
  28.3 9.3 %all_to_all.5 = f32[4,128,256]{2,1,0:T(8,128)S(1)} all-to-all(f32[4,128,256]{2,1,0:T(8,128)S(1)} %broadcast_in_dim.12), channel_id=1, replica_groups={{0,2,4,6},{1,3,5,7},{8,10,12,14},{9,11,13,15},{16,18,20,22},{17,19,21,2..., dimensions={0} | all-to-all | bytes 1048576 | tf_op jit(solution)/shard_map/all_to_all | solution.py:674
  37.7 1.9 %collective-permute-start.3 = (f32[136,256]{1,0:T(8,128)S(1)}, f32[136,256]{1,0:T(8,128)S(1)}, u32[]{:S(2)}, u32[]{:S(2)}) collective-permute-start(f32[136,256]{1,0:T(8,128)S(1)} %pad_maximum_fusion), channel_id=1, source_target_pairs={{0,1},{1,0},{2,3},{3,2},{4,5},{5,4},{6,7},{7,6},{8,9},{9,8},{10,11... | collective-permute-start | bytes 417800 | tf_op jit(solution)/shard_map/ppermute | solution.py:678
  39.6 1.3 %collective-permute-done.3.other = f32[136,256]{1,0:T(8,128)S(1)} collective-permute-done((f32[136,256]{1,0:T(8,128)S(1)}, f32[136,256]{1,0:T(8,128)S(1)}, u32[]{:S(2)}, u32[]{:S(2)}) %collective-permute-start.3) | collective-permute-done | bytes 139296 | tf_op jit(solution)/shard_map/ppermute | solution.py:678
  40.9 0.7 %join.1 = (f32[256,256]{1,0:T(8,128)}, f32[3,2,2,25]{3,2,1,0:T(2,128)}) custom-call(s32[1]{0:T(128)} %bitcast.1.core, f32[128,256]{1,0:T(8,128)S(1)} %reduce_sum.9.mine, f32[136,256]{1,0:T(8,128)S(1)} %collective-permute-done.3.other, f32[8,256]{1,0:T(8,128)S(1)} %get-tuple-element.55.coded), custom_call_target="tpu_custom_call" | custom-call | tf_op jit(solution)/shard_map/join/pallas_call | solution.py:679
  (3 shorter events, 0.1 us)
Async XLA Ops:
  3.1 14.4 %collective-permute-start.1 = (f32[2,2,8,32,256]{4,3,2,1,0:T(8,128)S(1)}, f32[2,2,8,32,256]{4,3,2,1,0:T(8,128)S(1)}, u32[]{:S(2)}, u32[]{:S(2)}) collective-permute-start(f32[2,2,8,32,256]{4,3,2,1,0:T(8,128)S(1)} %get-tuple-element.32.fields), channel_id=1, source_target_pairs={{0,1},{1,0},{2,3},{3,2},{4,5},{5,4},{6,7},{7,6},{8,9},{9,8},{10,11... | collective-permute-start | bytes 3145736 | tf_op jit(solution)/shard_map/ppermute | solution.py:617
  11.9 3.5 %collective-permute-start = (f32[272,256]{1,0:T(8,128)S(1)}, f32[272,256]{1,0:T(8,128)S(1)}, u32[]{:S(2)}, u32[]{:S(2)}) collective-permute-start(f32[272,256]{1,0:T(8,128)S(1)} %get-tuple-element.30), channel_id=1, source_target_pairs={{0,1},{1,0},{2,3},{3,2},{4,5},{5,4},{6,7},{7,6},{8,9},{9,8},{10,11... | collective-permute-start | bytes 835592 | tf_op jit(solution)/shard_map/ppermute | solution.py:616
  15.3 2.2 %copy-start = (f32[32,25]{1,0:T(8,128)S(1)}, f32[32,25]{1,0:T(8,128)}, u32[]{:S(2)}) copy-start(f32[32,25]{1,0:T(8,128)} %encoder.1) | copy-start | bytes 9604
  15.6 10.1 %collective-permute-start.2 = (f32[480,256]{1,0:T(8,128)S(1)}, f32[480,256]{1,0:T(8,128)S(1)}, u32[]{:S(2)}, u32[]{:S(2)}) collective-permute-start(f32[480,256]{1,0:T(8,128)S(1)} %pack.1.message), channel_id=1, source_target_pairs={{1,8},{8,1},{3,10},{10,3},{5,12},{12,5},{7,14},{14,7},{9,16},{16,9... | collective-permute-start | bytes 1474568 | tf_op jit(solution)/shard_map/ppermute | solution.py:628
  37.7 3.3 %collective-permute-start.3 = (f32[136,256]{1,0:T(8,128)S(1)}, f32[136,256]{1,0:T(8,128)S(1)}, u32[]{:S(2)}, u32[]{:S(2)}) collective-permute-start(f32[136,256]{1,0:T(8,128)S(1)} %pad_maximum_fusion), channel_id=1, source_target_pairs={{0,1},{1,0},{2,3},{3,2},{4,5},{5,4},{6,7},{7,6},{8,9},{9,8},{10,11... | collective-permute-start | bytes 417800 | tf_op jit(solution)/shard_map/ppermute | solution.py:678

commit v6 on v5

--- a/solution.py
+++ b/solution.py
@@ -28,9 +28,12 @@
     return high, (a - high.astype(F32)).astype(jnp.bfloat16)
 
 
-def pick(a, onehot, contract):
-    high, low = halves(a)
-    return dot(high, onehot, contract) + dot(low, onehot, contract)
+def side_by_side(a):
+    return jnp.concatenate(halves(a), axis=1)
+
+
+def doubled(onehot, axis):
+    return jnp.concatenate([onehot, onehot], axis=axis)
 
 
 def edge_masks(shape):
@@ -134,7 +137,7 @@
         copy.wait()
     plane, _, row_x, col = split_cells(cell_lanes(rec_cells), width_x, width_y)
     live = live_lanes(rec_live, slots, capsules)
-    columns = pick_columns(col, width_y)
+    columns = doubled(pick_columns(col, width_y), 0)
     rows = pick_rows(row_x, width_x)
     for side in range(2):
         for copy in copies[side]:
@@ -160,7 +163,7 @@
         base = side * 7 * width_x
 
         def put(k, value):
-            stack[base + k * width_x : base + (k + 1) * width_x, :] = value
+            stack[base + k * width_x : base + (k + 1) * width_x, :] = side_by_side(value)
 
         for s in range(shots):
             first = {}
@@ -187,7 +190,7 @@
         put(2, damp[near])
         put(3, pd_s[near] * vel_s[wall_low])
         put(6, pd_s[far] * vel_s[wall_low])
-        found = pick(stack[base : base + 7 * width_x, :], columns, (1, 0))
+        found = dot(stack[base : base + 7 * width_x, :], columns, (1, 0))
         is_near = (plane == near).astype(F32)
         is_far = (plane == far).astype(F32)
 
@@ -388,10 +391,10 @@
         fixed = b1[s, edge] - pres_s[edge] * step
         change = -(pd_s[edge] * step)
         step2 = vel_b * (here + damp_s[edge] * fixed - q_h)
-        halo_s[s * width_x : (s + 1) * width_x, :] = p1_h
-        halo_s[(shots + s) * width_x : (shots + s + 1) * width_x, :] = q_h
-        halo_s[(2 * shots + s) * width_x : (2 * shots + s + 1) * width_x, :] = pd_h * (
-            plane_part(q_h, w_h) + step2
+        halo_s[s * width_x : (s + 1) * width_x, :] = side_by_side(p1_h)
+        halo_s[(shots + s) * width_x : (shots + s + 1) * width_x, :] = side_by_side(q_h)
+        halo_s[(2 * shots + s) * width_x : (2 * shots + s + 1) * width_x, :] = side_by_side(
+            pd_h * (plane_part(q_h, w_h) + step2)
         )
         b1[s, edge] = fixed
         total = plane_part(change, w_e) - vel_in * change - step2
@@ -426,10 +429,10 @@
                 damp = damp_s[z0 + dz, pl.ds(start, WINDOW), :]
                 for s in range(shots):
                     k = index[n, r, dz, s] = len(index)
-                    stack[k * WINDOW : (k + 1) * WINDOW, :] = (
+                    stack[k * WINDOW : (k + 1) * WINDOW, :] = side_by_side(
                         damp * field[s, z0 + dz, pl.ds(start, WINDOW), :]
                     )
-    found = pick(stack[...], columns, (1, 0))
+    found = dot(stack[...], doubled(columns, 0), (1, 0))
     blank = jnp.zeros((1, LANES), F32)
     lines, goals = [], []
     for n in range(2):
@@ -446,7 +449,7 @@
     picked = pick_rows(tiny[5:6, :].astype(jnp.int32), width_x).astype(F32)
     columns_h = pick_columns(tiny[6:7, :].astype(jnp.int32), width_y)
     rows_h = picked * near
-    found = pick(halo_s[...], columns_h, (1, 0))
+    found = dot(halo_s[...], doubled(columns_h, 0), (1, 0))
     for s in range(shots):
         own_tiny = tiny if s < pair else tiny_second
         total = picked * (
@@ -482,10 +485,10 @@
     parts = [None] * len(index)
     for (n, r, dz, s), k in index.items():
         line_of = n * shots + s
-        parts[k] = found_rows[r, dz] * source[line_of : line_of + 1, :]
-    spread[...] = pick(jnp.concatenate(parts, axis=0), columns, (1, 1))
-    lines = [rows_h * source[8 + s : 9 + s, :] for s in range(shots)]
-    placed = pick(jnp.concatenate(lines, axis=0), columns_h, (1, 1))
+        parts[k] = side_by_side(found_rows[r, dz] * source[line_of : line_of + 1, :])
+    spread[...] = dot(jnp.concatenate(parts, axis=0), doubled(columns, 1), (1, 1))
+    lines = [side_by_side(rows_h * source[8 + s : 9 + s, :]) for s in range(shots)]
+    placed = dot(jnp.concatenate(lines, axis=0), doubled(columns_h, 1), (1, 1))
     sums = jnp.zeros((width_x, width_y), F32)
     sums_in = jnp.zeros((width_x, width_y), F32)
     for s in range(shots):
@@ -588,7 +591,7 @@
             VMEM(slab, F32), VMEM(slab, F32), VMEM(slab, F32), VMEM(slab, jnp.int32),
         ],
         scratch_shapes=[
-            VMEM(slab, F32), VMEM(slab, F32), VMEM((14 * width_x, width_y), F32),
+            VMEM(slab, F32), VMEM(slab, F32), VMEM((14 * width_x, 2 * width_y), jnp.bfloat16),
             VMEM((2, *message), F32),
             pltpu.SMEM(rec_live.shape, jnp.int32), VMEM(rec_cells.shape, jnp.int32),
             VMEM(target.shape, F32),
@@ -658,8 +661,8 @@
         out_specs=ins(6),
         out_shape=outs(half, line, line, four, four, slab),
         scratch_shapes=[
-            VMEM((6 * shots * width_x, width_y), F32), VMEM((windows, width_y), F32),
-            VMEM((windows, width_y), F32),
+            VMEM((6 * shots * width_x, 2 * width_y), jnp.bfloat16),
+            VMEM((windows, 2 * width_y), jnp.bfloat16), VMEM((windows, width_y), F32),
         ],
         input_output_aliases={14: 3, 15: 4, 16: 5},
         compiler_params=params,

time: 41.9 us -> 41.7 us (level)
  no operation moved by 1% of the time
where the time goes in v6:
time: 41.7 us; the launch traced here: 41.4 us
  starting transfers between devices  14.5 us (35%)
  blocking collectives  9.33 us (22%)
  Pallas kernels  8.66 us (21%)
  waiting for transfers between devices  8.12 us (19%)
  between operations  0.74 us (2%)
    all_to_all x1, blocking collectives, body(): lax.all_to_all(copies, 'shot', split_axis=0, concat_axis=0, tiled=True, a...  9.33 us
    ppermute x1, starting transfers between devices, body(): others = lax.ppermute(fields, 'shot', pairs)  8.75 us
    ppermute x1, waiting for transfers between devices, body(): halo = lax.ppermute(face, ('slab', 'shot'), facing)  5.27 us
    pallas_call x1, Pallas kernels, body(): pl.pallas_call(functools.partial(middle_kernel, capsules), in_specs=ins(9...  2.92 us
    pallas_call x1, Pallas kernels, body(): pl.pallas_call(edge_kernel, in_specs=ins(10, 1, 9), out_specs=ins(7), out...  2.46 us
    pallas_call x1, Pallas kernels, body(): pl.pallas_call(functools.partial(last_kernel, capsules), in_specs=ins(17,...  2.28 us
    ppermute x1, starting transfers between devices, body(): got = lax.ppermute(sent, 'shot', pairs)  1.92 us
    ppermute x1, starting transfers between devices, body(): halo = lax.ppermute(face, ('slab', 'shot'), facing)  1.92 us
  transfers between devices with their start and end apart: 4, of which 3 were waited for; matrix products, arithmetic and copies ran while one was open for 0% of the time, Pallas kernels for 8%

profile of v6, /device:TPU:1, one launch (start us, length us, event | category | flops | bytes accessed | tf_op | source)
XLA Modules:
  0.0 41.4 jit_solution(8058154147533429209)
XLA Ops:
  0.6 2.5 %edge.1 = (f32[480,256]{1,0:T(8,128)S(1)}, f32[272,256]{1,0:T(8,128)S(1)}, f32[2,2,8,32,256]{4,3,2,1,0:T(8,128)S(1)}, f32[8,32,256]{2,1,0:T(8,128)S(1)}, f32[8,3...) custom-call(s32[1]{0:T(128)} %bitcast.core_ref, s32[3]{0:T(128)} %live_h.1, ...), custom_call_target="tpu_custom_call" | custom-call | tf_op jit(solution)/shard_map/edge/pallas_call | solution.py:585
  3.1 8.7 %collective-permute-start.1 = (f32[2,2,8,32,256]{4,3,2,1,0:T(8,128)S(1)}, f32[2,2,8,32,256]{4,3,2,1,0:T(8,128)S(1)}, u32[]{:S(2)}, u32[]{:S(2)}) collective-permute-start(f32[2,2,8,32,256]{4,3,2,1,0:T(8,128)S(1)} %get-tuple-element.32.fields), channel_id=1, source_target_pairs={{0,1},{1,0},{2,3},{3,2},{4,5},{5,4},{6,7},{7,6},{8,9},{9,8},{10,11... | collective-permute-start | bytes 3145736 | tf_op jit(solution)/shard_map/ppermute | solution.py:620
  11.9 1.9 %collective-permute-start = (f32[272,256]{1,0:T(8,128)S(1)}, f32[272,256]{1,0:T(8,128)S(1)}, u32[]{:S(2)}, u32[]{:S(2)}) collective-permute-start(f32[272,256]{1,0:T(8,128)S(1)} %get-tuple-element.30), channel_id=1, source_target_pairs={{0,1},{1,0},{2,3},{3,2},{4,5},{5,4},{6,7},{7,6},{8,9},{9,8},{10,11... | collective-permute-start | bytes 835592 | tf_op jit(solution)/shard_map/ppermute | solution.py:619
  13.8 1.5 %collective-permute-done.got = f32[272,256]{1,0:T(8,128)S(1)} collective-permute-done((f32[272,256]{1,0:T(8,128)S(1)}, f32[272,256]{1,0:T(8,128)S(1)}, u32[]{:S(2)}, u32[]{:S(2)}) %collective-permute-start) | collective-permute-done | bytes 278560 | tf_op jit(solution)/shard_map/ppermute | solution.py:619
  15.3 0.0 copy-start
  15.3 0.3 pack.1.message
  15.6 1.9 %collective-permute-start.2 = (f32[480,256]{1,0:T(8,128)S(1)}, f32[480,256]{1,0:T(8,128)S(1)}, u32[]{:S(2)}, u32[]{:S(2)}) collective-permute-start(f32[480,256]{1,0:T(8,128)S(1)} %pack.1.message), channel_id=1, source_target_pairs={{1,8},{8,1},{3,10},{10,3},{5,12},{12,5},{7,14},{14,7},{9,16},{16,9... | collective-permute-start | bytes 1474568 | tf_op jit(solution)/shard_map/ppermute | solution.py:631
  17.5 0.0 collective-permute-done.1.others
  17.5 0.0 copy-done
  17.5 2.9 %middle.1 = (f32[4,8,32,256]{3,2,1,0:T(8,128)S(1)}, f32[4,8,32,256]{3,2,1,0:T(8,128)S(1)}, f32[8,32,256]{2,1,0:T(8,128)S(1)}, f32[8,32,256]{2,1,0:T(8,128)S(1)},...) custom-call(s32[1]{0:T(128)} %bitcast.core_ref, ...), custom_call_target="tpu_custom_call" | custom-call | flops 30000000 | bytes 9000000 | tf_op jit(solution)/shard_map/middle/pallas_call | solution.py:636
  20.5 5.3 %collective-permute-done.2.halo = f32[480,256]{1,0:T(8,128)S(1)} collective-permute-done((f32[480,256]{1,0:T(8,128)S(1)}, f32[480,256]{1,0:T(8,128)S(1)}, u32[]{:S(2)}, u32[]{:S(2)}) %collective-permute-start.2) | collective-permute-done | bytes 491552 | tf_op jit(solution)/shard_map/ppermute | solution.py:631
  25.7 2.3 %last.1 = (f32[128,256]{1,0:T(8,128)S(1)}, f32[8,256]{1,0:T(8,128)S(1)}, f32[8,256]{1,0:T(8,128)S(1)}, f32[4,8,32,256]{3,2,1,0:T(8,128)S(1)}, f32[4,8,32,256]{3,2,1,0:T(8,128)S(1)}, /*index=5*/f32[8,32,256]{2,1,0:T(8,128)S(1)}) custom-call(s32[1]{0:T(128)} %bitcast.core_ref, ...), custom_call_target="tpu_custom_call", output_to_operand_aliasing={{3}: (14, {}), {4}: (15, {}), {5}: (16, {})} | custom-call | tf_op jit(solution)/shard_map/last/pallas_call | solution.py:658
  28.1 9.3 %all_to_all.5 = f32[4,128,256]{2,1,0:T(8,128)S(1)} all-to-all(f32[4,128,256]{2,1,0:T(8,128)S(1)} %broadcast_in_dim.12), channel_id=1, replica_groups={{0,2,4,6},{1,3,5,7},{8,10,12,14},{9,11,13,15},{16,18,20,22},{17,19,21,2..., dimensions={0} | all-to-all | bytes 1048576 | tf_op jit(solution)/shard_map/all_to_all | solution.py:677
  37.5 1.9 %collective-permute-start.3 = (f32[136,256]{1,0:T(8,128)S(1)}, f32[136,256]{1,0:T(8,128)S(1)}, u32[]{:S(2)}, u32[]{:S(2)}) collective-permute-start(f32[136,256]{1,0:T(8,128)S(1)} %pad_maximum_fusion), channel_id=1, source_target_pairs={{0,1},{1,0},{2,3},{3,2},{4,5},{5,4},{6,7},{7,6},{8,9},{9,8},{10,11... | collective-permute-start | bytes 417800 | tf_op jit(solution)/shard_map/ppermute | solution.py:681
  39.4 1.3 %collective-permute-done.3.other = f32[136,256]{1,0:T(8,128)S(1)} collective-permute-done((f32[136,256]{1,0:T(8,128)S(1)}, f32[136,256]{1,0:T(8,128)S(1)}, u32[]{:S(2)}, u32[]{:S(2)}) %collective-permute-start.3) | collective-permute-done | bytes 139296 | tf_op jit(solution)/shard_map/ppermute | solution.py:681
  40.7 0.7 %join.1 = (f32[256,256]{1,0:T(8,128)}, f32[3,2,2,25]{3,2,1,0:T(2,128)}) custom-call(s32[1]{0:T(128)} %bitcast.1.core, f32[128,256]{1,0:T(8,128)S(1)} %reduce_sum.9.mine, f32[136,256]{1,0:T(8,128)S(1)} %collective-permute-done.3.other, f32[8,256]{1,0:T(8,128)S(1)} %get-tuple-element.55.coded), custom_call_target="tpu_custom_call" | custom-call | tf_op jit(solution)/shard_map/join/pallas_call | solution.py:682
  (3 shorter events, 0.1 us)
Async XLA Ops:
  3.1 14.4 %collective-permute-start.1 = (f32[2,2,8,32,256]{4,3,2,1,0:T(8,128)S(1)}, f32[2,2,8,32,256]{4,3,2,1,0:T(8,128)S(1)}, u32[]{:S(2)}, u32[]{:S(2)}) collective-permute-start(f32[2,2,8,32,256]{4,3,2,1,0:T(8,128)S(1)} %get-tuple-element.32.fields), channel_id=1, source_target_pairs={{0,1},{1,0},{2,3},{3,2},{4,5},{5,4},{6,7},{7,6},{8,9},{9,8},{10,11... | collective-permute-start | bytes 3145736 | tf_op jit(solution)/shard_map/ppermute | solution.py:620
  11.9 3.5 %collective-permute-start = (f32[272,256]{1,0:T(8,128)S(1)}, f32[272,256]{1,0:T(8,128)S(1)}, u32[]{:S(2)}, u32[]{:S(2)}) collective-permute-start(f32[272,256]{1,0:T(8,128)S(1)} %get-tuple-element.30), channel_id=1, source_target_pairs={{0,1},{1,0},{2,3},{3,2},{4,5},{5,4},{6,7},{7,6},{8,9},{9,8},{10,11... | collective-permute-start | bytes 835592 | tf_op jit(solution)/shard_map/ppermute | solution.py:619
  15.3 2.2 %copy-start = (f32[32,25]{1,0:T(8,128)S(1)}, f32[32,25]{1,0:T(8,128)}, u32[]{:S(2)}) copy-start(f32[32,25]{1,0:T(8,128)} %encoder.1) | copy-start | bytes 9604
  15.6 10.1 %collective-permute-start.2 = (f32[480,256]{1,0:T(8,128)S(1)}, f32[480,256]{1,0:T(8,128)S(1)}, u32[]{:S(2)}, u32[]{:S(2)}) collective-permute-start(f32[480,256]{1,0:T(8,128)S(1)} %pack.1.message), channel_id=1, source_target_pairs={{1,8},{8,1},{3,10},{10,3},{5,12},{12,5},{7,14},{14,7},{9,16},{16,9... | collective-permute-start | bytes 1474568 | tf_op jit(solution)/shard_map/ppermute | solution.py:631
  37.5 3.3 %collective-permute-start.3 = (f32[136,256]{1,0:T(8,128)S(1)}, f32[136,256]{1,0:T(8,128)S(1)}, u32[]{:S(2)}, u32[]{:S(2)}) collective-permute-start(f32[136,256]{1,0:T(8,128)S(1)} %pad_maximum_fusion), channel_id=1, source_target_pairs={{0,1},{1,0},{2,3},{3,2},{4,5},{5,4},{6,7},{7,6},{8,9},{9,8},{10,11... | collective-permute-start | bytes 417800 | tf_op jit(solution)/shard_map/ppermute | solution.py:681

commit v7 on v6

--- a/solution.py
+++ b/solution.py
@@ -237,17 +237,11 @@
         copy.wait()
 
 
-def middle_kernel(
-    capsules, core_ref, message, encoder, others, fields,
-    density, speed, admittance, mask,
-    b1, b2, vel_s, pres_s, damp_s, pd_s, back_e, grad, rows_out, code_high, code_low, corners,
-    q_s, w_s,
+def two_steps(
+    core, fields, mask, vel_s, pres_s, damp_s, pd_s, b1, b2, back_e, q_s, w_s, grad, known
 ):
-    _, pair, depth, width_x, width_y = fields.shape
-    shots = 2 * pair
-    slots, steps, channels = corners.shape[0], 2, encoder.shape[1]
+    _, shots, depth, width_x, width_y = fields.shape
     masks = edge_masks((width_x, width_y))
-    core = core_ref[0]
     half = depth // 2
 
     def plane_at(d):
@@ -256,32 +250,20 @@
     def coupling(d):
         return vel_s[d + core * (depth - 2 - 2 * d)]
 
-    def value_of(kind, s, z):
-        return (others if s < pair else fields)[kind, s % pair, z]
-
-    for z in range(depth):
-        dens = density[z]
-        spd = speed[z]
-        pres = 0.5 * dens * spd * spd
-        damp = 1.0 - admittance[z] * mask[z].astype(F32)
-        vel_s[z] = 0.5 / dens
-        pres_s[z] = pres
-        damp_s[z] = damp
-        pd_s[z] = pres * damp
     for d in range(depth - 1):
         z = plane_at(d)
         w = plane_weights(vel_s[z], masks)
         inwards, outwards = coupling(d), coupling(d - 1) if d > 0 else None
         for s in range(shots):
-            here = value_of(0, s, z)
-            total = plane_part(here, w) + inwards * (value_of(0, s, plane_at(d + 1)) - here)
+            here = fields[0, s, z]
+            total = plane_part(here, w) + inwards * (fields[0, s, plane_at(d + 1)] - here)
             if d > 0:
-                total += outwards * (value_of(0, s, plane_at(d - 1)) - here)
+                total += outwards * (fields[0, s, plane_at(d - 1)] - here)
             value = here + pres_s[z] * total
             b1[s, z] = value
             q_s[s, d] = here + damp_s[z] * value
             if d <= half:
-                w_s[s, d] = pd_s[z] * value_of(1, s, z)
+                w_s[s, d] = pd_s[z] * fields[1, s, z]
     for d in range(depth - 2):
         z = plane_at(d)
         w = plane_weights(vel_s[z], masks)
@@ -296,7 +278,7 @@
             b2[s, z] = value
             if d >= half:
                 continue
-            weighted, start = w_s[s, d], value_of(1, s, z)
+            weighted, start = w_s[s, d], fields[1, s, z]
             back = plane_part(weighted, w) + inwards * (w_s[s, d + 1] - weighted)
             if d > 0:
                 back += outwards * (w_s[s, d - 1] - weighted)
@@ -305,11 +287,34 @@
                 back_e[s, d] = back
             else:
                 sums += value * start + b1[s, z] * back
-        if d < half:
-            grad[z] = -(mask[z].astype(F32) * sums)
-        else:
-            grad[z] = sums
+        sums = -(mask[z].astype(F32) * sums) if d < half else sums
+        grad[z] = sums if known is None else known[z] + sums
     grad[plane_at(depth - 2)] = jnp.zeros((width_x, width_y), F32)
+
+
+def other_kernel(
+    core_ref, fields, mask, vel_s, pres_s, damp_s, pd_s, known, b1, b2, back_e, grad, q_s, w_s
+):
+    two_steps(core_ref[0], fields, mask, vel_s, pres_s, damp_s, pd_s, b1, b2, back_e, q_s, w_s, grad, known)
+
+
+def middle_kernel(
+    capsules, core_ref, message, encoder, fields, density, speed, admittance, mask,
+    b1, b2, vel_s, pres_s, damp_s, pd_s, back_e, grad, rows_out, code_high, code_low, corners,
+    q_s, w_s,
+):
+    _, pair, depth, width_x, _ = fields.shape
+    slots, steps, channels = corners.shape[0], 2, encoder.shape[1]
+    for z in range(depth):
+        dens = density[z]
+        spd = speed[z]
+        pres = 0.5 * dens * spd * spd
+        damp = 1.0 - admittance[z] * mask[z].astype(F32)
+        vel_s[z] = 0.5 / dens
+        pres_s[z] = pres
+        damp_s[z] = damp
+        pd_s[z] = pres * damp
+    two_steps(core_ref[0], fields, mask, vel_s, pres_s, damp_s, pd_s, b1, b2, back_e, q_s, w_s, grad, None)
     lane = lax.broadcasted_iota(jnp.int32, (LANES, LANES), 1)
     line = lax.broadcasted_iota(jnp.int32, (LANES, LANES), 0)
     same = (lax.div(lane, capsules) == lax.div(line, capsules)) & (line < slots * capsules)
@@ -354,8 +359,8 @@
 
 def last_kernel(
     capsules, core_ref, corners, halo, others, fields, mask, vel_s, pres_s, damp_s, pd_s, back_e,
-    rows_in, code_high, code_low, b1_in, b2_in, grad_in,
-    out, coded, coded_other, b1, b2, grad,
+    back_o, rows_in, code_high, code_low, b1_in, b2_in, b1_own_in, b2_own_in, grad_in,
+    out, coded, coded_other, b1_other, b2_other, b1_own, b2_own, grad,
     halo_s, stack, spread,
 ):
     _, pair, depth, width_x, width_y = fields.shape
@@ -371,6 +376,15 @@
     def value_of(kind, s, z):
         return (others if s < pair else fields)[kind, s % pair, z]
 
+    def edge_back(s, d):
+        return (back_e if s < pair else back_o)[s % pair, d]
+
+    def b1(s):
+        return (b1_other if s < pair else b1_own).at[s % pair]
+
+    def b2(s):
+        return (b2_other if s < pair else b2_own).at[s % pair]
+
     def face(k, s):
         start = (second if s >= pair else 0) + (k + s % pair) * width_x
         return halo[start : start + width_x, :]
@@ -388,7 +402,7 @@
         step = vel_b * (here - beyond)
         p1_h = face(2, s) + pd_h * step
         q_h = beyond + p1_h
-        fixed = b1[s, edge] - pres_s[edge] * step
+        fixed = b1(s)[edge] - pres_s[edge] * step
         change = -(pd_s[edge] * step)
         step2 = vel_b * (here + damp_s[edge] * fixed - q_h)
         halo_s[s * width_x : (s + 1) * width_x, :] = side_by_side(p1_h)
@@ -396,10 +410,10 @@
         halo_s[(2 * shots + s) * width_x : (2 * shots + s + 1) * width_x, :] = side_by_side(
             pd_h * (plane_part(q_h, w_h) + step2)
         )
-        b1[s, edge] = fixed
+        b1(s)[edge] = fixed
         total = plane_part(change, w_e) - vel_in * change - step2
-        b2[s, edge] = b2[s, edge] + change + pres_s[edge] * total
-        b2[s, inner] = b2[s, inner] + pres_s[inner] * (vel_in * change)
+        b2(s)[edge] = b2(s)[edge] + change + pres_s[edge] * total
+        b2(s)[inner] = b2(s)[inner] + pres_s[inner] * (vel_in * change)
 
     places = []
     low, high = 2 * core, 4 + 2 * core
@@ -430,7 +444,7 @@
                 for s in range(shots):
                     k = index[n, r, dz, s] = len(index)
                     stack[k * WINDOW : (k + 1) * WINDOW, :] = side_by_side(
-                        damp * field[s, z0 + dz, pl.ds(start, WINDOW), :]
+                        damp * field(s)[z0 + dz, pl.ds(start, WINDOW), :]
                     )
     found = dot(stack[...], doubled(columns, 0), (1, 0))
     blank = jnp.zeros((1, LANES), F32)
@@ -494,9 +508,9 @@
     for s in range(shots):
         weighted = face(4, s) + pd_h * rows_of(placed, s, width_x)
         start = value_of(1, s, edge)
-        back = back_e[s, 0] - vel_b * (pd_s[edge] * start - weighted)
-        sums += b2[s, edge] * start + b1[s, edge] * back
-        sums_in += b2[s, inner] * value_of(1, s, inner) + b1[s, inner] * back_e[s, 1]
+        back = edge_back(s, 0) - vel_b * (pd_s[edge] * start - weighted)
+        sums += b2(s)[edge] * start + b1(s)[edge] * back
+        sums_in += b2(s)[inner] * value_of(1, s, inner) + b1(s)[inner] * edge_back(s, 1)
     grad[edge] = -(mask[edge].astype(F32) * sums)
     grad[inner] = -(mask[inner].astype(F32) * sums_in)
 
@@ -521,10 +535,10 @@
                 total += between if dz == 0 else -between
                 total += damp_s[z0 + dz, window, :] * now[dz] + before[dz]
                 sums[1 + dz] += (
-                    b2[s, z0 + dz, window, :] * now[dz] + b1[s, z0 + dz, window, :] * total
+                    b2(s)[z0 + dz, window, :] * now[dz] + b1(s)[z0 + dz, window, :] * total
                 )
-            sums[0] += b1[s, lower, window, :] * outer[0]
-            sums[3] += b1[s, upper, window, :] * outer[1]
+            sums[0] += b1(s)[lower, window, :] * outer[0]
+            sums[3] += b1(s)[upper, window, :] * outer[1]
         inside = (jnp.where(z0 > 0, 1.0, 0.0), 1.0, 1.0, jnp.where(z0 + 2 < depth, 1.0, 0.0))
         for z, total, factor in zip((lower, z0, z0 + 1, upper), sums, inside):
             wall = mask[z, window, :].astype(F32)
@@ -631,45 +645,55 @@
     halo = lax.ppermute(face, ("slab", "shot"), facing)
 
     table = jax.ShapeDtypeStruct((LANES, 2 * LANES), jnp.bfloat16)
-    four = (2 * shots, *slab)
     rows_plane = (width_x, width_y)
+    edge_planes = (shots, 2, *rows_plane)
+    work = [
+        VMEM((shots, depth - 1, *rows_plane), F32),
+        VMEM((shots, depth // 2 + 1, *rows_plane), F32),
+    ]
+    cost = pl.CostEstimate(flops=15_000_000, bytes_accessed=5_000_000, transcendentals=0)
     b1, b2, vel, pres, damp, pd, back, grad, rows, high, low, corners = pl.pallas_call(
         functools.partial(middle_kernel, capsules),
-        in_specs=ins(9, 1),
+        in_specs=ins(8, 1),
         out_specs=[*ins(11), *ins(1, 1)],
         out_shape=outs(
-            four, four, slab, slab, slab, slab, (2 * shots, 2, *rows_plane), slab,
+            field, field, slab, slab, slab, slab, edge_planes, slab,
             (16, LANES), table, table, jax.ShapeDtypeStruct((slots,), jnp.int32),
         ),
-        scratch_shapes=[
-            VMEM((2 * shots, depth - 1, *rows_plane), F32),
-            VMEM((2 * shots, depth // 2 + 1, *rows_plane), F32),
-        ],
+        scratch_shapes=work,
         compiler_params=params,
-        cost_estimate=pl.CostEstimate(flops=30_000_000, bytes_accessed=9_000_000, transcendentals=0),
+        cost_estimate=cost,
         name="middle",
-    )(
-        core[None], face, encoder, others, fields, density, speed, admittance, bound_mask,
-    )
+    )(core[None], face, encoder, fields, density, speed, admittance, bound_mask)
+    b1_other, b2_other, back_other, grad = pl.pallas_call(
+        other_kernel,
+        in_specs=ins(8, 1),
+        out_specs=ins(4),
+        out_shape=outs(field, field, edge_planes, slab),
+        scratch_shapes=work,
+        compiler_params=params,
+        cost_estimate=cost,
+        name="other",
+    )(core[None], others, bound_mask, vel, pres, damp, pd, grad)
 
     windows = steps * slots * 2 * 2 * shots * WINDOW
     half = (depth // 2 * width_x, width_y)
     line = (8, width_y)
-    total, coded, coded_other, _, _, _ = pl.pallas_call(
+    total, coded, coded_other, *_ = pl.pallas_call(
         functools.partial(last_kernel, capsules),
-        in_specs=ins(17, 2),
-        out_specs=ins(6),
-        out_shape=outs(half, line, line, four, four, slab),
+        in_specs=ins(20, 2),
+        out_specs=ins(8),
+        out_shape=outs(half, line, line, field, field, field, field, slab),
         scratch_shapes=[
             VMEM((6 * shots * width_x, 2 * width_y), jnp.bfloat16),
             VMEM((windows, 2 * width_y), jnp.bfloat16), VMEM((windows, width_y), F32),
         ],
-        input_output_aliases={14: 3, 15: 4, 16: 5},
+        input_output_aliases={15: 3, 16: 4, 17: 5, 18: 6, 19: 7},
         compiler_params=params,
         name="last",
     )(
-        core[None], corners, halo, others, fields, bound_mask, vel, pres, damp, pd, back,
-        rows, high, low, b1, b2, grad,
+        core[None], corners, halo, others, fields, bound_mask, vel, pres, damp, pd, back_other,
+        back, rows, high, low, b1_other, b2_other, b1, b2, grad,
     )
 
     groups = [list(range(c, peers, 2)) for c in range(2)]

time: 41.7 us -> 41.7 us (level)
    pallas_call x2 -> x3, Pallas kernels: 5.2 us -> 5.42 us  [the longest x1 2.3 us: body(): pl.pallas_call(functools.partial(last_kernel, capsules), in_specs=ins(20,...]
where the time goes in v7:
time: 41.7 us; the launch traced here: 41.5 us
  starting transfers between devices  14.5 us (35%)
  blocking collectives  9.33 us (22%)
  Pallas kernels  8.88 us (21%)
  waiting for transfers between devices  7.92 us (19%)
  between operations  0.74 us (2%)
    all_to_all x1, blocking collectives, body(): lax.all_to_all(copies, 'shot', split_axis=0, concat_axis=0, tiled=True, a...  9.33 us
    ppermute x1, starting transfers between devices, body(): others = lax.ppermute(fields, 'shot', pairs)  8.75 us
    ppermute x1, waiting for transfers between devices, body(): halo = lax.ppermute(face, ('slab', 'shot'), facing)  5.07 us
    pallas_call x1, Pallas kernels, body(): pl.pallas_call(edge_kernel, in_specs=ins(10, 1, 9), out_specs=ins(7), out...  2.46 us
    pallas_call x1, Pallas kernels, body(): pl.pallas_call(functools.partial(last_kernel, capsules), in_specs=ins(20,...  2.3 us
    ppermute x1, starting transfers between devices, body(): halo = lax.ppermute(face, ('slab', 'shot'), facing)  1.92 us
    ppermute x1, starting transfers between devices, body(): lax.ppermute(jnp.concatenate([total, coded_other], axis=0), 'shot', pairs)  1.92 us
    ppermute x1, starting transfers between devices, body(): got = lax.ppermute(sent, 'shot', pairs)  1.92 us
  transfers between devices with their start and end apart: 4, of which 3 were waited for; matrix products, arithmetic and copies ran while one was open for 0% of the time, Pallas kernels for 8%

profile of v7, /device:TPU:1, one launch (start us, length us, event | category | flops | bytes accessed | tf_op | source)
XLA Modules:
  0.0 41.5 jit_solution(16762400602896739527)
XLA Ops:
  0.6 2.5 %edge.1 = (f32[480,256]{1,0:T(8,128)S(1)}, f32[272,256]{1,0:T(8,128)S(1)}, f32[2,2,8,32,256]{4,3,2,1,0:T(8,128)S(1)}, f32[8,32,256]{2,1,0:T(8,128)S(1)}, f32[8,3...) custom-call(s32[1]{0:T(128)} %bitcast.core_ref, s32[3]{0:T(128)} %live_h.1, ...), custom_call_target="tpu_custom_call" | custom-call | tf_op jit(solution)/shard_map/edge/pallas_call | solution.py:599
  3.1 8.7 %collective-permute-start.2 = (f32[2,2,8,32,256]{4,3,2,1,0:T(8,128)S(1)}, f32[2,2,8,32,256]{4,3,2,1,0:T(8,128)S(1)}, u32[]{:S(2)}, u32[]{:S(2)}) collective-permute-start(f32[2,2,8,32,256]{4,3,2,1,0:T(8,128)S(1)} %get-tuple-element.36.fields), channel_id=1, source_target_pairs={{0,1},{1,0},{2,3},{3,2},{4,5},{5,4},{6,7},{7,6},{8,9},{9,8},{10,11... | collective-permute-start | bytes 3145736 | tf_op jit(solution)/shard_map/ppermute | solution.py:634
  11.9 1.9 %collective-permute-start = (f32[272,256]{1,0:T(8,128)S(1)}, f32[272,256]{1,0:T(8,128)S(1)}, u32[]{:S(2)}, u32[]{:S(2)}) collective-permute-start(f32[272,256]{1,0:T(8,128)S(1)} %get-tuple-element.34), channel_id=1, source_target_pairs={{0,1},{1,0},{2,3},{3,2},{4,5},{5,4},{6,7},{7,6},{8,9},{9,8},{10,11... | collective-permute-start | bytes 835592 | tf_op jit(solution)/shard_map/ppermute | solution.py:633
  13.8 1.5 %collective-permute-done.got = f32[272,256]{1,0:T(8,128)S(1)} collective-permute-done((f32[272,256]{1,0:T(8,128)S(1)}, f32[272,256]{1,0:T(8,128)S(1)}, u32[]{:S(2)}, u32[]{:S(2)}) %collective-permute-start) | collective-permute-done | bytes 278560 | tf_op jit(solution)/shard_map/ppermute | solution.py:633
  15.3 0.0 copy-start
  15.3 0.3 pack.1.message
  15.6 1.9 %collective-permute-start.1 = (f32[480,256]{1,0:T(8,128)S(1)}, f32[480,256]{1,0:T(8,128)S(1)}, u32[]{:S(2)}, u32[]{:S(2)}) collective-permute-start(f32[480,256]{1,0:T(8,128)S(1)} %pack.1.message), channel_id=1, source_target_pairs={{1,8},{8,1},{3,10},{10,3},{5,12},{12,5},{7,14},{14,7},{9,16},{16,9... | collective-permute-start | bytes 1474568 | tf_op jit(solution)/shard_map/ppermute | solution.py:645
  17.5 0.0 copy-done
  17.5 1.9 %middle.1 = (f32[2,8,32,256]{3,2,1,0:T(8,128)S(1)}, f32[2,8,32,256]{3,2,1,0:T(8,128)S(1)}, f32[8,32,256]{2,1,0:T(8,128)S(1)}, f32[8,32,256]{2,1,0:T(8,128)S(1)},...) custom-call(s32[1]{0:T(128)} %bitcast.core_ref, ...), custom_call_target="tpu_custom_call" | custom-call | flops 15000000 | bytes 5000000 | tf_op jit(solution)/shard_map/middle/pallas_call | solution.py:655
  19.4 0.0 collective-permute-done.2.fields.others
  19.4 1.2 %other.1 = (f32[2,8,32,256]{3,2,1,0:T(8,128)S(1)}, f32[2,8,32,256]{3,2,1,0:T(8,128)S(1)}, f32[2,2,32,256]{3,2,1,0:T(8,128)S(1)}, f32[8,32,256]{2,1,0:T(8,128)S(1)}) custom-call(s32[1]{0:T(128)} %bitcast.core_ref, f32[2,2,8,32,256]{4,3,2,1,0:T(8,128)S(1)} %collective-permute-done.2.fields.others, s32[8,32,256]{2,1,0:T(8,128)S(1)} %get-tuple-element.40.mask, ...), custom_call_target="tpu_custom_call" | custom-call | flops 15000000 | bytes 5000000 | tf_op jit(solution)/shard_map/other/pallas_call | solution.py:668
  20.7 5.1 %collective-permute-done.1.halo = f32[480,256]{1,0:T(8,128)S(1)} collective-permute-done((f32[480,256]{1,0:T(8,128)S(1)}, f32[480,256]{1,0:T(8,128)S(1)}, u32[]{:S(2)}, u32[]{:S(2)}) %collective-permute-start.1) | collective-permute-done | bytes 491552 | tf_op jit(solution)/shard_map/ppermute | solution.py:645
  25.7 2.3 %last.1 = (f32[128,256]{1,0:T(8,128)S(1)}, f32[8,256]{1,0:T(8,128)S(1)}, f32[8,256]{1,0:T(8,128)S(1)}, f32[2,8,32,256]{3,2,1,0:T(8,128)S(1)}, f32[2,8,32,256]{3,...) custom-call(s32[1]{0:T(128)} %bitcast.core_ref, ...), custom_call_target="tpu_custom_call", output_to_operand_aliasing={{3}: (15, {}), {4}: (16, {}), {5}: (17, {}), {6}: (18, {}),... | custom-call | tf_op jit(solution)/shard_map/last/pallas_call | solution.py:682
  28.1 9.3 %all_to_all.5 = f32[4,128,256]{2,1,0:T(8,128)S(1)} all-to-all(f32[4,128,256]{2,1,0:T(8,128)S(1)} %broadcast_in_dim.13), channel_id=1, replica_groups={{0,2,4,6},{1,3,5,7},{8,10,12,14},{9,11,13,15},{16,18,20,22},{17,19,21,2..., dimensions={0} | all-to-all | bytes 1048576 | tf_op jit(solution)/shard_map/all_to_all | solution.py:701
  37.5 1.9 %collective-permute-start.3 = (f32[136,256]{1,0:T(8,128)S(1)}, f32[136,256]{1,0:T(8,128)S(1)}, u32[]{:S(2)}, u32[]{:S(2)}) collective-permute-start(f32[136,256]{1,0:T(8,128)S(1)} %pad_maximum_fusion), channel_id=1, source_target_pairs={{0,1},{1,0},{2,3},{3,2},{4,5},{5,4},{6,7},{7,6},{8,9},{9,8},{10,11... | collective-permute-start | bytes 417800 | tf_op jit(solution)/shard_map/ppermute | solution.py:705
  39.4 1.3 %collective-permute-done.3.other = f32[136,256]{1,0:T(8,128)S(1)} collective-permute-done((f32[136,256]{1,0:T(8,128)S(1)}, f32[136,256]{1,0:T(8,128)S(1)}, u32[]{:S(2)}, u32[]{:S(2)}) %collective-permute-start.3) | collective-permute-done | bytes 139296 | tf_op jit(solution)/shard_map/ppermute | solution.py:705
  40.7 0.7 %join.1 = (f32[256,256]{1,0:T(8,128)}, f32[3,2,2,25]{3,2,1,0:T(2,128)}) custom-call(s32[1]{0:T(128)} %bitcast.1.core, f32[128,256]{1,0:T(8,128)S(1)} %reduce_sum.9.mine, f32[136,256]{1,0:T(8,128)S(1)} %collective-permute-done.3.other, f32[8,256]{1,0:T(8,128)S(1)} %get-tuple-element.63.coded), custom_call_target="tpu_custom_call" | custom-call | tf_op jit(solution)/shard_map/join/pallas_call | solution.py:706
  (3 shorter events, 0.1 us)
Async XLA Ops:
  3.1 16.3 %collective-permute-start.2 = (f32[2,2,8,32,256]{4,3,2,1,0:T(8,128)S(1)}, f32[2,2,8,32,256]{4,3,2,1,0:T(8,128)S(1)}, u32[]{:S(2)}, u32[]{:S(2)}) collective-permute-start(f32[2,2,8,32,256]{4,3,2,1,0:T(8,128)S(1)} %get-tuple-element.36.fields), channel_id=1, source_target_pairs={{0,1},{1,0},{2,3},{3,2},{4,5},{5,4},{6,7},{7,6},{8,9},{9,8},{10,11... | collective-permute-start | bytes 3145736 | tf_op jit(solution)/shard_map/ppermute | solution.py:634
  11.9 3.5 %collective-permute-start = (f32[272,256]{1,0:T(8,128)S(1)}, f32[272,256]{1,0:T(8,128)S(1)}, u32[]{:S(2)}, u32[]{:S(2)}) collective-permute-start(f32[272,256]{1,0:T(8,128)S(1)} %get-tuple-element.34), channel_id=1, source_target_pairs={{0,1},{1,0},{2,3},{3,2},{4,5},{5,4},{6,7},{7,6},{8,9},{9,8},{10,11... | collective-permute-start | bytes 835592 | tf_op jit(solution)/shard_map/ppermute | solution.py:633
  15.3 2.2 %copy-start = (f32[32,25]{1,0:T(8,128)S(1)}, f32[32,25]{1,0:T(8,128)}, u32[]{:S(2)}) copy-start(f32[32,25]{1,0:T(8,128)} %encoder.1) | copy-start | bytes 9604
  15.6 10.1 %collective-permute-start.1 = (f32[480,256]{1,0:T(8,128)S(1)}, f32[480,256]{1,0:T(8,128)S(1)}, u32[]{:S(2)}, u32[]{:S(2)}) collective-permute-start(f32[480,256]{1,0:T(8,128)S(1)} %pack.1.message), channel_id=1, source_target_pairs={{1,8},{8,1},{3,10},{10,3},{5,12},{12,5},{7,14},{14,7},{9,16},{16,9... | collective-permute-start | bytes 1474568 | tf_op jit(solution)/shard_map/ppermute | solution.py:645
  37.5 3.3 %collective-permute-start.3 = (f32[136,256]{1,0:T(8,128)S(1)}, f32[136,256]{1,0:T(8,128)S(1)}, u32[]{:S(2)}, u32[]{:S(2)}) collective-permute-start(f32[136,256]{1,0:T(8,128)S(1)} %pad_maximum_fusion), channel_id=1, source_target_pairs={{0,1},{1,0},{2,3},{3,2},{4,5},{5,4},{6,7},{7,6},{8,9},{9,8},{10,11... | collective-permute-start | bytes 417800 | tf_op jit(solution)/shard_map/ppermute | solution.py:705
